TPU v7x, 512 devices: a whole 4x4x16 slice. The times are simulated.
512 devices in a mesh: exp: 64 (over x, z), rep: 8 (over y, core).
Axes of the slice: x: 4, y: 4, z: 16, core: 2. Of those that a mesh axis runs over, the one named last changes fastest.
Arguments:
- latent: bfloat16 [128, 16, 64], P('exp'), may hold values from -6 to 6
- stem_weight: bfloat16 [144, 1536], replicated, may hold values from -0.5 to 0.5
- norm_gain: float32 [1536], replicated, may hold values from 0.4 to 1.6
- router_weight: bfloat16 [1536, 8], replicated, may hold values from -0.15625 to 0.15625
- routes: int32 [8192, 2], P('exp'), may hold values from 0 to 7, all different within a row; in each aligned block of 128 rows (0 to 127, 128 to 255, ...) at most 40 rows name the same one
- gate_weight: bfloat16 [1536, 24576], P('rep', 'exp'), may hold values from -0.15625 to 0.15625
- up_weight: bfloat16 [1536, 24576], P('rep', 'exp'), may hold values from -0.15625 to 0.15625
- down_weight: bfloat16 [24576, 1536], P('exp', 'rep'), may hold values from -0.109375 to 0.109375
- grad_mixed: bfloat16 [8192, 1536], P('exp'), may hold values from -6 to 6
Outputs:
- mixed: bfloat16 [8192, 1536], P('exp')
- grad_latent: float32 [128, 16, 64], P('exp')
- grad_gate: float32 [1536, 24576], P('rep', 'exp')
- grad_up: float32 [1536, 24576], P('rep', 'exp')
- grad_down: float32 [24576, 1536], P('exp', 'rep')
Inputs may be any that keep to these rules, and one draw needn't show every extreme that they name: `routes`: A token's 2 experts differ. Within the 128 tokens of one device, no expert is named more than 40 times, and in every draw some device's tokens name some expert exactly 40 times.
All inputs are finite; a program needn't handle non-finite values.
Results may differ from a plain program's by a relative error of at most 0.023.
Values may be sent and summed in bfloat16 or wider, within the bound.
A program may use at most 64 MiB of HBM per device.

v0:
```python
import jax
import jax.numpy as jnp
from jax import lax
from jax.sharding import PartitionSpec as P

CAP = 40


def with_halo(cells, sides, width):
    for axis, dim in sides:
        count = lax.axis_size(axis)
        ends = count - 1
        head = lax.slice_in_dim(cells, 0, width, axis=dim)
        tail = lax.slice_in_dim(cells, cells.shape[dim] - width, cells.shape[dim], axis=dim)
        cells = jnp.concatenate(
            [
                lax.ppermute(tail, axis, [(i, (i + 1) % count) for i in range(ends)]),
                cells,
                lax.ppermute(head, axis, [((i + 1) % count, i) for i in range(ends)]),
            ],
            axis=dim,
        )
    return cells


def rms_norm(values, gain):
    return values * lax.rsqrt(jnp.mean(values * values, axis=-1, keepdims=True) + 1e-06) * gain


def gating(picked):
    chosen = jax.nn.sigmoid(picked)
    return chosen / jnp.sum(chosen, axis=-1, keepdims=True)


def local(
    latent,
    stem_weight,
    norm_gain,
    router_weight,
    routes,
    gate_weight,
    up_weight,
    down_weight,
    grad_mixed,
):
    rows_here = latent.shape[0]
    channels = latent.shape[1]
    width = latent.shape[2]
    model_width = stem_weight.shape[1]
    experts = router_weight.shape[1]
    top_count = routes.shape[1]
    tok_here = rows_here * width
    shards = lax.axis_size("exp") // experts
    group_size = CAP // lax.axis_size("rep")
    slots = experts * CAP
    padded = with_halo(latent, (("exp", 0),), 1)
    padded = jnp.pad(padded, ((0, 0), (0, 0), (1, 1)))
    pieces = jnp.stack(
        [padded[i : i + rows_here, :, j : j + width] for i in range(3) for j in range(3)], axis=0
    )
    patches = jnp.transpose(pieces, (1, 3, 0, 2)).reshape(tok_here, 9 * channels)
    stem = jnp.dot(patches, stem_weight, preferred_element_type=jnp.float32).astype(jnp.bfloat16)
    stem_value = stem.astype(jnp.float32)
    normed = rms_norm(stem_value, norm_gain).astype(jnp.bfloat16)
    logits = jnp.dot(normed, router_weight, preferred_element_type=jnp.float32)
    picked = jnp.take_along_axis(logits, routes, axis=1)
    gates = gating(picked)
    upstream = grad_mixed.astype(jnp.float32)
    grad_rows = (
        (gates[:, :, None] * upstream[:, None, :]).astype(jnp.bfloat16).reshape(-1, model_width)
    )
    flat_routes = routes.reshape(-1)
    onehot = (flat_routes[:, None] == jnp.arange(experts, dtype=jnp.int32)[None, :]).astype(
        jnp.int32
    )
    position = jnp.sum(onehot * (jnp.cumsum(onehot, axis=0) - 1), axis=1)
    slot_index = flat_routes * CAP + position
    send_rows = (
        jnp.zeros((slots, model_width), jnp.bfloat16)
        .at[slot_index]
        .set(jnp.repeat(normed, top_count, axis=0))
    )
    send_grads = jnp.zeros((slots, model_width), jnp.bfloat16).at[slot_index].set(grad_rows)
    group_start = lax.axis_index("rep") * group_size
    group_rows = lax.dynamic_slice_in_dim(
        send_rows.reshape(experts, CAP, model_width), group_start, group_size, 1
    )
    group_grads = lax.dynamic_slice_in_dim(
        send_grads.reshape(experts, CAP, model_width), group_start, group_size, 1
    )
    fan_rows = jnp.repeat(group_rows, shards, axis=0)
    fan_grads = jnp.repeat(group_grads, shards, axis=0)
    gate_full, up_full = (
        lax.all_gather(gate_weight, "rep", axis=0, tiled=True),
        lax.all_gather(up_weight, "rep", axis=0, tiled=True),
    )
    down_full = lax.all_gather(down_weight, "rep", axis=1, tiled=True)
    hid_here = gate_full.shape[1]
    recv_rows = lax.all_to_all(fan_rows, "exp", split_axis=0, concat_axis=0, tiled=True)
    flat = recv_rows.reshape(-1, model_width)
    pre_gate = jnp.dot(flat, gate_full, preferred_element_type=jnp.float32)
    pre_up = jnp.dot(flat, up_full, preferred_element_type=jnp.float32)
    forward_hidden = (jax.nn.silu(pre_gate) * pre_up).astype(jnp.bfloat16)
    part = jnp.dot(forward_hidden, down_full, preferred_element_type=jnp.float32).astype(
        jnp.bfloat16
    )
    part, hidden, pre_gate, pre_up = (
        part.reshape(recv_rows.shape),
        forward_hidden,
        pre_gate,
        pre_up,
    )
    returned = lax.all_to_all(part, "exp", split_axis=0, concat_axis=0, tiled=True)
    recv_grads = lax.all_to_all(fan_grads, "exp", split_axis=0, concat_axis=0, tiled=True)
    flat = recv_grads.reshape(-1, model_width)
    grad_hidden = lax.dot_general(
        flat, down_full, (((1,), (1,)), ((), ())), preferred_element_type=jnp.float32
    )
    sigma = jax.nn.sigmoid(pre_gate)
    backward_grad_gate_pre = (
        grad_hidden * pre_up * sigma * (1.0 + pre_gate * (1.0 - sigma))
    ).astype(jnp.bfloat16)
    backward_grad_up_pre = (grad_hidden * pre_gate * sigma).astype(jnp.bfloat16)
    back = lax.dot_general(
        backward_grad_gate_pre,
        gate_full,
        (((1,), (1,)), ((), ())),
        preferred_element_type=jnp.float32,
    )
    back = back + lax.dot_general(
        backward_grad_up_pre, up_full, (((1,), (1,)), ((), ())), preferred_element_type=jnp.float32
    )
    back, grad_gate_pre, grad_up_pre = (
        back.astype(jnp.bfloat16).reshape(recv_grads.shape),
        backward_grad_gate_pre,
        backward_grad_up_pre,
    )
    returned_back = lax.all_to_all(back, "exp", split_axis=0, concat_axis=0, tiled=True)
    group_out = jnp.sum(
        returned.reshape(experts, shards, group_size, model_width).astype(jnp.float32), axis=1
    ).astype(jnp.bfloat16)
    group_back = jnp.sum(
        returned_back.reshape(experts, shards, group_size, model_width).astype(jnp.float32), axis=1
    ).astype(jnp.bfloat16)
    slot_out, slot_back = (
        lax.all_gather(group_out, "rep", axis=1, tiled=True),
        lax.all_gather(group_back, "rep", axis=1, tiled=True),
    )
    slot_out = slot_out.reshape(slots, model_width).astype(jnp.float32)
    slot_back = slot_back.reshape(slots, model_width).astype(jnp.float32)
    expert_out = slot_out[slot_index].reshape(tok_here, top_count, model_width)
    expert_back = slot_back[slot_index].reshape(tok_here, top_count, model_width)
    mixed = (stem_value + jnp.sum(gates[:, :, None] * expert_out, axis=1)).astype(jnp.bfloat16)
    grad_gates = jnp.sum(upstream[:, None, :] * expert_out, axis=-1)
    _, gate_pull = jax.vjp(gating, picked)
    grad_picked = gate_pull(grad_gates)[0]
    selector = (routes[:, :, None] == jnp.arange(experts, dtype=jnp.int32)).astype(jnp.float32)
    grad_logits = jnp.sum(selector * grad_picked[:, :, None], axis=1)
    grad_normed = jnp.sum(expert_back, axis=1) + jnp.dot(
        grad_logits, router_weight.astype(jnp.float32).T, precision=lax.Precision.HIGHEST
    )
    _, norm_pull = jax.vjp(lambda values: rms_norm(values, norm_gain), stem_value)
    grad_stem = (upstream + norm_pull(grad_normed)[0]).astype(jnp.bfloat16)
    grad_block = with_halo(grad_stem.reshape(rows_here, width, model_width), (("exp", 0),), 1)
    projected = jnp.dot(
        grad_block.reshape(-1, model_width), stem_weight.T, preferred_element_type=jnp.float32
    )
    projected = projected.reshape(rows_here + 2, width, 9, channels)
    shifted = jnp.pad(projected, ((0, 0), (1, 1), (0, 0), (0, 0)))
    terms = [
        shifted[2 - i : 2 - i + rows_here, 2 - j : 2 - j + width, 3 * i + j, :]
        for i in range(3)
        for j in range(3)
    ]
    grad_latent = jnp.sum(jnp.stack(terms, axis=0), axis=0).transpose(0, 2, 1)
    flat_rows = recv_rows.reshape(-1, model_width)
    flat_grads = recv_grads.reshape(-1, model_width)
    dims = (((0,), (0,)), ((), ()))
    term_gate = lax.dot_general(flat_rows, grad_gate_pre, dims, preferred_element_type=jnp.float32)
    term_up = lax.dot_general(flat_rows, grad_up_pre, dims, preferred_element_type=jnp.float32)
    term_down = lax.dot_general(flat_grads, hidden, dims, preferred_element_type=jnp.float32)
    summed = lax.psum_scatter(
        jnp.concatenate([term_gate, term_up, term_down], axis=1).astype(jnp.bfloat16),
        "rep",
        scatter_dimension=0,
        tiled=True,
    ).astype(jnp.float32)
    grad_gate = summed[:, :hid_here]
    grad_up = summed[:, hid_here : 2 * hid_here]
    grad_down = summed[:, 2 * hid_here :].T
    return (mixed, grad_latent, grad_gate, grad_up, grad_down)


def solution(mesh):
    return jax.shard_map(
        local,
        mesh=mesh,
        in_specs=(
            P("exp", None, None),
            P(),
            P(),
            P(),
            P("exp", None),
            P("rep", "exp"),
            P("rep", "exp"),
            P("exp", "rep"),
            P("exp", None),
        ),
        out_specs=(
            P("exp", None),
            P("exp", None, None),
            P("rep", "exp"),
            P("rep", "exp"),
            P("exp", "rep"),
        ),
        check_vma=False,
    )
```

profile of v0, /device:TPU:1, one launch (start us, length us, event | category | flops | bytes accessed | tf_op | source)
XLA Modules:
  0.0 455.4 jit_solution(8518326553651853229)
XLA Ops:
  7.9 1.3 collective-permute-start.1
  9.2 5.0 %collective-permute-start = (bf16[1,16,64]{2,1,0:T(8,128)(2,1)S(1)}, bf16[1,16,64]{2,1,0:T(8,128)(2,1)S(1)}, u32[]{:S(2)}, u32[]{:S(2)}) collective-permute-start(bf16[1,16,64]{2,1,0:T(8,128)(2,1)S(1)} %get-tuple-element.54), channel_id=1, source_target_pairs={{0,8},{8,16},{16,24},{24,32},{32,40},{40,48},{48,56},{56,64},{64,7... | collective-permute-start | bytes 6152 | tf_op jit(solution)/shard_map/ppermute | solution.py:17
  17.9 2.6 mul.190
  20.4 2.4 mul.191
  25.0 1.4 gather_fusion.2
  26.9 1.3 broadcast_in_dim.17
  28.2 3.0 reshape.269
  31.2 3.4 scatter_custom_fusion
  34.6 2.9 scatter_custom_fusion.1
  37.5 1.2 constant_dynamic-slice_fusion
  38.8 1.3 broadcast_in_dim.18
  40.0 18.1 %all-to-all-start = ((bf16[64,5,1536]{2,1,0:T(8,128)(2,1)}), bf16[64,5,1536]{2,1,0:T(8,128)(2,1)S(1)}, u32[]{:S(2)}, u32[]{:S(2)}) async-start(bf16[64,5,1536]{2,1,0:T(8,128)(2,1)} %bitcast.108), calls=%async_computation | async-start | bytes 3145728 | tf_op jit(solution)/shard_map/all_to_all | solution.py:99
  58.9 69.7 %all-to-all-done = bf16[64,5,1536]{2,1,0:T(8,128)(2,1)S(1)} async-done(((bf16[64,5,1536]{2,1,0:T(8,128)(2,1)}), bf16[64,5,1536]{2,1,0:T(8,128)(2,1)S(1)}, u32[]{:S(2)}, u32[]{:S(2)}) %all-to-all-start) | async-done | bytes 983072 | tf_op jit(solution)/shard_map/all_to_all | solution.py:99
  128.6 1.4 broadcast_in_dim.19
  130.3 12.9 %all-to-all-start.2 = ((bf16[64,5,1536]{2,1,0:T(8,128)(2,1)}), bf16[64,5,1536]{2,1,0:T(8,128)(2,1)}, u32[]{:S(2)}, u32[]{:S(2)}) async-start(bf16[64,5,1536]{2,1,0:T(8,128)(2,1)} %bitcast.107), calls=%async_computation.2 | async-start | bytes 3145728 | tf_op jit(solution)/shard_map/all_to_all | solution.py:114
  144.6 1.6 reshape.226
  146.2 67.1 %all-to-all-done.2 = bf16[64,5,1536]{2,1,0:T(8,128)(2,1)} async-done(((bf16[64,5,1536]{2,1,0:T(8,128)(2,1)}), bf16[64,5,1536]{2,1,0:T(8,128)(2,1)}, u32[]{:S(2)}, u32[]{:S(2)}) %all-to-all-start.2) | async-done | bytes 983072 | tf_op jit(solution)/shard_map/all_to_all | solution.py:114
  213.4 2.4 reshape.232
  215.7 2.7 fusion.42
  218.5 2.7 fusion.43
  221.2 3.4 multiply_convert_fusion.3
  226.8 1.4 reshape.233
  228.2 13.1 %all-to-all-start.3 = ((bf16[64,5,1536]{2,1,0:T(8,128)(2,1)}), bf16[64,5,1536]{2,1,0:T(8,128)(2,1)}, u32[]{:S(2)}, u32[]{:S(2)}) async-start(bf16[64,5,1536]{2,1,0:T(8,128)(2,1)} %reshape.233), calls=%async_computation.3 | async-start | bytes 3145728 | tf_op jit(solution)/shard_map/all_to_all | solution.py:138
  241.4 2.0 convolution_convert_fusion.3
  243.4 1.4 reshape.227
  244.8 2.1 convolution_convert_fusion
  246.9 1.8 convolution_convert_fusion.1
  248.7 1.8 convolution_convert_fusion.2
  250.6 61.1 %all-to-all-done.3 = bf16[64,5,1536]{2,1,0:T(8,128)(2,1)} async-done(((bf16[64,5,1536]{2,1,0:T(8,128)(2,1)}), bf16[64,5,1536]{2,1,0:T(8,128)(2,1)}, u32[]{:S(2)}, u32[]{:S(2)}) %all-to-all-start.3) | async-done | bytes 983072 | tf_op jit(solution)/shard_map/all_to_all | solution.py:138
  311.7 12.9 %all-to-all-start.1 = ((bf16[64,5,1536]{2,1,0:T(8,128)(2,1)}), bf16[64,5,1536]{2,1,0:T(8,128)(2,1)}, u32[]{:S(2)}, u32[]{:S(2)}) async-start(bf16[64,5,1536]{2,1,0:T(8,128)(2,1)} %reshape.227), calls=%async_computation.1 | async-start | bytes 3145728 | tf_op jit(solution)/shard_map/all_to_all | solution.py:113
  324.7 3.2 pad_maximum_fusion
  327.9 5.8 %copy.115 = bf16[1536,1152]{1,0:T(8,128)(2,1)} copy(bf16[1536,1152]{0,1:T(8,128)(2,1)} %pad_maximum_fusion) | data formatting | bytes 7077888
  335.7 1.7 bitcast_reduce_fusion
  337.5 14.9 %all_gather.19 = bf16[8,40,1536]{2,0,1:T(8,128)(2,1)S(1)} all-gather(bf16[8,5,1536]{2,0,1:T(8,128)(2,1)S(1)} %copy.107), channel_id=1, replica_groups=mesh['exp'=64,'rep'=8] {'rep'}, dimensions={1}, use_global_device_ids=true | all-gather | bytes 1105920 | tf_op jit(solution)/shard_map/all_gather | solution.py:147
  352.7 2.3 gather_fusion.1
  355.0 3.1 reshape.235
  358.1 36.8 %all-to-all-done.1 = bf16[64,5,1536]{2,1,0:T(8,128)(2,1)} async-done(((bf16[64,5,1536]{2,1,0:T(8,128)(2,1)}), bf16[64,5,1536]{2,1,0:T(8,128)(2,1)}, u32[]{:S(2)}, u32[]{:S(2)}) %all-to-all-start.1) | async-done | bytes 983072 | tf_op jit(solution)/shard_map/all_to_all | solution.py:113
  394.9 1.7 bitcast_reduce_fusion.1
  396.7 20.9 %all_gather.18 = bf16[8,40,1536]{2,0,1:T(8,128)(2,1)S(1)} all-gather(bf16[8,5,1536]{2,0,1:T(8,128)(2,1)S(1)} %copy.104), channel_id=1, replica_groups=mesh['exp'=64,'rep'=8] {'rep'}, dimensions={1}, use_global_device_ids=true | all-gather | bytes 1105920 | tf_op jit(solution)/shard_map/all_gather | solution.py:146
  418.0 2.4 gather_fusion
  420.3 3.1 reshape.229
  423.5 5.0 %multiply_reduce_fusion = (f32[128,2]{1,0:T(8,128)S(1)}, f32[128,1536]{1,0:T(8,128)}) fusion(f32[128,2,1536]{2,1,0:T(2,128)} %reshape.229, f32[128,1536]{1,0:T(8,128)} %convert_element_type.77, f32[128,2]{1,0:T(8,128)S(1)} %copy.100), kind=kLoop, calls=%fused_computation.18 | loop fusion | flops 1376000 | bytes 3147776 | tf_op jit(solution)/shard_map/reduce_sum | solution.py:154
  428.5 3.0 reduce_sum.177
  431.6 1.9 multiply_reduce_fusion.2
  434.6 1.3 collective-permute-start.3
  435.9 4.0 collective-permute-start.2
  439.9 2.9 collective-permute-done.3
  444.9 1.2 copy.116
  (121 shorter events, 20.4 us)
Async XLA Ops:
  7.2 16.5 %copy-start = (bf16[144,1536]{1,0:T(8,128)(2,1)S(1)}, bf16[144,1536]{1,0:T(8,128)(2,1)}, u32[]{:S(2)}) copy-start(bf16[144,1536]{1,0:T(8,128)(2,1)} %param.10) | copy-start | bytes 1327108
  7.9 15.2 %collective-permute-start.1 = (bf16[1,16,64]{2,1,0:T(8,128)(2,1)S(1)}, bf16[1,16,64]{2,1,0:T(8,128)(2,1)S(1)}, u32[]{:S(2)}, u32[]{:S(2)}) collective-permute-start(bf16[1,16,64]{2,1,0:T(8,128)(2,1)S(1)} %get-tuple-element.55), channel_id=1, source_target_pairs={{8,0},{16,8},{24,16},{32,24},{40,32},{48,40},{56,48},{64,56},{72,6... | collective-permute-start | bytes 6152 | tf_op jit(solution)/shard_map/ppermute | solution.py:19
  9.2 13.9 %collective-permute-start = (bf16[1,16,64]{2,1,0:T(8,128)(2,1)S(1)}, bf16[1,16,64]{2,1,0:T(8,128)(2,1)S(1)}, u32[]{:S(2)}, u32[]{:S(2)}) collective-permute-start(bf16[1,16,64]{2,1,0:T(8,128)(2,1)S(1)} %get-tuple-element.54), channel_id=1, source_target_pairs={{0,8},{8,16},{16,24},{24,32},{32,40},{40,48},{48,56},{56,64},{64,7... | collective-permute-start | bytes 6152 | tf_op jit(solution)/shard_map/ppermute | solution.py:17
  20.4 2.7 copy-start.13
  22.8 1.8 copy-start.15
  22.8 1.9 copy-start.14
  24.1 0.7 copy-start.19
  24.1 0.5 copy-start.17
  25.0 1.6 copy-start.16
  40.0 88.5 %all-to-all-start = ((bf16[64,5,1536]{2,1,0:T(8,128)(2,1)}), bf16[64,5,1536]{2,1,0:T(8,128)(2,1)S(1)}, u32[]{:S(2)}, u32[]{:S(2)}) async-start(bf16[64,5,1536]{2,1,0:T(8,128)(2,1)} %bitcast.108), calls=%async_computation | async-start | bytes 3145728 | tf_op jit(solution)/shard_map/all_to_all | solution.py:99
  58.1 157.6 %all-gather.4.cloned.1.call-start = ((), (), s32[]{:S(2)}) async-start(), calls=%async_computation.5 | async-start | bytes 1327104 | tf_op jit(solution)/shard_map/all_gather | solution.py:94
  128.6 1.7 copy-start.1
  130.3 83.1 %all-to-all-start.2 = ((bf16[64,5,1536]{2,1,0:T(8,128)(2,1)}), bf16[64,5,1536]{2,1,0:T(8,128)(2,1)}, u32[]{:S(2)}, u32[]{:S(2)}) async-start(bf16[64,5,1536]{2,1,0:T(8,128)(2,1)} %bitcast.107), calls=%async_computation.2 | async-start | bytes 3145728 | tf_op jit(solution)/shard_map/all_to_all | solution.py:114
  143.1 75.3 %all-gather.6.cloned.1.call-start = ((), (), s32[]{:S(2)}) async-start(), calls=%async_computation.6 | async-start | bytes 1327104 | tf_op jit(solution)/shard_map/all_gather | solution.py:95
  143.9 77.3 %all-gather.8.cloned.1.call-start = ((), (), s32[]{:S(2)}) async-start(), calls=%async_computation.7 | async-start | bytes 1327104 | tf_op jit(solution)/shard_map/all_gather | solution.py:97
  221.2 3.4 copy-start.3
  224.6 0.7 copy-start.8
  224.6 0.8 copy-start.10
  224.6 1.4 copy-start.4
  228.2 13.2 %copy-start.12 = (bf16[320,384]{1,0:T(8,128)(2,1)S(1)}, bf16[320,384]{1,0:T(8,128)(2,1)}, u32[]{:S(2)}) copy-start(bf16[320,384]{1,0:T(8,128)(2,1)} %get-tuple-element.47) | copy-start | bytes 737284
  228.2 83.5 %all-to-all-start.3 = ((bf16[64,5,1536]{2,1,0:T(8,128)(2,1)}), bf16[64,5,1536]{2,1,0:T(8,128)(2,1)}, u32[]{:S(2)}, u32[]{:S(2)}) async-start(bf16[64,5,1536]{2,1,0:T(8,128)(2,1)} %reshape.233), calls=%async_computation.3 | async-start | bytes 3145728 | tf_op jit(solution)/shard_map/all_to_all | solution.py:138
  244.8 2.1 copy-start.11
  246.9 1.9 copy-start.9
  311.7 83.2 %all-to-all-start.1 = ((bf16[64,5,1536]{2,1,0:T(8,128)(2,1)}), bf16[64,5,1536]{2,1,0:T(8,128)(2,1)}, u32[]{:S(2)}, u32[]{:S(2)}) async-start(bf16[64,5,1536]{2,1,0:T(8,128)(2,1)} %reshape.227), calls=%async_computation.1 | async-start | bytes 3145728 | tf_op jit(solution)/shard_map/all_to_all | solution.py:113
  324.6 120.2 %reduce-scatter.4.cloned.1.call-start = ((), (), s32[]{:S(2)}) async-start(), calls=%async_computation.8 | async-start | bytes 3981312
  333.7 1.0 copy-start.5
  423.5 5.1 %copy-start.2 = (f32[128,2,1536]{2,1,0:T(2,128)S(1)}, f32[128,2,1536]{2,1,0:T(2,128)}, u32[]{:S(2)}) copy-start(f32[128,2,1536]{2,1,0:T(2,128)} %reshape.235) | copy-start | bytes 4718596
  431.5 1.9 copy-start.20
  431.5 1.9 copy-start.6
  431.5 1.9 copy-start.7
  431.5 1.9 copy-start.18
  434.6 8.2 %collective-permute-start.3 = (bf16[1,64,1536]{2,1,0:T(8,128)(2,1)S(1)}, bf16[1,64,1536]{2,1,0:T(8,128)(2,1)S(1)}, u32[]{:S(2)}, u32[]{:S(2)}) collective-permute-start(bf16[1,64,1536]{2,1,0:T(8,128)(2,1)S(1)} %get-tuple-element.53), channel_id=1, source_target_pairs={{8,0},{16,8},{24,16},{32,24},{40,32},{48,40},{56,48},{64,56},{72,6... | collective-permute-start | bytes 589832 | tf_op jit(solution)/shard_map/ppermute | solution.py:19
  435.9 7.8 %collective-permute-start.2 = (bf16[1,64,1536]{2,1,0:T(8,128)(2,1)S(1)}, bf16[1,64,1536]{2,1,0:T(8,128)(2,1)S(1)}, u32[]{:S(2)}, u32[]{:S(2)}) collective-permute-start(bf16[1,64,1536]{2,1,0:T(8,128)(2,1)S(1)} %get-tuple-element.52), channel_id=1, source_target_pairs={{0,8},{8,16},{16,24},{24,32},{32,40},{40,48},{48,56},{56,64},{64,7... | collective-permute-start | bytes 589832 | tf_op jit(solution)/shard_map/ppermute | solution.py:17
Sparse Core Ops, SparseCore 0:
  61.1 33.4 all-gather.3
  146.1 32.8 all-gather.5
  181.1 31.0 all-gather.7
  333.8 44.5 reduce-scatter.3
where the time goes:
time: 460 us; the launch traced here: 455 us
  waiting for transfers between devices  240 us (52%)
  starting transfers between devices  68.9 us (15%)
  local copies, waits for them, and re-layouts  52.1 us (11%)
  blocking collectives  35.8 us (8%)
  other arithmetic  22.8 us (5%)
  matrix products  21 us (5%)
  between operations  14.3 us (3%)
    all_to_all x1, waiting for transfers between devices, local(): lax.all_to_all(fan_rows, 'exp', split_axis=0, concat_axis=0, tiled=True)  69.7 us
    all_to_all x1, waiting for transfers between devices, local(): lax.all_to_all(fan_grads, 'exp', split_axis=0, concat_axis=0, tiled=True)  67.1 us
    all_to_all x1, waiting for transfers between devices, local(): lax.all_to_all(back, 'exp', split_axis=0, concat_axis=0, tiled=True)  61.1 us
    all_to_all x1, waiting for transfers between devices, local(): lax.all_to_all(part, 'exp', split_axis=0, concat_axis=0, tiled=True)  36.8 us
    all_gather x1, blocking collectives, local(): lax.all_gather(group_out, 'rep', axis=1, tiled=True)  20.9 us
    all_to_all x1, starting transfers between devices, local(): lax.all_to_all(fan_rows, 'exp', split_axis=0, concat_axis=0, tiled=True)  18.1 us
    all_gather x1, blocking collectives, local(): lax.all_gather(group_back, 'rep', axis=1, tiled=True)  14.9 us
    all_to_all x1, starting transfers between devices, local(): lax.all_to_all(back, 'exp', split_axis=0, concat_axis=0, tiled=True)  13.1 us
  transfers between devices with their start and end apart: 12, of which 6 were waited for; matrix products, arithmetic and copies ran while one was open for 15% of the time, Pallas kernels for 0%

commit v1 on v0

v1 whole, which is shorter than its diff:
```python
import jax
import jax.numpy as jnp
from jax import lax
from jax.sharding import PartitionSpec as P

CAP = 40
F32 = jnp.float32
BF = jnp.bfloat16


def dot32(a, b, dims=None):
    if dims is None:
        return jnp.dot(a, b, preferred_element_type=F32)
    return lax.dot_general(a, b, (dims, ((), ())), preferred_element_type=F32)


def split(v):
    hi = v.astype(BF)
    return hi, (v - hi.astype(F32)).astype(BF)


def halo(cells):
    count = lax.axis_size("exp")
    head, tail = cells[:1], cells[-1:]
    return jnp.concatenate(
        [
            lax.ppermute(tail, "exp", [(i, i + 1) for i in range(count - 1)]),
            cells,
            lax.ppermute(head, "exp", [(i + 1, i) for i in range(count - 1)]),
        ],
        axis=0,
    )


def gating(picked):
    chosen = jax.nn.sigmoid(picked)
    return chosen / jnp.sum(chosen, axis=-1, keepdims=True)


def local(latent, stem_weight, norm_gain, router_weight, routes, gate_weight, up_weight, down_weight, grad_mixed):
    rows_here, channels, width = latent.shape
    taps, model_width = stem_weight.shape
    experts = router_weight.shape[1]
    top = routes.shape[1]
    tok = rows_here * width
    nrep = lax.axis_size("rep")
    nexp = lax.axis_size("exp")
    shards = nexp // experts
    sub = CAP // nrep
    rep = lax.axis_index("rep")
    across = [[e * shards + m for e in range(experts)] for m in range(shards)]
    along = [[e * shards + m for m in range(shards)] for e in range(experts)]

    dsl = model_width // nrep
    s_here = lax.dynamic_slice_in_dim(stem_weight, rep * dsl, dsl, 1)
    gain_here = lax.dynamic_slice_in_dim(norm_gain, rep * dsl, dsl, 0)
    sg_hi, sg_lo = split(s_here.astype(F32) * gain_here)
    w2 = jnp.concatenate([gate_weight, up_weight], axis=1)
    g_full = lax.psum(dot32(sg_hi, w2) + dot32(sg_lo, w2), "rep")
    g_hi, g_lo = split(g_full)
    down = lax.all_gather(down_weight, "rep", axis=1, tiled=True)

    padded = jnp.pad(halo(latent), ((0, 0), (0, 0), (1, 1)))
    pieces = jnp.stack([padded[i : i + rows_here, :, j : j + width] for i in range(3) for j in range(3)], axis=0)
    patches = jnp.transpose(pieces, (1, 3, 0, 2)).reshape(tok, taps)
    stem = dot32(patches, stem_weight).astype(BF)
    sv = stem.astype(F32)
    rstd = lax.rsqrt(jnp.mean(sv * sv, axis=-1, keepdims=True) + 1e-06)
    normed = (sv * rstd * norm_gain).astype(BF)
    logits = dot32(normed, router_weight)
    selector = (routes[:, :, None] == jnp.arange(experts, dtype=jnp.int32)).astype(F32)
    picked = jnp.sum(logits[:, None, :] * selector, axis=-1)
    gates = gating(picked)

    sel_i = selector.astype(jnp.int32)
    both = jnp.sum(sel_i, axis=1)
    before = jnp.cumsum(both, axis=0) - both
    position = jnp.sum(sel_i * before[:, None, :], axis=-1)
    slot = routes * CAP + position
    slot_ids = jnp.arange(experts * CAP, dtype=jnp.int32)
    hot = [(slot[:, k][:, None] == slot_ids[None, :]) for k in range(top)]
    hot_here = [
        lax.dynamic_slice_in_dim(h.reshape(tok, experts, CAP), rep * sub, sub, 2).reshape(tok, experts * sub) for h in hot
    ]
    hot_any = sum(h.astype(BF) for h in hot_here)
    rstd_parts = split(rstd)
    gate_parts = [split(gates[:, k][:, None]) for k in range(top)]
    wide = jnp.concatenate(
        [grad_mixed, patches, rstd_parts[0], rstd_parts[1], jnp.zeros((tok, 110), BF)], axis=1
    )
    send = dot32(hot_any, wide, (((0,), (0,)))).astype(BF)
    send_gate = sum(
        dot32(hot_here[k].astype(BF), jnp.concatenate(gate_parts[k], axis=1), ((0,), (0,))) for k in range(top)
    ).astype(BF)
    send = jnp.concatenate([send[:, : model_width + 146], send_gate, send[:, model_width + 148 :]], axis=1)
    send = send.reshape(experts, sub, -1)
    stage = lax.all_to_all(send, "exp", split_axis=0, concat_axis=0, tiled=True, axis_index_groups=across)
    recv = lax.all_gather(stage, "exp", axis=0, tiled=True, axis_index_groups=along)
    flat = recv.reshape(-1, recv.shape[-1])
    gm = flat[:, :model_width]
    pr = flat[:, model_width : model_width + taps]
    extra = flat[:, model_width + taps : model_width + taps + 4].astype(F32)
    rs = extra[:, 0:1] + extra[:, 1:2]
    gt = extra[:, 2:3] + extra[:, 3:4]

    hid = gate_weight.shape[1]
    pre = rs * (dot32(pr, g_hi) + dot32(pr, g_lo))
    pg, pu = pre[:, :hid], pre[:, hid:]
    sigma = jax.nn.sigmoid(pg)
    hidden = pg * sigma * pu
    hg = (gt * hidden).astype(BF)
    out = dot32(hg, down)
    u = dot32(gm, down, ((1,), (1,)))
    gg = jnp.sum(hidden * u, axis=-1, keepdims=True)
    gu = (rs * gt) * u
    dpre = jnp.concatenate([gu * pu * sigma * (1.0 + pg * (1.0 - sigma)), gu * pg * sigma], axis=1).astype(BF)
    back = dot32(dpre, g_hi, ((1,), (1,))) + dot32(dpre, g_lo, ((1,), (1,)))
    t_part = dot32(pr, dpre, ((0,), (0,)))
    d_part = dot32(gm, hg, ((0,), (0,)))
    gg_hi, gg_lo = split(gg)
    ret = jnp.concatenate(
        [out.astype(BF), back.astype(BF), gg_hi, gg_lo, jnp.zeros((out.shape[0], 110), BF)], axis=1
    ).reshape(shards, experts, sub, -1)
    summed = lax.psum_scatter(ret, "exp", scatter_dimension=0, axis_index_groups=along, tiled=True)[0]
    mine = lax.all_to_all(summed, "exp", split_axis=0, concat_axis=0, tiled=True, axis_index_groups=across)
    slots_back = lax.all_gather(mine, "rep", axis=1, tiled=True).reshape(experts * CAP, -1)

    t_full = lax.psum(t_part, "rep")
    t_hi, t_lo = split(t_full)
    gw = (dot32(s_here, t_hi, ((0,), (0,))) + dot32(s_here, t_lo, ((0,), (0,)))) * gain_here[:, None]
    grad_gate, grad_up = gw[:, :hid], gw[:, hid:]
    grad_down = lax.psum_scatter(d_part.astype(BF), "rep", scatter_dimension=0, tiled=True).astype(F32).T

    hot_sum = sum(h.astype(BF) for h in hot)
    tok_sum = dot32(hot_sum, slots_back)
    mixed = (sv + tok_sum[:, :model_width]).astype(BF)
    ggs = slots_back[:, model_width + taps : model_width + taps + 2]
    grad_gates = jnp.concatenate(
        [jnp.sum(dot32(hot[k].astype(BF), ggs), axis=-1, keepdims=True) for k in range(top)], axis=1
    )
    _, gate_pull = jax.vjp(gating, picked)
    grad_picked = gate_pull(grad_gates)[0]
    grad_logits = jnp.sum(selector * grad_picked[:, :, None], axis=1)
    sg_all = stem_weight.astype(F32) * norm_gain
    rproj = jnp.dot(sg_all, router_weight.astype(F32), precision=lax.Precision.HIGHEST)
    b = tok_sum[:, model_width : model_width + taps] + rstd * jnp.dot(
        grad_logits, rproj.T, precision=lax.Precision.HIGHEST
    )
    c = jnp.sum(patches.astype(F32) * b, axis=-1, keepdims=True) * (rstd * rstd / model_width)
    proj = dot32(grad_mixed, stem_weight, ((1,), (1,))) + b - c * dot32(stem, stem_weight, ((1,), (1,)))
    block = halo(proj.reshape(rows_here, width, taps)).reshape(rows_here + 2, width, 9, channels)
    shifted = jnp.pad(block, ((0, 0), (1, 1), (0, 0), (0, 0)))
    terms = [
        shifted[2 - i : 2 - i + rows_here, 2 - j : 2 - j + width, 3 * i + j, :] for i in range(3) for j in range(3)
    ]
    grad_latent = sum(terms).transpose(0, 2, 1)
    return (mixed, grad_latent, grad_gate, grad_up, grad_down)


def solution(mesh):
    return jax.shard_map(
        local,
        mesh=mesh,
        in_specs=(
            P("exp", None, None),
            P(),
            P(),
            P(),
            P("exp", None),
            P("rep", "exp"),
            P("rep", "exp"),
            P("exp", "rep"),
            P("exp", None),
        ),
        out_specs=(P("exp", None), P("exp", None, None), P("rep", "exp"), P("rep", "exp"), P("exp", "rep")),
        check_vma=False,
    )
```

time: 460 us -> 312 us (0.68)
  waiting for transfers between devices: 240 us -> 177 us
  starting transfers between devices: 68.9 us -> 10 us
  local copies, waits for them, and re-layouts: 52.1 us -> 19.4 us
  blocking collectives: 35.8 us -> 58.8 us
  other arithmetic: 22.8 us -> 9.22 us
    all_to_all x4 -> x0, waiting for transfers between devices: 235 us -> none  [the longest x1 69.7 us: local(): lax.all_to_all(fan_rows, 'exp', split_axis=0, concat_axis=0, tiled=True)]
    all_gather x3, waiting for transfers between devices: 0.01 us -> 86.1 us  [the longest x1 58.4 us: local(): lax.all_gather(stage, 'exp', axis=0, tiled=True, axis_index_groups=along)]
    reduce_scatter x0 -> x2, waiting for transfers between devices: none -> 74 us  [the longest x1 60.4 us: local(): lax.psum_scatter(ret, 'exp', scatter_dimension=0, axis_index_groups=along...]
    all_to_all x0 -> x2, blocking collectives: none -> 58.8 us  [the longest x1 33.3 us: local(): lax.all_to_all(send, 'exp', split_axis=0, concat_axis=0, tiled=True, axis...]
    all_to_all x4 -> x0, starting transfers between devices: 57 us -> none  [the longest x1 18.1 us: local(): lax.all_to_all(fan_rows, 'exp', split_axis=0, concat_axis=0, tiled=True)]
    all_gather x2 -> x0, blocking collectives: 35.8 us -> none  [the longest x1 20.9 us: local(): lax.all_gather(group_out, 'rep', axis=1, tiled=True)]
    reshape x8 -> x6, local copies, waits for them, and re-layouts: 16 us -> 1.61 us  [the longest x1 1.31 us: local(): flat = recv.reshape(-1, recv.shape[-1])]
    psum x0 -> x2, waiting for transfers between devices: none -> 13.2 us  [the longest x1 13.2 us: local(): g_full = lax.psum(dot32(sg_hi, w2) + dot32(sg_lo, w2), 'rep')]
  transfers between devices with their start and end apart: 12 -> 11, of which waited for: 6 -> 8; matrix products, arithmetic and copies ran while one was open for 15% -> 7% of each run, Pallas kernels for 0% -> 0%
where the time goes in v1:
time: 312 us; the launch traced here: 309 us
  waiting for transfers between devices  177 us (57%)
  blocking collectives  58.8 us (19%)
  local copies, waits for them, and re-layouts  19.4 us (6%)
  matrix products  18.2 us (6%)
  between operations  16 us (5%)
  starting transfers between devices  10 us (3%)
  other arithmetic  9.22 us (3%)
    reduce_scatter x1, waiting for transfers between devices, local(): lax.psum_scatter(ret, 'exp', scatter_dimension=0, axis_index_groups=along...  60.4 us
    all_gather x1, waiting for transfers between devices, local(): lax.all_gather(stage, 'exp', axis=0, tiled=True, axis_index_groups=along)  58.4 us
    all_to_all x1, blocking collectives, local(): lax.all_to_all(send, 'exp', split_axis=0, concat_axis=0, tiled=True, axis...  33.3 us
    all_to_all x1, blocking collectives, local(): lax.all_to_all(summed, 'exp', split_axis=0, concat_axis=0, tiled=True, ax...  25.5 us
    all_gather x1, waiting for transfers between devices, local(): lax.all_gather(mine, 'rep', axis=1, tiled=True).reshape(experts * CAP, -1)  14 us
    all_gather x1, waiting for transfers between devices, local(): down = lax.all_gather(down_weight, 'rep', axis=1, tiled=True)  13.6 us
    reduce_scatter x1, waiting for transfers between devices, local(): lax.psum_scatter(d_part.astype(BF), 'rep', scatter_dimension=0, tiled=True)  13.6 us
    psum x1, waiting for transfers between devices, local(): g_full = lax.psum(dot32(sg_hi, w2) + dot32(sg_lo, w2), 'rep')  13.2 us
  transfers between devices with their start and end apart: 11, of which 8 were waited for; matrix products, arithmetic and copies ran while one was open for 7% of the time, Pallas kernels for 0%

profile of v1, /device:TPU:1, one launch (start us, length us, event | category | flops | bytes accessed | tf_op | source)
XLA Modules:
  0.0 309.1 jit_solution(7389787148921936075)
XLA Ops:
  8.1 0.8 fusion.85
  8.8 4.3 %collective-permute-start = (bf16[1,16,64]{2,1,0:T(8,128)(2,1)S(1)}, bf16[1,16,64]{2,1,0:T(8,128)(2,1)S(1)}, u32[]{:S(2)}, u32[]{:S(2)}) collective-permute-start(bf16[1,16,64]{2,1,0:T(8,128)(2,1)S(1)} %get-tuple-element.47), channel_id=1, source_target_pairs={{0,8},{8,16},{16,24},{24,32},{32,40},{40,48},{48,56},{56,64},{64,7... | collective-permute-start | bytes 6152 | tf_op jit(solution)/shard_map/ppermute | solution.py:27
  13.2 1.3 collective-permute-start.1
  14.5 0.7 convert_reduce_fusion
  15.5 0.7 multiply_reduce_fusion.3
  16.3 0.7 multiply_add_fusion.1
  17.2 0.6 collective-permute-done.1
  17.7 0.8 fusion.59
  18.5 0.8 constant_dynamic-update-slice_fusion.7
  19.4 0.7 constant_dynamic-update-slice_fusion.4
  20.2 0.7 constant_dynamic-update-slice_fusion.1
  23.3 33.3 %all_to_all.10 = bf16[8,5,1792]{2,1,0:T(8,128)(2,1)S(1)} all-to-all(bf16[8,5,1792]{2,1,0:T(8,128)(2,1)S(1)} %reshape.239), channel_id=1, replica_groups={{0,64,128,192,256,320,384,448},{8,72,136,200,264,328,392,456},{16,80,14..., dimensions={0} | all-to-all | bytes 286720 | tf_op jit(solution)/shard_map/all_to_all | solution.py:97
  56.6 0.7 copy.149
  57.8 1.1 convolution_add_fusion.2
  58.9 0.7 all-gather.6.cloned.1.call-update
  59.6 58.4 %all-gather.4.cloned.1.call-done = bf16[64,5,1792]{2,0,1:T(8,128)(2,1)} async-done(((bf16[8,5,1792]{2,0,1:T(8,128)(2,1)}), bf16[64,5,1792]{2,0,1:T(8,128)(2,1)}) %all-gather.4.cloned.1.call-update) | async-done | bytes 1146896 | tf_op jit(solution)/shard_map/all_gather | solution.py:98
  118.1 1.9 copy.150
  120.0 1.3 reshape.240
  121.3 1.0 slice_convert_fusion
  122.7 13.2 %all-reduce.5.cloned.1.call-done = f32[144,768]{1,0:T(8,128)} async-done(((f32[144,768]{1,0:T(8,128)}), f32[144,768]{1,0:T(8,128)}) %all-reduce.5.cloned.1.call-update) | async-done | bytes 442384 | tf_op jit(solution)/shard_map/psum | solution.py:59
  135.9 1.4 fusion.29
  137.3 1.2 fusion
  138.5 13.6 %all-gather.6.cloned.1.call-done = bf16[384,1536]{0,1:T(8,128)(2,1)} async-done(((bf16[384,192]{0,1:T(8,128)(2,1)}), bf16[384,1536]{0,1:T(8,128)(2,1)}) %all-gather.6.cloned.1.call-update) | async-done | bytes 1179664 | tf_op jit(solution)/shard_map/all_gather | solution.py:61
  152.1 3.2 %multiply_convert_fusion.1 = (bf16[320,384]{1,0:T(8,128)(2,1)S(1)}, bf16[320,384]{1,0:T(8,128)(2,1)S(1)}, f32[320]{0:T(512)S(1)}, f32[320,384]{1,0:T(8,128)}) fusion(f32[320,768]{1,0:T(8,128)} %fusion, f32[320]{0:T(512)S(1)} %get-tuple-element.30, bf16[384,1536]{0,1:T(8,128)(2,1)} %all-gather.6.cloned.1.call-done, bf16[320,1792]{1,0:T(8,128)(2,1)S(1)} %copy-done.3), kind=kOutput, calls=%fused_computation.36 | convolution fusion | flops 379698880 | bytes 4132096 | tf_op jit(solution)/shard_map/dot_general | solution.py:14
  155.6 1.0 copy.155
  156.6 1.0 copy.154
  158.4 0.8 concatenate.73
  159.2 2.0 convolution_convert_fusion.1
  161.7 3.5 %concatenate.74 = bf16[8,8,5,1792]{3,2,1,0:T(8,128)(2,1)} concatenate(bf16[8,8,5,1536]{3,2,1,0:T(8,128)(2,1)S(1)} %concatenate.71, bf16[8,8,5,144]{3,2,1,0:T(8,128)(2,1)} %concatenate.73, bf16[8,8,5,1]{3,2,1,0:T(8,128)(2,1)} %copy.154, bf16[8,8,5,1]{3,2,1,0:T(8,128)(2,1)} %copy.155, bf16[8,8,5,110]{3,2,1,0:T(8,128)(2,1)S(1)} %broadcast_in_dim.9), dimensions={3} | concatenate | bytes 2293760 | tf_op jit(solution)/shard_map/concatenate | solution.py:121
  165.3 1.2 copy-done.4
  166.5 1.1 fusion.25
  167.7 2.0 convolution_convert_fusion
  169.8 60.4 %reduce-scatter.3.cloned.1.call-done = bf16[1,8,5,1792]{3,2,1,0:T(8,128)(2,1)} async-done(((bf16[8,8,5,1792]{3,2,1,0:T(8,128)(2,1)}), bf16[1,8,5,1792]{3,2,1,0:T(8,128)(2,1)}) %reduce-scatter.3.cloned.1.call-update) | async-done | bytes 143376 | tf_op jit(solution)/shard_map/reduce_scatter | solution.py:124
  230.2 25.5 %all_to_all.11 = bf16[8,5,1792]{2,1,0:T(8,128)(2,1)S(1)} all-to-all(bf16[8,5,1792]{2,1,0:T(8,128)(2,1)} %bitcast.103), channel_id=1, replica_groups={{0,64,128,192,256,320,384,448},{8,72,136,200,264,328,392,456},{16,80,14..., dimensions={0} | all-to-all | bytes 286720 | tf_op jit(solution)/shard_map/all_to_all | solution.py:125
  255.7 0.7 copy.156
  256.4 0.6 fusion.6
  257.0 1.4 fusion.32
  258.8 0.9 fusion.84
  259.6 13.6 %reduce-scatter.5.cloned.1.call-done = bf16[192,384]{1,0:T(8,128)(2,1)} async-done(((bf16[1536,384]{1,0:T(8,128)(2,1)}), bf16[192,384]{1,0:T(8,128)(2,1)}) %reduce-scatter.5.cloned.1.call-update) | async-done | bytes 147472 | tf_op jit(solution)/shard_map/reduce_scatter | solution.py:132
  273.2 1.6 convert_bitcast_fusion
  274.9 14.0 %all-gather.8.cloned.1.call-done = bf16[8,40,1792]{2,0,1:T(8,128)(2,1)} async-done(((bf16[8,5,1792]{2,0,1:T(8,128)(2,1)}), bf16[8,40,1792]{2,0,1:T(8,128)(2,1)}) %all-gather.8.cloned.1.call-update) | async-done | bytes 1146896 | tf_op jit(solution)/shard_map/all_gather | solution.py:126
  288.9 1.4 copy.157
  292.6 2.8 collective-permute-start.2
  295.4 1.3 collective-permute-start.3
  296.7 0.8 fusion.15
  297.7 2.8 collective-permute-done.3
  300.5 0.5 select_maximum_fusion
  301.2 0.6 copy.163
  (121 shorter events, 8.7 us)
Async XLA Ops:
  8.0 13.6 %copy-start = (bf16[1536,8]{0,1:T(8,128)(2,1)S(1)}, bf16[1536,8]{0,1:T(8,128)(2,1)}, u32[]{:S(2)}) copy-start(bf16[1536,8]{0,1:T(8,128)(2,1)} %param.12) | copy-start | bytes 73732
  8.0 13.2 %copy-start.1 = (bf16[144,1536]{1,0:T(8,128)(2,1)S(1)}, bf16[144,1536]{1,0:T(8,128)(2,1)}, u32[]{:S(2)}) copy-start(bf16[144,1536]{1,0:T(8,128)(2,1)} %param.10) | copy-start | bytes 1327108
  8.0 13.6 %copy-start.17 = (f32[1536]{0:T(1024)S(1)}, f32[1536]{0:T(1024)}, u32[]{:S(2)}) copy-start(f32[1536]{0:T(1024)} %param.11) | copy-start | bytes 18436
  8.0 110.1 %all-gather.4.cloned.1.call-start = ((), (), s32[]{:S(2)}) async-start(), calls=%async_computation.4 | async-start | bytes 1290240 | tf_op jit(solution)/shard_map/all_gather | solution.py:98
  8.8 8.3 %collective-permute-start = (bf16[1,16,64]{2,1,0:T(8,128)(2,1)S(1)}, bf16[1,16,64]{2,1,0:T(8,128)(2,1)S(1)}, u32[]{:S(2)}, u32[]{:S(2)}) collective-permute-start(bf16[1,16,64]{2,1,0:T(8,128)(2,1)S(1)} %get-tuple-element.47), channel_id=1, source_target_pairs={{0,8},{8,16},{16,24},{24,32},{32,40},{40,48},{48,56},{56,64},{64,7... | collective-permute-start | bytes 6152 | tf_op jit(solution)/shard_map/ppermute | solution.py:27
  13.2 4.5 %collective-permute-start.1 = (bf16[1,16,64]{2,1,0:T(8,128)(2,1)S(1)}, bf16[1,16,64]{2,1,0:T(8,128)(2,1)S(1)}, u32[]{:S(2)}, u32[]{:S(2)}) collective-permute-start(bf16[1,16,64]{2,1,0:T(8,128)(2,1)S(1)} %get-tuple-element.48), channel_id=1, source_target_pairs={{8,0},{16,8},{24,16},{32,24},{40,32},{48,40},{56,48},{64,56},{72,6... | collective-permute-start | bytes 6152 | tf_op jit(solution)/shard_map/ppermute | solution.py:29
  15.5 6.5 %copy-start.16 = (s32[128,2]{0,1:T(2,128)S(1)}, s32[128,2]{0,1:T(2,128)}, u32[]{:S(2)}) copy-start(s32[128,2]{0,1:T(2,128)} %param.13) | copy-start | bytes 3076
  18.5 4.2 %copy-start.6 = (bf16[128,1536]{1,0:T(8,128)(2,1)S(1)}, bf16[128,1536]{1,0:T(8,128)(2,1)}, u32[]{:S(2)}) copy-start(bf16[128,1536]{1,0:T(8,128)(2,1)} %param.17) | copy-start | bytes 1179652
  22.8 34.6 %copy-start.14 = (bf16[192,384]{1,0:T(8,128)(2,1)S(1)}, bf16[192,384]{1,0:T(8,128)(2,1)}, u32[]{:S(2)}) copy-start(bf16[192,384]{1,0:T(8,128)(2,1)} %param.14) | copy-start | bytes 442372
  22.8 34.6 %copy-start.15 = (bf16[192,384]{1,0:T(8,128)(2,1)S(1)}, bf16[192,384]{1,0:T(8,128)(2,1)}, u32[]{:S(2)}) copy-start(bf16[192,384]{1,0:T(8,128)(2,1)} %param.15) | copy-start | bytes 442372
  57.3 78.6 %all-reduce.5.cloned.1.call-start = ((), (), s32[]{:S(2)}) async-start(), calls=%async_computation.5 | async-start | bytes 884736 | tf_op jit(solution)/shard_map/psum | solution.py:59
  58.8 93.3 %all-gather.6.cloned.1.call-start = ((), (), s32[]{:S(2)}) async-start(), calls=%async_computation.6 | async-start | bytes 1327104 | tf_op jit(solution)/shard_map/all_gather | solution.py:61
  59.6 170.6 %reduce-scatter.3.cloned.1.call-start = ((), (), s32[]{:S(2)}) async-start(), calls=%async_computation.7 | async-start | bytes 2064384 | tf_op jit(solution)/shard_map/reduce_scatter | solution.py:124
  122.3 15.0 %copy-start.3 = (bf16[320,1792]{1,0:T(8,128)(2,1)S(1)}, bf16[320,1792]{1,0:T(8,128)(2,1)}, u32[]{:S(2)}) copy-start(bf16[320,1792]{1,0:T(8,128)(2,1)} %reshape.240) | copy-start | bytes 3440644
  135.9 1.4 copy-start.2
  155.3 2.9 copy-start.8
  155.3 3.0 copy-start.10
  157.9 1.3 copy-start.12
  165.2 1.3 copy-start.4
  165.2 1.3 copy-start.9
  165.2 1.4 copy-start.11
  165.2 2.5 copy-start.13
  165.2 91.8 %all-reduce.7.cloned.1.call-start = ((), (), s32[]{:S(2)}) async-start(), calls=%async_computation.9 | async-start | bytes 884736 | tf_op jit(solution)/shard_map/psum | solution.py:128
  167.7 105.6 %reduce-scatter.5.cloned.1.call-start = ((), (), s32[]{:S(2)}) async-start(), calls=%async_computation.10 | async-start | bytes 1327104 | tf_op jit(solution)/shard_map/reduce_scatter | solution.py:132
  169.7 119.2 %all-gather.8.cloned.1.call-start = ((), (), s32[]{:S(2)}) async-start(), calls=%async_computation.8 | async-start | bytes 1290240 | tf_op jit(solution)/shard_map/all_gather | solution.py:126
  257.0 1.4 copy-start.5
  290.9 1.0 copy-start.7
  292.6 5.1 %collective-permute-start.2 = (f32[1,64,144]{1,2,0:T(8,128)S(1)}, f32[1,64,144]{1,2,0:T(8,128)S(1)}, u32[]{:S(2)}, u32[]{:S(2)}) collective-permute-start(f32[1,64,144]{1,2,0:T(8,128)S(1)} %get-tuple-element.45), channel_id=1, source_target_pairs={{0,8},{8,16},{16,24},{24,32},{32,40},{40,48},{48,56},{56,64},{64,7... | collective-permute-start | bytes 110600 | tf_op jit(solution)/shard_map/ppermute | solution.py:27
  295.4 5.1 %collective-permute-start.3 = (f32[1,64,144]{1,2,0:T(8,128)S(1)}, f32[1,64,144]{1,2,0:T(8,128)S(1)}, u32[]{:S(2)}, u32[]{:S(2)}) collective-permute-start(f32[1,64,144]{1,2,0:T(8,128)S(1)} %get-tuple-element.46), channel_id=1, source_target_pairs={{8,0},{16,8},{24,16},{32,24},{40,32},{48,40},{56,48},{64,56},{72,6... | collective-permute-start | bytes 110600 | tf_op jit(solution)/shard_map/ppermute | solution.py:29
Sparse Core Ops, SparseCore 0:
  57.4 60.6 all-gather.3
  120.2 31.8 all-gather.5
  165.3 64.7 reduce-scatter.2
  232.8 40.3 reduce-scatter.4
Sparse Core Ops, SparseCore 1:
  60.1 75.7 all-reduce.4
  168.1 75.6 all-reduce.6
  256.5 32.4 all-gather.7

commit v2 on v1

v2 whole, which is shorter than its diff:
```python
import jax
import jax.numpy as jnp
from jax import lax
from jax.experimental import pallas as pl
from jax.experimental.pallas import tpu as pltpu
from jax.sharding import PartitionSpec as P

F32 = jnp.float32
BF = jnp.bfloat16
EXP = 8
SH = 8
REP = 8
TILES = 5
ROWS = 8
TAPS = 192
TP = TAPS // REP
MESH = pl.DeviceIdType.MESH
VM = pl.BlockSpec(memory_space=pltpu.VMEM)


def dot32(a, b, dims=None):
    if dims is None:
        return jnp.dot(a, b, preferred_element_type=F32)
    return lax.dot_general(a, b, (dims, ((), ())), preferred_element_type=F32)


def split(v):
    hi = v.astype(BF)
    return hi, (v - hi.astype(F32)).astype(BF)


def rcopy(src, dst, ssem, rsem, exp, rep):
    return pltpu.make_async_remote_copy(
        src_ref=src, dst_ref=dst, send_sem=ssem, recv_sem=rsem, device_id={"exp": exp, "rep": rep}, device_id_type=MESH
    )


class Place:
    def __init__(self):
        self.exp = lax.axis_index("exp")
        self.rep = lax.axis_index("rep")
        self.e = self.exp // SH
        self.m = self.exp % SH
        self.y = self.rep // 2
        self.c = self.rep % 2
        self.tile = self.tile_of(self.rep)
        self.d = 1 - 2 * self.c
        self.fwd = self.rep_at(self.d)
        self.bwd = self.rep_at(-self.d)
        self.partner = self.y * 2 + 1 - self.c

    def rep_at(self, dy):
        return ((self.y + dy + 4) % 4) * 2 + self.c

    def tile_of(self, rep):
        return (rep + 3 * self.e) % 8

    def peers(self):
        return [((self.e + k) % EXP) * SH + self.m for k in range(1, EXP)]

    def enter(self):
        bar = pltpu.get_barrier_semaphore()

        def greet(exp, rep):
            pl.semaphore_signal(bar, inc=1, device_id={"exp": exp, "rep": rep}, device_id_type=MESH)

        for peer in self.peers():
            greet(peer, self.rep)
        for rep in (self.fwd, self.bwd, self.partner):
            greet(self.exp, rep)

        @pl.when(self.m > 0)
        def _():
            greet(self.exp - 1, self.rep)

        @pl.when(self.m < SH - 1)
        def _():
            greet(self.exp + 1, self.rep)

        pl.semaphore_wait(bar, 10 + (self.m > 0).astype(jnp.int32) + (self.m < SH - 1).astype(jnp.int32))


class Gather:
    def __init__(self, pc, src, piece, ssem, rsem, valid=None):
        self.pc, self.src, self.piece, self.ssem, self.rsem = pc, src, piece, ssem, rsem
        self.valid = valid

    def guard(self, rep, fn):
        if self.valid is None:
            fn()
        else:
            pl.when(self.valid(rep))(fn)

    def copy(self, src, rep_of, k, target):
        return rcopy(src, self.piece(rep_of), self.ssem.at[k], self.rsem.at[rep_of], self.pc.exp, target)

    def moves(self):
        pc = self.pc
        far = pc.rep_at(2)
        own, part = pc.rep, pc.partner
        return [
            (self.src, own, 0, pc.fwd),
            (self.src, own, 1, pc.bwd),
            (self.src, own, 2, part),
            (self.piece(pc.bwd), pc.bwd, 3, pc.fwd),
            (self.piece(pc.bwd), pc.bwd, 4, part),
            (self.piece(pc.fwd), pc.fwd, 5, part),
            (self.piece(far), far, 6, part),
        ]

    def start(self):
        def go():
            for mv in self.moves()[:3]:
                self.copy(*mv).start()

        self.guard(self.pc.rep, go)

    def arrive(self, rep):
        self.copy(self.piece(rep), rep, 0, self.pc.partner).wait_recv()

    def relay(self):
        mv = self.moves()

        def near():
            self.arrive(self.pc.bwd)
            self.copy(*mv[3]).start()
            self.copy(*mv[4]).start()

        self.guard(self.pc.bwd, near)

        def other():
            self.arrive(self.pc.fwd)
            self.copy(*mv[5]).start()

        self.guard(self.pc.fwd, other)

    def relay_far(self):
        far = self.pc.rep_at(2)

        def go():
            self.arrive(far)
            self.copy(*self.moves()[6]).start()

        self.guard(far, go)

    def finish(self):
        for dy in range(4):
            rep = ((self.pc.y + dy) % 4) * 2 + 1 - self.pc.c
            self.guard(rep, lambda rep=rep: self.arrive(rep))
        for mv in self.moves():
            self.guard(mv[1], lambda mv=mv: self.copy(*mv).wait_send())


class Scatter:
    def __init__(self, pc, src, got, total, side, ssem, rsem):
        self.pc, self.src, self.got, self.total, self.side, self.ssem, self.rsem = pc, src, got, total, side, ssem, rsem

    def copy(self, k):
        pc = self.pc
        y, d = pc.y, pc.d
        at = lambda dy: self.total.at[(y + dy + 4) % 4]
        src, dst, rep = (
            (self.src.at[1 - pc.c], self.got, pc.partner),
            (at(2), self.side.at[0], pc.fwd),
            (at(-d), self.side.at[1], pc.bwd),
            (at(d), self.side.at[2], pc.fwd),
        )[k]
        return rcopy(src, dst, self.ssem.at[k], self.rsem.at[k], pc.exp, rep)

    def start(self):
        self.copy(0).start()

    def add(self):
        self.copy(0).wait_recv()

        def body(k, _):
            self.total[k] = (self.src[self.pc.c, k].astype(F32) + self.got[k].astype(F32)).astype(self.total.dtype)
            return 0

        lax.fori_loop(0, 4, body, 0)
        self.copy(1).start()
        self.copy(2).start()

    def pass_on(self):
        pc = self.pc
        self.copy(1).wait_recv()
        at = (pc.y + pc.d + 4) % 4
        self.total[at] = (self.total[at].astype(F32) + self.side[0].astype(F32)).astype(self.total.dtype)
        self.copy(3).start()

    def result(self):
        self.copy(2).wait_recv()
        self.copy(3).wait_recv()
        return self.total[self.pc.y].astype(F32) + self.side[1].astype(F32) + self.side[2].astype(F32)

    def finish(self):
        for k in range(4):
            self.copy(k).wait_send()


def scatter_scratch(block, dtype):
    return [
        pltpu.VMEM((4,) + block, dtype),
        pltpu.VMEM((4,) + block, dtype),
        pltpu.VMEM((3,) + block, dtype),
        pltpu.SemaphoreType.DMA((4,)),
        pltpu.SemaphoreType.DMA((4,)),
    ]


def gather_scratch():
    return [pltpu.SemaphoreType.DMA((7,)), pltpu.SemaphoreType.DMA((REP,))]


def dispatch_kernel(
    send, gp, wd, recv, gfull, wfull,
    g_got, g_tot, g_side, g_ss, g_rs, gmine,
    ag_ss, ag_rs, wg_ss, wg_rs,
    st_ss, st_rs, ln_ss, ln_rs, loc,
):
    pc = Place()
    m = pc.m
    pc.enter()

    def stage(k):
        peer = (pc.e + k) % EXP
        return rcopy(send.at[peer], recv.at[m, pc.tile], st_ss.at[k], st_rs.at[pc.tile], peer * SH + m, pc.rep)

    own_copy = pltpu.make_async_copy(send.at[pc.e], recv.at[m, pc.tile], loc.at[0])

    @pl.when(pc.tile < TILES)
    def _():
        for k in (1, 7, 2, 6, 3, 5, 4):
            stage(k).start()
        own_copy.start()

    gather_w = Gather(pc, wd, lambda rep: wfull.at[rep], wg_ss, wg_rs)
    own_w = pltpu.make_async_copy(wd, wfull.at[pc.rep], loc.at[1])
    scatter_g = Scatter(pc, gp, g_got, g_tot, g_side, g_ss, g_rs)
    scatter_g.start()
    gather_w.start()
    own_w.start()
    scatter_g.add()
    scatter_g.pass_on()
    spot = lambda rep: gfull.at[(rep % 2) * 4 + rep // 2]
    gmine[...] = scatter_g.result()
    gather_g = Gather(pc, gmine, spot, ag_ss, ag_rs)
    own_g = pltpu.make_async_copy(gmine, spot(pc.rep), loc.at[2])
    gather_g.start()
    own_g.start()

    @pl.when(pc.tile < TILES)
    def _():
        own_copy.wait()

    def right(i, s):
        return rcopy(
            recv.at[m - s, i], recv.at[m - s, i], ln_ss.at[0, s, i], ln_rs.at[m - s, i], pc.exp + 1, pc.rep
        )

    def left(i, s):
        return rcopy(
            recv.at[m + s, i], recv.at[m + s, i], ln_ss.at[1, s, i], ln_rs.at[m + s, i], pc.exp - 1, pc.rep
        )

    can_right = lambda s: (m < SH - 1) & (m - s >= 0)
    can_left = lambda s: (m > 0) & (m + s < SH)

    def landed(p, i):
        rcopy(recv.at[p, i], recv.at[p, i], ln_ss.at[0, 0, i], ln_rs.at[p, i], pc.exp, pc.partner).wait_recv()

    def first(i, _):
        source = (5 * (pc.rep - i + 8)) % 8

        @pl.when(source != pc.e)
        def _():
            rcopy(recv.at[m, i], recv.at[m, i], st_ss.at[0], st_rs.at[i], pc.exp, pc.partner).wait_recv()

        @pl.when(can_right(0))
        def _():
            right(i, 0).start()

        @pl.when(can_left(0))
        def _():
            left(i, 0).start()

        return 0

    lax.fori_loop(0, TILES, first, 0)
    gather_w.relay()

    def step(n, _):
        s = n // TILES
        i = n % TILES

        @pl.when(m - s >= 0)
        def _():
            landed(m - s, i)

        @pl.when(can_right(s))
        def _():
            right(i, s).start()

        @pl.when(m + s < SH)
        def _():
            landed(m + s, i)

        @pl.when(can_left(s))
        def _():
            left(i, s).start()

        return 0

    lax.fori_loop(TILES, 2 * TILES, step, 0)
    gather_g.relay()
    gather_w.relay_far()
    lax.fori_loop(2 * TILES, 4 * TILES, step, 0)
    gather_g.relay_far()
    lax.fori_loop(4 * TILES, SH * TILES, step, 0)

    gather_w.finish()
    gather_g.finish()
    scatter_g.finish()
    own_w.wait()
    own_g.wait()

    @pl.when(pc.tile < TILES)
    def _():
        for k in range(1, EXP):
            stage(k).wait_send()

    def drain(n, _):
        s = n // TILES
        i = n % TILES

        @pl.when(can_right(s))
        def _():
            right(i, s).wait_send()

        @pl.when(can_left(s))
        def _():
            left(i, s).wait_send()

        return 0

    lax.fori_loop(0, SH * TILES, drain, 0)


def combine_kernel(
    part, dp, tp, slots, gd, tfull,
    acc_l, acc_r, sums,
    d_got, d_tot, d_side, d_ss, d_rs,
    t_got, t_tot, t_side, t_ss, t_rs, tmine,
    tg_ss, tg_rs, sg_ss, sg_rs,
    ln_ss, l_rs, r_rs, st_ss, st_rs, loc,
):
    pc = Place()
    m = pc.m
    pc.enter()
    scatter_d = Scatter(pc, dp, d_got, d_tot, d_side, d_ss, d_rs)
    scatter_t = Scatter(pc, tp, t_got, t_tot, t_side, t_ss, t_rs)

    def right(p, i):
        return rcopy(part.at[p, i], acc_l.at[p, i], ln_ss.at[p, i], l_rs.at[p, i], pc.exp + 1, pc.rep)

    def left(p, i):
        return rcopy(part.at[p, i], acc_r.at[p, i], ln_ss.at[p, i], r_rs.at[p, i], pc.exp - 1, pc.rep)

    def plus(p, i, acc):
        part[p, i] = (part[p, i].astype(F32) + acc[p, i].astype(F32)).astype(BF)

    def step(n, _):
        tau = n // TILES
        i = n % TILES
        p = 7 - tau + m

        @pl.when((tau >= m) & (m > 0))
        def _():
            right_in = rcopy(part.at[p, i], acc_l.at[p, i], ln_ss.at[p, i], l_rs.at[p, i], pc.exp, pc.partner)
            right_in.wait_recv()
            plus(p, i, acc_l)

        @pl.when((tau >= m) & (m < SH - 1))
        def _():
            right(p, i).start()

        q = tau - 7 + m

        @pl.when((q >= 0) & (m < SH - 1))
        def _():
            left_in = rcopy(part.at[q, i], acc_r.at[q, i], ln_ss.at[q, i], r_rs.at[q, i], pc.exp, pc.partner)
            left_in.wait_recv()
            plus(q, i, acc_r)

        @pl.when((q >= 0) & (m > 0))
        def _():
            left(q, i).start()

        return 0

    def steps(lo, hi):
        lax.fori_loop(lo * TILES, hi * TILES, step, 0)

    steps(0, 1)
    scatter_t.start()
    scatter_d.start()
    steps(1, 2)
    scatter_t.add()
    scatter_d.add()
    steps(2, 3)
    scatter_t.pass_on()
    scatter_d.pass_on()
    steps(3, 4)
    tmine[...] = scatter_t.result()
    spot = lambda rep: tfull.at[(rep % 2) * 4 + rep // 2]
    gather_t = Gather(pc, tmine, spot, tg_ss, tg_rs)
    own_t = pltpu.make_async_copy(tmine, spot(pc.rep), loc.at[0])
    gather_t.start()
    own_t.start()
    steps(4, 5)
    gd[...] = scatter_d.result()
    steps(5, 6)
    gather_t.relay()
    steps(6, 7)

    def give(i):
        source = (5 * (pc.rep - i + 8)) % 8
        return source, rcopy(
            sums.at[i], slots.at[i, pc.e], st_ss.at[i], st_rs.at[pc.e], source * SH + m, pc.rep
        )

    def keep(i):
        return pltpu.make_async_copy(sums.at[i], slots.at[i, pc.e], loc.at[1])

    def last(i, _):
        sums[i] = part[m, i]

        @pl.when(m > 0)
        def _():
            rcopy(part.at[m, i], acc_l.at[m, i], ln_ss.at[m, i], l_rs.at[m, i], pc.exp, pc.partner).wait_recv()
            sums[i] = (sums[i].astype(F32) + acc_l[m, i].astype(F32)).astype(BF)

        @pl.when(m < SH - 1)
        def _():
            rcopy(part.at[m, i], acc_r.at[m, i], ln_ss.at[m, i], r_rs.at[m, i], pc.exp, pc.partner).wait_recv()
            sums[i] = (sums[i].astype(F32) + acc_r[m, i].astype(F32)).astype(BF)

        source, copy = give(i)

        @pl.when(source != pc.e)
        def _():
            copy.start()

        @pl.when(source == pc.e)
        def _():
            keep(i).start()

        return 0

    lax.fori_loop(0, TILES, last, 0)
    gather_t.relay_far()

    @pl.when(pc.tile < TILES)
    def _():
        keep(pc.tile).wait()
        for k in range(1, EXP):
            e = (pc.e + k) % EXP
            rcopy(
                slots.at[pc.tile, e], slots.at[pc.tile, e], st_ss.at[0], st_rs.at[e], pc.exp, pc.partner
            ).wait_recv()

    def has_rows(rep):
        return pc.tile_of(rep) < TILES

    gather_s = Gather(
        pc, slots.at[pc.tile % TILES], lambda rep: slots.at[pc.tile_of(rep) % TILES], sg_ss, sg_rs, has_rows
    )
    gather_s.start()
    gather_s.relay()
    gather_s.relay_far()
    gather_t.finish()
    scatter_t.finish()
    scatter_d.finish()
    own_t.wait()

    def drain(n, _):
        p = n // TILES
        i = n % TILES

        @pl.when((p > m) & (m < SH - 1))
        def _():
            right(p, i).wait_send()

        @pl.when((p < m) & (m > 0))
        def _():
            left(p, i).wait_send()

        return 0

    lax.fori_loop(0, SH * TILES, drain, 0)

    def drain_last(i, _):
        source, copy = give(i)

        @pl.when(source != pc.e)
        def _():
            copy.wait_send()

        return 0

    lax.fori_loop(0, TILES, drain_last, 0)
    gather_s.finish()


def dispatch(send, gp, wd):
    width = send.shape[-1]
    return pl.pallas_call(
        dispatch_kernel,
        out_shape=(
            jax.ShapeDtypeStruct((SH, TILES, ROWS, width), BF),
            jax.ShapeDtypeStruct((REP,) + gp.shape[2:], F32),
            jax.ShapeDtypeStruct((REP,) + wd.shape, BF),
        ),
        in_specs=[VM] * 3,
        out_specs=(VM,) * 3,
        scratch_shapes=scatter_scratch(gp.shape[2:], F32)
        + [pltpu.VMEM(gp.shape[2:], F32)]
        + gather_scratch()
        + gather_scratch()
        + [
            pltpu.SemaphoreType.DMA((EXP,)),
            pltpu.SemaphoreType.DMA((TILES,)),
            pltpu.SemaphoreType.DMA((2, SH, TILES)),
            pltpu.SemaphoreType.DMA((SH, TILES)),
            pltpu.SemaphoreType.DMA((3,)),
        ],
        compiler_params=pltpu.CompilerParams(collective_id=0, has_side_effects=True),
        name="dispatch",
    )(send, gp, wd)


def combine(part, dp, tp):
    width = part.shape[-1]
    shape = part.shape
    return pl.pallas_call(
        combine_kernel,
        out_shape=(
            jax.ShapeDtypeStruct((TILES, EXP, ROWS, width), BF),
            jax.ShapeDtypeStruct(dp.shape[2:], F32),
            jax.ShapeDtypeStruct((REP,) + tp.shape[2:], F32),
        ),
        in_specs=[VM] * 3,
        out_specs=(VM,) * 3,
        scratch_shapes=[pltpu.VMEM(shape, BF), pltpu.VMEM(shape, BF), pltpu.VMEM(shape[1:], BF)]
        + scatter_scratch(dp.shape[2:], BF)
        + scatter_scratch(tp.shape[2:], F32)
        + [pltpu.VMEM(tp.shape[2:], F32)]
        + gather_scratch()
        + gather_scratch()
        + [
            pltpu.SemaphoreType.DMA((SH, TILES)),
            pltpu.SemaphoreType.DMA((SH, TILES)),
            pltpu.SemaphoreType.DMA((SH, TILES)),
            pltpu.SemaphoreType.DMA((TILES,)),
            pltpu.SemaphoreType.DMA((EXP,)),
            pltpu.SemaphoreType.DMA((2,)),
        ],
        compiler_params=pltpu.CompilerParams(collective_id=1, has_side_effects=True),
        name="combine",
    )(part, dp, tp)


def halo(cells):
    count = lax.axis_size("exp")
    head, tail = cells[:1], cells[-1:]
    return jnp.concatenate(
        [
            lax.ppermute(tail, "exp", [(i, i + 1) for i in range(count - 1)]),
            cells,
            lax.ppermute(head, "exp", [(i + 1, i) for i in range(count - 1)]),
        ],
        axis=0,
    )


def gating(picked):
    chosen = jax.nn.sigmoid(picked)
    return chosen / jnp.sum(chosen, axis=-1, keepdims=True)


def local(latent, stem_weight, norm_gain, router_weight, routes, gate_weight, up_weight, down_weight, grad_mixed):
    rows_here, channels, width = latent.shape
    taps, model_width = stem_weight.shape
    experts = router_weight.shape[1]
    top = routes.shape[1]
    tok = rows_here * width
    rep = lax.axis_index("rep")
    expert_here = lax.axis_index("exp") // SH
    tile = (rep + 3 * expert_here) % 8
    hid = gate_weight.shape[1]
    extra = TAPS - taps

    dsl = model_width // REP
    s_here = lax.dynamic_slice_in_dim(stem_weight, rep * dsl, dsl, 1)
    gain_here = lax.dynamic_slice_in_dim(norm_gain, rep * dsl, dsl, 0)
    sg_hi, sg_lo = split(jnp.pad(s_here.astype(F32) * gain_here, ((0, extra), (0, 0))))
    w2 = jnp.concatenate([gate_weight, up_weight], axis=1)
    gp = (dot32(sg_hi, w2) + dot32(sg_lo, w2)).reshape(2, 4, TP, 2 * hid)

    padded = jnp.pad(halo(latent), ((0, 0), (0, 0), (1, 1)))
    pieces = jnp.stack([padded[i : i + rows_here, :, j : j + width] for i in range(3) for j in range(3)], axis=0)
    patches = jnp.transpose(pieces, (1, 3, 0, 2)).reshape(tok, taps)
    stem = dot32(patches, stem_weight).astype(BF)
    sv = stem.astype(F32)
    rstd = lax.rsqrt(jnp.mean(sv * sv, axis=-1, keepdims=True) + 1e-06)
    normed = (sv * rstd * norm_gain).astype(BF)
    logits = dot32(normed, router_weight)
    selector = (routes[:, :, None] == jnp.arange(experts, dtype=jnp.int32)).astype(F32)
    picked = jnp.sum(logits[:, None, :] * selector, axis=-1)
    gates = gating(picked)

    both = jnp.sum(selector, axis=1)
    earlier = (jnp.arange(tok)[:, None] > jnp.arange(tok)[None, :]).astype(BF)
    before = dot32(earlier, both.astype(BF))
    position = jnp.sum(selector * before[:, None, :], axis=-1).astype(jnp.int32)
    in_tile = position - ROWS * tile
    here = jnp.where((in_tile >= 0) & (in_tile < ROWS), routes * ROWS + in_tile, -1)
    here_ids = jnp.arange(experts * ROWS, dtype=jnp.int32)
    hot_here = [(here[:, k][:, None] == here_ids).astype(BF) for k in range(top)]
    full = (position // ROWS) * (experts * ROWS) + routes * ROWS + position % ROWS
    full_ids = jnp.arange(TILES * experts * ROWS, dtype=jnp.int32)
    hot = [(full[:, k][:, None] == full_ids).astype(BF) for k in range(top)]

    r_hi, r_lo = split(rstd)
    side = jnp.concatenate([jnp.pad(patches, ((0, 0), (0, extra))), r_hi, r_lo], axis=1)
    send_gm = dot32(hot_here[0] + hot_here[1], grad_mixed, ((0,), (0,))).astype(BF)
    send_side = dot32(hot_here[0] + hot_here[1], side, ((0,), (0,))).astype(BF)
    send_gate = sum(
        dot32(hot_here[k], jnp.concatenate(split(gates[:, k : k + 1]), axis=1), ((0,), (0,))) for k in range(top)
    ).astype(BF)
    send = jnp.concatenate([send_gm, send_side, send_gate, jnp.zeros((experts * ROWS, 60), BF)], axis=1)
    recv, g_full, w_full = dispatch(
        send.reshape(experts, ROWS, -1), gp, down_weight.T
    )
    flat = recv.reshape(-1, recv.shape[-1])
    gm = flat[:, :model_width]
    pr = flat[:, model_width : model_width + TAPS]
    more = flat[:, model_width + TAPS : model_width + TAPS + 4].astype(F32)
    rs = more[:, 0:1] + more[:, 1:2]
    gt = more[:, 2:3] + more[:, 3:4]
    g_hi, g_lo = split(g_full.reshape(TAPS, 2 * hid))
    down_t = w_full.reshape(model_width, hid)

    pre = rs * (dot32(pr, g_hi) + dot32(pr, g_lo))
    pg, pu = pre[:, :hid], pre[:, hid:]
    sigma = jax.nn.sigmoid(pg)
    hidden = pg * sigma * pu
    hg = (gt * hidden).astype(BF)
    out = dot32(hg, down_t, ((1,), (1,)))
    u = dot32(gm, down_t)
    gg = jnp.sum(hidden * u, axis=-1, keepdims=True)
    gu = (rs * gt) * u
    dpre = jnp.concatenate([gu * pu * sigma * (1.0 + pg * (1.0 - sigma)), gu * pg * sigma], axis=1).astype(BF)
    back = dot32(dpre, g_hi, ((1,), (1,))) + dot32(dpre, g_lo, ((1,), (1,)))
    t_part = dot32(pr, dpre, ((0,), (0,))).reshape(2, 4, TP, 2 * hid)
    d_part = dot32(gm, hg, ((0,), (0,))).astype(BF)
    d_part = d_part.reshape(4, 2, dsl, hid).transpose(1, 0, 2, 3)
    gg_hi, gg_lo = split(gg)
    part = jnp.concatenate(
        [out.astype(BF), back.astype(BF), gg_hi, gg_lo, jnp.zeros((out.shape[0], 62), BF)], axis=1
    ).reshape(recv.shape)
    slots_back, gd, t_full = combine(part, d_part, t_part)
    slots_back = slots_back.reshape(TILES * experts * ROWS, -1)

    t_hi, t_lo = split(t_full.reshape(TAPS, 2 * hid)[:taps])
    gw = (dot32(s_here, t_hi, ((0,), (0,))) + dot32(s_here, t_lo, ((0,), (0,)))) * gain_here[:, None]
    grad_gate, grad_up = gw[:, :hid], gw[:, hid:]
    grad_down = gd.T

    tok_sum = dot32(hot[0] + hot[1], slots_back)
    mixed = (sv + tok_sum[:, :model_width]).astype(BF)
    ggs = slots_back[:, model_width + TAPS : model_width + TAPS + 2]
    grad_gates = jnp.concatenate(
        [jnp.sum(dot32(hot[k], ggs), axis=-1, keepdims=True) for k in range(top)], axis=1
    )
    _, gate_pull = jax.vjp(gating, picked)
    grad_picked = gate_pull(grad_gates)[0]
    grad_logits = jnp.sum(selector * grad_picked[:, :, None], axis=1)
    sg_all = stem_weight.astype(F32) * norm_gain
    rproj = jnp.dot(sg_all, router_weight.astype(F32), precision=lax.Precision.HIGHEST)
    b = tok_sum[:, model_width : model_width + taps] + rstd * jnp.dot(
        grad_logits, rproj.T, precision=lax.Precision.HIGHEST
    )
    c = jnp.sum(patches.astype(F32) * b, axis=-1, keepdims=True) * (rstd * rstd / model_width)
    proj = dot32(grad_mixed, stem_weight, ((1,), (1,))) + b - c * dot32(stem, stem_weight, ((1,), (1,)))
    block = halo(proj.reshape(rows_here, width, taps)).reshape(rows_here + 2, width, 9, channels)
    shifted = jnp.pad(block, ((0, 0), (1, 1), (0, 0), (0, 0)))
    terms = [
        shifted[2 - i : 2 - i + rows_here, 2 - j : 2 - j + width, 3 * i + j, :] for i in range(3) for j in range(3)
    ]
    grad_latent = sum(terms).transpose(0, 2, 1)
    return (mixed, grad_latent, grad_gate, grad_up, grad_down)


def solution(mesh):
    return jax.shard_map(
        local,
        mesh=mesh,
        in_specs=(
            P("exp", None, None),
            P(),
            P(),
            P(),
            P("exp", None),
            P("rep", "exp"),
            P("rep", "exp"),
            P("exp", "rep"),
            P("exp", None),
        ),
        out_specs=(P("exp", None), P("exp", None, None), P("rep", "exp"), P("rep", "exp"), P("exp", "rep")),
        check_vma=False,
    )
```

time: 312 us -> 176 us (0.56)
  waiting for transfers between devices: 177 us -> 1.77 us
  Pallas kernels: 0 us -> 119 us
  blocking collectives: 58.8 us -> 0 us
  between operations: 16 us -> 1.3 us
  other arithmetic: 9.22 us -> 5.73 us
    pallas_call x0 -> x2, Pallas kernels: none -> 119 us  [the longest x1 64.5 us: combine(): pl.pallas_call(combine_kernel, out_shape=(jax.ShapeDtypeStruct((TILES, EX...]
    all_gather x3 -> x0, waiting for transfers between devices: 86.1 us -> none  [the longest x1 58.4 us: local(): lax.all_gather(stage, 'exp', axis=0, tiled=True, axis_index_groups=along)]
    reduce_scatter x2 -> x0, waiting for transfers between devices: 74 us -> none  [the longest x1 60.4 us: local(): lax.psum_scatter(ret, 'exp', scatter_dimension=0, axis_index_groups=along...]
    all_to_all x2 -> x0, blocking collectives: 58.8 us -> none  [the longest x1 33.3 us: local(): lax.all_to_all(send, 'exp', split_axis=0, concat_axis=0, tiled=True, axis...]
    psum x2 -> x0, waiting for transfers between devices: 13.2 us -> none  [the longest x1 13.2 us: local(): g_full = lax.psum(dot32(sg_hi, w2) + dot32(sg_lo, w2), 'rep')]
    all_gather x2 -> x0, local copies, waits for them, and re-layouts: 3.36 us -> none  [the longest x1 1.92 us: local(): lax.all_gather(stage, 'exp', axis=0, tiled=True, axis_index_groups=along)]
    dot_general x12 -> x13, matrix products: 9.71 us -> 8.52 us  [dot32(): return lax.dot_general(a, b, (dims, ((), ())), preferred_element_type=F32)]
    dot_general x10 -> x11, matrix products: 7.62 us -> 7.63 us  [dot32(): return jnp.dot(a, b, preferred_element_type=F32)]
  transfers between devices with their start and end apart: 11 -> 4, of which waited for: 8 -> 1; matrix products, arithmetic and copies ran while one was open for 7% -> 6% of each run, Pallas kernels for 0% -> 0%
where the time goes in v2:
time: 176 us; the launch traced here: 175 us
  Pallas kernels  119 us (68%)
  local copies, waits for them, and re-layouts  18.7 us (11%)
  matrix products  18.7 us (11%)
  starting transfers between devices  9.52 us (5%)
  other arithmetic  5.73 us (3%)
  waiting for transfers between devices  1.77 us (1%)
    pallas_call x1, Pallas kernels, combine(): pl.pallas_call(combine_kernel, out_shape=(jax.ShapeDtypeStruct((TILES, EX...  64.5 us
    pallas_call x1, Pallas kernels, dispatch(): pl.pallas_call(dispatch_kernel, out_shape=(jax.ShapeDtypeStruct((SH, TILE...  54.6 us
    dot_general x13, matrix products, dot32(): return lax.dot_general(a, b, (dims, ((), ())), preferred_element_type=F32)  8.52 us
    dot_general x11, matrix products, dot32(): return jnp.dot(a, b, preferred_element_type=F32)  7.63 us
    ppermute x2, starting transfers between devices, halo(): lax.ppermute(tail, 'exp', [(i, i + 1) for i in range(count - 1)])  6.93 us
    unnamed x75, local copies, waits for them, and re-layouts  4.49 us
  transfers between devices with their start and end apart: 4, of which 1 were waited for; matrix products, arithmetic and copies ran while one was open for 6% of the time, Pallas kernels for 0%

profile of v2, /device:TPU:1, one launch (start us, length us, event | category | flops | bytes accessed | tf_op | source)
XLA Modules:
  0.0 174.8 jit_solution(5805455338600350352)
XLA Ops:
  0.6 0.8 fusion.107
  1.4 4.3 %collective-permute-start = (bf16[1,16,64]{2,1,0:T(8,128)(2,1)S(1)}, bf16[1,16,64]{2,1,0:T(8,128)(2,1)S(1)}, u32[]{:S(2)}, u32[]{:S(2)}) collective-permute-start(bf16[1,16,64]{2,1,0:T(8,128)(2,1)S(1)} %get-tuple-element.53), channel_id=1, source_target_pairs={{0,8},{8,16},{16,24},{24,32},{32,40},{40,48},{48,56},{56,64},{64,7... | collective-permute-start | bytes 6152 | tf_op jit(solution)/shard_map/ppermute | solution.py:578
  5.8 1.3 collective-permute-start.1
  7.1 0.7 convert_reduce_fusion
  7.8 0.8 dynamic_slice.7
  8.5 2.2 %fusion.6 = f32[144,8]{0,1:T(8,128)} fusion(bf16[1536,8]{0,1:T(8,128)(2,1)} %param.12, bf16[144,1536]{1,0:T(8,128)(2,1)} %param.10, f32[1536]{0:T(1024)} %param.11), kind=kOutput, calls=%fused_computation.25 | convolution fusion | flops 21676032 | bytes 477696 | tf_op jit(solution)/shard_map/dot_general | solution.py:690
  10.7 1.0 convert_multiply_fusion.2
  11.7 0.9 constant_dynamic-update-slice_fusion.10
  12.6 0.9 constant_dynamic-update-slice_fusion.9
  13.9 1.1 convolution_add_fusion.2
  15.7 0.4 fusion.12
  16.5 0.6 fusion.105
  17.1 0.5 multiply_divide_fusion.1
  17.6 0.5 slice_bitcast_fusion.9
  18.7 0.3 convolution_convert_fusion.3
  19.3 0.8 concatenate.69
  20.1 54.6 %dispatch.1 = (bf16[8,5,8,1792]{3,2,1,0:T(8,128)(2,1)}, f32[8,24,768]{2,1,0:T(8,128)}, bf16[8,192,384]{2,1,0:T(8,128)(2,1)}) custom-call(bf16[8,8,1792]{2,1,0:T(8,128)(2,1)} %bitcast.130, f32[2,4,24,768]{3,2,1,0:T(8,128)} %bitcast.123, bf16[192,384]{1,0:T(8,128)(2,1)} %bitcast.138), custom_call_target="tpu_custom_call" | custom-call | tf_op jit(solution)/shard_map/dispatch/pallas_call | solution.py:517
  74.7 1.1 slice.198
  76.0 1.1 fusion.16
  77.8 0.9 copy-done.2
  78.7 0.9 multiply_convert_fusion.1
  79.6 1.1 fusion.28
  80.7 1.2 fusion.27
  81.9 0.7 convolution_convert_fusion.1
  82.6 0.5 copy-done.12
  83.2 1.0 convolution_convert_fusion
  84.2 1.0 copy.84
  85.2 0.9 copy.86
  86.2 1.0 copy.85
  87.1 2.3 %fusion.2 = bf16[320,192]{0,1:T(8,128)(2,1)} fusion(f32[320,192]{0,1:T(8,128)} %fusion.28, bf16[192,768]{1,0:T(8,128)(2,1)} %copy-done.3, bf16[320,384]{1,0:T(8,128)(2,1)} %copy-done.31, bf16[320,384]{1,0:T(8,128)(2,1)} %copy-done.30), kind=kOutput, calls=%fused_computation.14 | convolution fusion | flops 95477760 | bytes 1155072 | tf_op jit(solution)/shard_map/dot_general | solution.py:24
  89.5 1.0 copy.82
  90.5 1.2 copy.99
  91.7 2.7 %concatenate.74.part = bf16[8,5,8,1792]{3,2,1,0:T(8,128)(2,1)} concatenate(bf16[8,5,8,1536]{3,2,1,0:T(8,128)(2,1)S(1)} %bitcast.122, bf16[8,5,8,192]{3,2,1,0:T(8,128)(2,1)S(1)} %bitcast.131, bf16[8,5,8,1]{3,2,1,0:T(8,128)(2,1)} %copy.86, bf16[8,5,8,1]{3,2,1,0:T(8,128)(2,1)S(1)} %subtract_convert_fusion, bf16[8,5,8,62]{3,2,1,0:T(8,128)(2,1)S(1)} %broadcast_in_dim.10), dimensions={3} | concatenate | bytes 2293760 | tf_op jit(solution)/shard_map/concatenate | solution.py:669
  94.4 64.5 %combine.1 = (bf16[5,8,8,1792]{3,2,1,0:T(8,128)(2,1)}, f32[192,384]{1,0:T(8,128)}, f32[8,24,768]{2,1,0:T(8,128)}) custom-call(bf16[8,5,8,1792]{3,2,1,0:T(8,128)(2,1)} %concatenate.74.part, bf16[2,4,192,384]{3,2,1,0:T(8,128)(2,1)} %bitcast.121, f32[2,4,24,768]{3,2,1,0:T(8,128)} %bitcast.132), custom_call_target="tpu_custom_call" | custom-call | tf_op jit(solution)/shard_map/combine/pallas_call | solution.py:545
  158.9 1.2 convolution_reduce_fusion
  160.1 1.2 convolution_reduce_fusion.1
  161.2 1.7 fusion.35
  163.0 0.8 fusion.15
  164.1 0.3 multiply_reduce_fusion.1
  165.1 2.6 %collective-permute-start.2 = (f32[1,64,144]{1,2,0:T(8,128)S(1)}, f32[1,64,144]{1,2,0:T(8,128)S(1)}, u32[]{:S(2)}, u32[]{:S(2)}) collective-permute-start(f32[1,64,144]{1,2,0:T(8,128)S(1)} %get-tuple-element.51), channel_id=1, source_target_pairs={{0,8},{8,16},{16,24},{24,32},{32,40},{40,48},{48,56},{56,64},{64,7... | collective-permute-start | bytes 110600 | tf_op jit(solution)/shard_map/ppermute | solution.py:578
  167.7 1.3 collective-permute-start.3
  169.1 0.3 fusion.51
  169.7 0.3 fusion.1
  170.0 0.9 fusion.106
  171.0 1.8 %collective-permute-done.3 = f32[1,64,144]{1,2,0:T(8,128)S(1)} collective-permute-done((f32[1,64,144]{1,2,0:T(8,128)S(1)}, f32[1,64,144]{1,2,0:T(8,128)S(1)}, u32[]{:S(2)}, u32[]{:S(2)}) %collective-permute-start.3) | collective-permute-done | bytes 36896 | tf_op jit(solution)/shard_map/ppermute | solution.py:580
  172.8 0.5 select_maximum_fusion
  173.4 0.6 copy.93
  174.1 0.7 copy.110
  (115 shorter events, 4.5 us)
Async XLA Ops:
  0.6 18.1 %copy-start = (bf16[128,1536]{1,0:T(8,128)(2,1)S(1)}, bf16[128,1536]{1,0:T(8,128)(2,1)}, u32[]{:S(2)}) copy-start(bf16[128,1536]{1,0:T(8,128)(2,1)} %param.17) | copy-start | bytes 1179652
  1.4 13.7 %collective-permute-start = (bf16[1,16,64]{2,1,0:T(8,128)(2,1)S(1)}, bf16[1,16,64]{2,1,0:T(8,128)(2,1)S(1)}, u32[]{:S(2)}, u32[]{:S(2)}) collective-permute-start(bf16[1,16,64]{2,1,0:T(8,128)(2,1)S(1)} %get-tuple-element.53), channel_id=1, source_target_pairs={{0,8},{8,16},{16,24},{24,32},{32,40},{40,48},{48,56},{56,64},{64,7... | collective-permute-start | bytes 6152 | tf_op jit(solution)/shard_map/ppermute | solution.py:578
  5.8 9.3 %collective-permute-start.1 = (bf16[1,16,64]{2,1,0:T(8,128)(2,1)S(1)}, bf16[1,16,64]{2,1,0:T(8,128)(2,1)S(1)}, u32[]{:S(2)}, u32[]{:S(2)}) collective-permute-start(bf16[1,16,64]{2,1,0:T(8,128)(2,1)S(1)} %get-tuple-element.54), channel_id=1, source_target_pairs={{8,0},{16,8},{24,16},{32,24},{40,32},{48,40},{56,48},{64,56},{72,6... | collective-permute-start | bytes 6152 | tf_op jit(solution)/shard_map/ppermute | solution.py:580
  8.5 5.1 %copy-start.18 = (f32[192]{0:T(256)}, f32[192]{0:T(256)S(1)}, u32[]{:S(2)}) copy-start(f32[192]{0:T(256)S(1)} %dynamic_slice.7) | copy-start | bytes 2308
  13.6 1.5 copy-start.10
  13.8 1.8 %copy-start.1 = (bf16[144,1536]{1,0:T(8,128)(2,1)S(1)}, bf16[144,1536]{1,0:T(8,128)(2,1)}, u32[]{:S(2)}) copy-start(bf16[144,1536]{1,0:T(8,128)(2,1)} %param.10) | copy-start | bytes 1327108
  13.9 2.3 %copy-start.14 = (bf16[1536,8]{0,1:T(8,128)(2,1)S(1)}, bf16[1536,8]{0,1:T(8,128)(2,1)}, u32[]{:S(2)}) copy-start(bf16[1536,8]{0,1:T(8,128)(2,1)} %param.12) | copy-start | bytes 73732
  13.9 2.3 %copy-start.17 = (f32[1536]{0:T(1024)S(1)}, f32[1536]{0:T(1024)}, u32[]{:S(2)}) copy-start(f32[1536]{0:T(1024)} %param.11) | copy-start | bytes 18436
  15.0 1.5 copy-start.15
  15.7 3.4 %copy-start.6 = (bf16[128,144]{0,1:T(8,128)(2,1)}, bf16[128,144]{0,1:T(8,128)(2,1)S(1)}, u32[]{:S(2)}) copy-start(bf16[128,144]{0,1:T(8,128)(2,1)S(1)} %reshape.215) | copy-start | bytes 110596
  16.1 2.3 %copy-start.25 = (f32[128]{0:T(128)}, f32[128]{0:T(128)S(1)}, u32[]{:S(2)}) copy-start(f32[128]{0:T(128)S(1)} %get-tuple-element.67) | copy-start | bytes 1540
  16.1 2.3 %copy-start.27 = (f32[128]{0:T(128)}, f32[128]{0:T(128)S(1)}, u32[]{:S(2)}) copy-start(f32[128]{0:T(128)S(1)} %get-tuple-element.66) | copy-start | bytes 1540
  17.1 1.5 copy-start.21
  74.7 2.4 %copy-start.11 = (bf16[8,5,8,1792]{3,2,1,0:T(8,128)(2,1)S(1)}, bf16[8,5,8,1792]{3,2,1,0:T(8,128)(2,1)}, u32[]{:S(2)}) copy-start(bf16[8,5,8,1792]{3,2,1,0:T(8,128)(2,1)} %get-tuple-element.11) | copy-start | bytes 3440644
  77.1 0.7 copy-start.3
  77.4 1.3 copy-start.2
  79.6 2.3 %copy-start.30 = (bf16[320,384]{1,0:T(8,128)(2,1)}, bf16[320,384]{1,0:T(8,128)(2,1)S(1)}, u32[]{:S(2)}) copy-start(bf16[320,384]{1,0:T(8,128)(2,1)S(1)} %get-tuple-element.45) | copy-start | bytes 737284
  79.6 2.3 %copy-start.31 = (bf16[320,384]{1,0:T(8,128)(2,1)}, bf16[320,384]{1,0:T(8,128)(2,1)S(1)}, u32[]{:S(2)}) copy-start(bf16[320,384]{1,0:T(8,128)(2,1)S(1)} %get-tuple-element.46) | copy-start | bytes 737284
  81.9 1.3 copy-start.12
  90.5 1.2 copy-start.4
  90.5 1.2 copy-start.5
  94.4 64.5 %copy-start.23 = (s32[128]{0:T(128)S(1)}, s32[128]{0:T(128)}, u32[]{:S(2)}) copy-start(s32[128]{0:T(128)} %get-tuple-element.71) | copy-start | bytes 1540
  94.4 65.7 %copy-start.24 = (s32[128]{0:T(128)S(1)}, s32[128]{0:T(128)}, u32[]{:S(2)}) copy-start(s32[128]{0:T(128)} %get-tuple-element.72) | copy-start | bytes 1540
  162.9 0.9 copy-start.20
  162.9 0.9 copy-start.29
  162.9 0.9 copy-start.22
  163.0 1.0 copy-start.16
  163.0 1.1 copy-start.7
  163.0 1.1 copy-start.13
  163.0 1.1 copy-start.28
  163.0 1.4 copy-start.26
  164.4 4.6 %copy-start.8 = (f32[8,24,768]{2,1,0:T(8,128)S(1)}, f32[8,24,768]{2,1,0:T(8,128)}, u32[]{:S(2)}) copy-start(f32[8,24,768]{2,1,0:T(8,128)} %get-tuple-element.15) | copy-start | bytes 1769476
  165.1 5.9 %collective-permute-start.2 = (f32[1,64,144]{1,2,0:T(8,128)S(1)}, f32[1,64,144]{1,2,0:T(8,128)S(1)}, u32[]{:S(2)}, u32[]{:S(2)}) collective-permute-start(f32[1,64,144]{1,2,0:T(8,128)S(1)} %get-tuple-element.51), channel_id=1, source_target_pairs={{0,8},{8,16},{16,24},{24,32},{32,40},{40,48},{48,56},{56,64},{64,7... | collective-permute-start | bytes 110600 | tf_op jit(solution)/shard_map/ppermute | solution.py:578
  167.7 5.1 %collective-permute-start.3 = (f32[1,64,144]{1,2,0:T(8,128)S(1)}, f32[1,64,144]{1,2,0:T(8,128)S(1)}, u32[]{:S(2)}, u32[]{:S(2)}) collective-permute-start(f32[1,64,144]{1,2,0:T(8,128)S(1)} %get-tuple-element.52), channel_id=1, source_target_pairs={{8,0},{16,8},{24,16},{32,24},{40,32},{48,40},{56,48},{64,56},{72,6... | collective-permute-start | bytes 110600 | tf_op jit(solution)/shard_map/ppermute | solution.py:580
  169.0 0.7 copy-start.19
  170.0 4.0 %copy-start.9 = (f32[192,384]{1,0:T(8,128)S(1)}, f32[192,384]{1,0:T(8,128)}, u32[]{:S(2)}) copy-start(f32[192,384]{1,0:T(8,128)} %get-tuple-element.16) | copy-start | bytes 884740

commit v3 on v1

v3 whole, which is shorter than its diff:
```python
import jax
import jax.numpy as jnp
from jax import lax
from jax.experimental import pallas as pl
from jax.experimental.pallas import tpu as pltpu
from jax.sharding import PartitionSpec as P

F32 = jnp.float32
BF = jnp.bfloat16
I32 = jnp.int32
EXP = 8
SH = 8
REP = 8
TILES = 5
ROWS = 8
PIECE = TILES * ROWS
CHUNKS = ((0, 2), (2, 2), (4, 1))
TAPS = 192
TP = TAPS // REP
SIDE = 256
MESH = pl.DeviceIdType.MESH
VM = pl.BlockSpec(memory_space=pltpu.VMEM)


def dot32(a, b, dims=None):
    if dims is None:
        return jnp.dot(a, b, preferred_element_type=F32)
    return lax.dot_general(a, b, (dims, ((), ())), preferred_element_type=F32)


NT = ((1,), (1,))
TN = ((0,), (0,))


def split(v):
    hi = v.astype(BF)
    return hi, (v - hi.astype(F32)).astype(BF)


def iota(shape, dim):
    return lax.broadcasted_iota(I32, shape, dim)


def rcopy(src, dst, ssem, rsem, exp, rep):
    return pltpu.make_async_remote_copy(
        src_ref=src, dst_ref=dst, send_sem=ssem, recv_sem=rsem, device_id={"exp": exp, "rep": rep}, device_id_type=MESH
    )


class Place:
    def __init__(self):
        self.exp = lax.axis_index("exp")
        self.rep = lax.axis_index("rep")
        self.e = self.exp // SH
        self.m = self.exp % SH
        self.y = self.rep // 2
        self.c = self.rep % 2
        self.tile = self.tile_of(self.rep)
        self.d = 1 - 2 * self.c
        self.fwd = self.rep_at(self.d)
        self.bwd = self.rep_at(-self.d)
        self.partner = self.y * 2 + 1 - self.c

    def rep_at(self, dy):
        return ((self.y + dy + 4) % 4) * 2 + self.c

    def tile_of(self, rep):
        return (rep + 3 * self.e) % 8

    def peers(self):
        return [((self.e + k) % EXP) * SH + self.m for k in range(1, EXP)]

    def enter(self):
        bar = pltpu.get_barrier_semaphore()

        def greet(exp, rep):
            pl.semaphore_signal(bar, inc=1, device_id={"exp": exp, "rep": rep}, device_id_type=MESH)

        for peer in self.peers():
            greet(peer, self.rep)
        for rep in (self.fwd, self.bwd, self.partner):
            greet(self.exp, rep)

        @pl.when(self.exp > 0)
        def _():
            greet(self.exp - 1, self.rep)

        @pl.when(self.exp < EXP * SH - 1)
        def _():
            greet(self.exp + 1, self.rep)

        pl.semaphore_wait(bar, 10 + (self.exp > 0).astype(jnp.int32) + (self.exp < EXP * SH - 1).astype(jnp.int32))


class Gather:
    def __init__(self, pc, src, piece, ssem, rsem, valid=None):
        self.pc, self.src, self.piece, self.ssem, self.rsem = pc, src, piece, ssem, rsem
        self.valid = valid

    def guard(self, rep, fn):
        if self.valid is None:
            fn()
        else:
            pl.when(self.valid(rep))(fn)

    def copy(self, src, rep_of, k, target):
        return rcopy(src, self.piece(rep_of), self.ssem.at[k], self.rsem.at[rep_of], self.pc.exp, target)

    def moves(self):
        pc = self.pc
        far = pc.rep_at(2)
        own, part = pc.rep, pc.partner
        return [
            (self.src, own, 0, pc.fwd),
            (self.src, own, 1, pc.bwd),
            (self.src, own, 2, part),
            (self.piece(pc.bwd), pc.bwd, 3, pc.fwd),
            (self.piece(pc.bwd), pc.bwd, 4, part),
            (self.piece(pc.fwd), pc.fwd, 5, part),
            (self.piece(far), far, 6, part),
        ]

    def start(self):
        def go():
            for mv in self.moves()[:3]:
                self.copy(*mv).start()

        self.guard(self.pc.rep, go)

    def arrive(self, rep):
        self.copy(self.piece(rep), rep, 0, self.pc.partner).wait_recv()

    def relay(self):
        mv = self.moves()

        def near():
            self.arrive(self.pc.bwd)
            self.copy(*mv[3]).start()
            self.copy(*mv[4]).start()

        self.guard(self.pc.bwd, near)

        def other():
            self.arrive(self.pc.fwd)
            self.copy(*mv[5]).start()

        self.guard(self.pc.fwd, other)

    def relay_far(self):
        far = self.pc.rep_at(2)

        def go():
            self.arrive(far)
            self.copy(*self.moves()[6]).start()

        self.guard(far, go)

    def finish(self):
        for dy in range(4):
            rep = ((self.pc.y + dy) % 4) * 2 + 1 - self.pc.c
            self.guard(rep, lambda rep=rep: self.arrive(rep))
        for mv in self.moves():
            self.guard(mv[1], lambda mv=mv: self.copy(*mv).wait_send())


class Scatter:
    def __init__(self, pc, src, got, total, side, ssem, rsem):
        self.pc, self.src, self.got, self.total, self.side, self.ssem, self.rsem = pc, src, got, total, side, ssem, rsem

    def copy(self, k):
        pc = self.pc
        y, d = pc.y, pc.d
        at = lambda dy: self.total.at[(y + dy + 4) % 4]
        src, dst, rep = (
            (self.src.at[1 - pc.c], self.got, pc.partner),
            (at(2), self.side.at[0], pc.fwd),
            (at(-d), self.side.at[1], pc.bwd),
            (at(d), self.side.at[2], pc.fwd),
        )[k]
        return rcopy(src, dst, self.ssem.at[k], self.rsem.at[k], pc.exp, rep)

    def start(self):
        self.copy(0).start()

    def add(self):
        self.copy(0).wait_recv()

        def body(k, _):
            self.total[k] = (self.src[self.pc.c, k].astype(F32) + self.got[k].astype(F32)).astype(self.total.dtype)
            return 0

        lax.fori_loop(0, 4, body, 0)
        self.copy(1).start()
        self.copy(2).start()

    def pass_on(self):
        pc = self.pc
        self.copy(1).wait_recv()
        at = (pc.y + pc.d + 4) % 4
        self.total[at] = (self.total[at].astype(F32) + self.side[0].astype(F32)).astype(self.total.dtype)
        self.copy(3).start()

    def result(self):
        self.copy(2).wait_recv()
        self.copy(3).wait_recv()
        return self.total[self.pc.y].astype(F32) + self.side[1].astype(F32) + self.side[2].astype(F32)

    def finish(self):
        for k in range(4):
            self.copy(k).wait_send()


def scatter_scratch(block, dtype):
    return [
        pltpu.VMEM((4,) + block, dtype),
        pltpu.VMEM((4,) + block, dtype),
        pltpu.VMEM((3,) + block, dtype),
        pltpu.SemaphoreType.DMA((4,)),
        pltpu.SemaphoreType.DMA((4,)),
    ]


def gather_scratch():
    return [pltpu.SemaphoreType.DMA((7,)), pltpu.SemaphoreType.DMA((REP,))]


def layer_kernel(
    latent, s_ref, gain_ref, wr_ref, routes_ref, routes_t_ref, wg_ref, wu_ref, wd_ref, gm_ref,
    mixed_ref, glat_ref, ggate_ref, gup_ref, gdown_ref,
    send, send_side, recv, recv_side, w_own, wfull, gp, gmine, gfull,
    h_prev, h_next, lat4, ptx, stem_ref, sg_hi, sg_lo,
    row32, gm_all, hg_ref, dpre_ref,
    part, acc_l, acc_r, sums, ret32, slots, dp, tp, tmine, tfull, a_out, a_prev, a_next,
    *sems
):
    (g_got, g_tot, g_side, g_ss, g_rs, d_got, d_tot, d_side, d_ss, d_rs, t_got, t_tot, t_side, t_ss, t_rs,
     ag_ss, ag_rs, wg_ss, wg_rs, tg_ss, tg_rs, sg_ss, sg_rs,
     st_ss, st_rs, sd_ss, sd_rs, ln_ss, ln_rs, sl_ss, sl_rs, ca_ss, cl_rs, cr_rs, ct_ss, ct_rs,
     ha_ss, ha_rs, hb_ss, hb_rs, loc) = sems
    pc = Place()
    m = pc.m
    tok, dm = gm_ref.shape
    hid = wg_ref.shape[1]
    taps = s_ref.shape[0]
    wide = tok // 2
    top = routes_ref.shape[1]
    has_rows = pc.tile < TILES

    upper = (iota((tok, tok), 0) < iota((tok, tok), 1)).astype(BF)
    lower = (iota((tok, tok), 0) > iota((tok, tok), 1)).astype(BF)
    r_row = [routes_t_ref[k : k + 1, :] for k in range(top)]
    r_col = [routes_ref[:, k : k + 1] for k in range(top)]
    sel_row = [(iota((EXP, tok), 0) == r).astype(F32) for r in r_row]
    sel_col = [(iota((tok, EXP), 1) == r).astype(F32) for r in r_col]
    before_row = dot32((sel_row[0] + sel_row[1]).astype(BF), upper)
    before_col = dot32(lower, (sel_col[0] + sel_col[1]).astype(BF))
    pos_row = [jnp.sum(s * before_row, axis=0, keepdims=True).astype(I32) for s in sel_row]
    pos_col = [jnp.sum(s * before_col, axis=1, keepdims=True).astype(I32) for s in sel_col]

    def here_id(pos, r):
        q = pos - ROWS * pc.tile
        return jnp.where((q >= 0) & (q < ROWS), r * ROWS + q, -1)

    def full_id(pos, r):
        t = lax.shift_right_logical(pos, 3)
        return t * (EXP * ROWS) + r * ROWS + (pos - t * ROWS)

    hot_here = [(iota((EXP * ROWS, tok), 0) == here_id(p, r)).astype(F32) for p, r in zip(pos_row, r_row)]
    hot_here_b = [h.astype(BF) for h in hot_here]
    picked_rows = dot32(hot_here_b[0] + hot_here_b[1], gm_ref[...])
    for e in range(EXP):
        send[e] = picked_rows[e * ROWS : (e + 1) * ROWS].astype(BF)
    eye = (iota((hid, hid), 0) == iota((hid, hid), 1)).astype(BF)
    w_own[...] = dot32(wd_ref[...], eye, TN).astype(BF)

    pc.enter()

    ha = (
        rcopy(latent.at[1], h_prev, ha_ss.at[0], ha_rs.at[0], pc.exp + 1, pc.rep),
        rcopy(latent.at[0], h_next, ha_ss.at[1], ha_rs.at[1], pc.exp - 1, pc.rep),
    )
    first_row, last_row = pc.exp == 0, pc.exp == EXP * SH - 1
    pl.when(jnp.logical_not(last_row))(lambda: ha[0].start())
    pl.when(jnp.logical_not(first_row))(lambda: ha[1].start())

    def stage(k, side):
        peer = (pc.e + k) % EXP
        src, dst, ss, rs = (send_side, recv_side, sd_ss, sd_rs) if side else (send, recv, st_ss, st_rs)
        return rcopy(src.at[peer], dst.at[m, pc.tile], ss.at[k], rs.at[pc.tile], peer * SH + m, pc.rep)

    keep_gm = pltpu.make_async_copy(send.at[pc.e], recv.at[m, pc.tile], loc.at[0])
    keep_side = pltpu.make_async_copy(send_side.at[pc.e], recv_side.at[m, pc.tile], loc.at[1])

    @pl.when(has_rows)
    def _():
        for k in (1, 7, 2, 6, 3, 5, 4):
            stage(k, False).start()
        keep_gm.start()

    gather_w = Gather(pc, w_own, lambda rep: wfull.at[rep], wg_ss, wg_rs)
    own_w = pltpu.make_async_copy(w_own, wfull.at[pc.rep], loc.at[2])
    gather_w.start()
    own_w.start()

    dsl = wg_ref.shape[0]
    sg = s_ref[...].astype(F32) * gain_ref[...]
    hi, lo = split(sg)
    pick = (iota((dm, dsl), 0) == iota((dm, dsl), 1) + pc.rep * dsl).astype(BF)
    s_hi = dot32(hi, pick).astype(BF)
    s_lo = dot32(lo, pick).astype(BF)
    sg_hi[...] = s_hi
    sg_lo[...] = s_lo
    zero_taps = jnp.zeros((TAPS - taps, 2 * hid), F32)
    share = jnp.concatenate(
        [dot32(s_hi, w[...]) + dot32(s_lo, w[...]) for w in (wg_ref, wu_ref)], axis=1
    )
    share = jnp.concatenate([share, zero_taps], axis=0)
    for k in range(REP):
        gp[k // 4, k % 4] = share[k * TP : (k + 1) * TP]
    rproj = dot32(hi, wr_ref[...], NT) + dot32(lo, wr_ref[...], NT)
    scatter_g = Scatter(pc, gp, g_got, g_tot, g_side, g_ss, g_rs)
    scatter_g.start()

    @pl.when(jnp.logical_not(first_row))
    def _():
        rcopy(latent.at[1], h_prev, ha_ss.at[0], ha_rs.at[0], pc.exp, pc.partner).wait_recv()
        lat4[0] = h_prev[...].astype(F32)

    @pl.when(first_row)
    def _():
        lat4[0] = jnp.zeros(lat4.shape[1:], F32)

    @pl.when(jnp.logical_not(last_row))
    def _():
        rcopy(latent.at[0], h_next, ha_ss.at[1], ha_rs.at[1], pc.exp, pc.partner).wait_recv()
        lat4[3] = h_next[...].astype(F32)

    @pl.when(last_row)
    def _():
        lat4[3] = jnp.zeros(lat4.shape[1:], F32)

    lat4[1] = latent[0].astype(F32)
    lat4[2] = latent[1].astype(F32)
    chan = lat4.shape[1]
    col = iota((chan, tok), 1)
    col = jnp.where(col >= wide, col - wide, col)

    def shifted(v, by):
        if by == 0:
            return v
        rolled = pltpu.roll(v, (-by) % tok, 1)
        return jnp.where(col == (0 if by < 0 else wide - 1), 0.0, rolled)

    for i in range(3):
        two = jnp.concatenate([lat4[i], lat4[i + 1]], axis=1)
        for j in range(3):
            ptx[pl.ds((3 * i + j) * chan, chan), :] = shifted(two, j - 1)
    ptx[pl.ds(taps, SIDE - taps), :] = jnp.zeros((SIDE - taps, tok), F32)
    pt = ptx[pl.ds(0, taps), :]
    stem = dot32(pt.astype(BF), s_ref[...], TN).astype(BF)
    stem_ref[...] = stem
    sv = stem.astype(F32)
    rstd = lax.rsqrt(jnp.mean(sv * sv, axis=-1, keepdims=True) + 1e-06)
    rstd_row = jnp.transpose(jnp.broadcast_to(rstd, (tok, tok)))[0:1, :]
    normed = (sv * rstd * gain_ref[...]).astype(BF)
    logits = dot32(wr_ref[...], normed, NT)
    picked = [jnp.sum(s * logits, axis=0, keepdims=True) for s in sel_row]
    chosen = [jax.nn.sigmoid(p) for p in picked]
    total = chosen[0] + chosen[1]
    gates = [c / total for c in chosen]
    r_hi, r_lo = split(rstd_row)
    ptx[pl.ds(TAPS, 1), :] = r_hi.astype(F32)
    ptx[pl.ds(TAPS + 1, 1), :] = r_lo.astype(F32)
    side = jnp.zeros((EXP * ROWS, SIDE), F32)
    for k in range(top):
        k_hi, k_lo = split(gates[k])
        ptx[pl.ds(TAPS + 2, 1), :] = k_hi.astype(F32)
        ptx[pl.ds(TAPS + 3, 1), :] = k_lo.astype(F32)
        side = side + dot32(hot_here_b[k], ptx[...].astype(BF), NT)
    for e in range(EXP):
        send_side[e] = side[e * ROWS : (e + 1) * ROWS].astype(BF)

    @pl.when(has_rows)
    def _():
        for k in (1, 7, 2, 6, 3, 5, 4):
            stage(k, True).start()
        keep_side.start()

    ends = (m < SH - 1, m > 0)

    def hop(way, p, c, s):
        at = pl.ds(CHUNKS[c][0], CHUNKS[c][1])
        ref = recv.at[p, at]
        return rcopy(ref, ref, ln_ss.at[way, s, c], ln_rs.at[p, c], pc.exp + 1 - 2 * way, pc.rep)

    def hop_side(way, p, s):
        ref = recv_side.at[p]
        return rcopy(ref, ref, sl_ss.at[way, s], sl_rs.at[p], pc.exp + 1 - 2 * way, pc.rep)

    def arrived(i, side):
        source = (5 * (pc.rep - i + 8)) % 8
        ref, ss, rs = (recv_side, sd_ss, sd_rs) if side else (recv, st_ss, st_rs)

        @pl.when(source != pc.e)
        def _():
            rcopy(ref.at[m, i], ref.at[m, i], ss.at[0], rs.at[i], pc.exp, pc.partner).wait_recv()

    def step(s, _):
        for c in range(len(CHUNKS)):
            for way, p in ((0, m - s), (1, m + s)):
                ok = (p >= 0) if way == 0 else (p < SH)

                @pl.when(ok)
                def _():
                    hop(way, p, c, s).wait_recv()

                    @pl.when(ends[way])
                    def _():
                        hop(way, p, c, s).start()

        return 0

    def step_side(s, _):
        for way, p in ((0, m - s), (1, m + s)):
            ok = (p >= 0) if way == 0 else (p < SH)

            @pl.when(ok)
            def _():
                hop_side(way, p, s).wait_recv()

                @pl.when(ends[way])
                def _():
                    hop_side(way, p, s).start()

        return 0

    scatter_g.add()

    @pl.when(has_rows)
    def _():
        keep_gm.wait()

    for c, (at, count) in enumerate(CHUNKS):
        for i in range(at, at + count):
            arrived(i, False)
        for way in range(2):
            pl.when(ends[way])(lambda way=way, c=c: hop(way, m, c, 0).start())
    scatter_g.pass_on()
    gather_w.relay()
    lax.fori_loop(1, 2, step, 0)
    gmine[...] = scatter_g.result()
    spot = lambda ref: lambda rep: ref.at[(rep % 2) * 4 + rep // 2]
    gather_g = Gather(pc, gmine, spot(gfull), ag_ss, ag_rs)
    own_g = pltpu.make_async_copy(gmine, spot(gfull)(pc.rep), loc.at[3])
    gather_g.start()
    own_g.start()

    @pl.when(has_rows)
    def _():
        keep_side.wait()

    for i in range(TILES):
        arrived(i, True)
    for way in range(2):
        pl.when(ends[way])(lambda way=way: hop_side(way, m, 0).start())
    gather_w.relay_far()
    lax.fori_loop(2, 3, step, 0)
    gather_g.relay()
    lax.fori_loop(1, 3, step_side, 0)
    lax.fori_loop(3, 4, step, 0)
    gather_g.relay_far()
    lax.fori_loop(3, 5, step_side, 0)
    lax.fori_loop(4, 5, step, 0)
    lax.fori_loop(5, 7, step_side, 0)
    lax.fori_loop(5, 6, step, 0)
    lax.fori_loop(7, 8, step_side, 0)
    lax.fori_loop(6, 7, step, 0)
    gather_g.finish()
    gather_w.finish()
    scatter_g.finish()
    own_w.wait()
    own_g.wait()

    def widen(ref, n):
        def body(k, _):
            for i in range(TILES):
                row32[pl.ds(k * PIECE + i * ROWS, ROWS), pl.ds(0, n)] = ref[k, i].astype(F32)
            return 0

        lax.fori_loop(0, SH, body, 0)

    widen(recv_side, SIDE)
    more = row32[:, pl.ds(0, SIDE)]
    pr = more[:, :TAPS].astype(BF)
    rs = more[:, TAPS : TAPS + 1] + more[:, TAPS + 1 : TAPS + 2]
    gt = more[:, TAPS + 2 : TAPS + 3] + more[:, TAPS + 3 : TAPS + 4]
    g_hi, g_lo = split(gfull[...].reshape(TAPS, 2 * hid))
    pre = rs * (dot32(pr, g_hi) + dot32(pr, g_lo))
    pg, pu = pre[:, :hid], pre[:, hid:]
    sigma = jax.nn.sigmoid(pg)
    silu = pg * sigma
    hidden = silu * pu
    slope = pu * sigma * (1.0 + pg * (1.0 - sigma))
    hg = (gt * hidden).astype(BF)
    down_t = wfull[...].reshape(dm, hid)
    ret32[:, pl.ds(0, dm)] = dot32(hg, down_t, NT)
    lax.fori_loop(7, 8, step, 0)
    widen(recv, dm)
    gm_all[...] = row32[...].astype(BF)
    u = dot32(gm_all[...], down_t)
    gg = jnp.sum(hidden * u, axis=-1, keepdims=True)
    gu = (rs * gt) * u
    dpre = jnp.concatenate([gu * slope, gu * silu], axis=1).astype(BF)
    dpre_ref[...] = dpre
    hg_ref[...] = hg
    back = dot32(dpre, g_hi, NT) + dot32(dpre, g_lo, NT)
    gg_hi = gg.astype(BF).astype(F32)
    lane = iota((SH * PIECE, SIDE - TAPS), 1)
    tail = jnp.where(lane == 0, gg_hi, jnp.where(lane == 1, gg - gg_hi, 0.0))
    ret32[:, pl.ds(dm, SIDE)] = jnp.concatenate([back, tail], axis=1)

    def narrow(k, _):
        for i in range(TILES):
            part[k, i] = ret32[pl.ds(k * PIECE + i * ROWS, ROWS), :].astype(BF)
        return 0

    lax.fori_loop(0, SH, narrow, 0)

    def give(way, p, c):
        at = pl.ds(CHUNKS[c][0], CHUNKS[c][1])
        dst, rsem = ((acc_l, cl_rs), (acc_r, cr_rs))[way]
        return rcopy(
            part.at[p, at], dst.at[p, at], ca_ss.at[p, c], rsem.at[p, c], pc.exp + 1 - 2 * way, pc.rep
        )

    def step_sum(tau, _):
        for c, (at, count) in enumerate(CHUNKS):
            for way, p in ((0, 7 - tau + m), (1, tau - 7 + m)):
                ok = (tau >= m) if way == 0 else (p >= 0)
                acc = (acc_l, acc_r)[way]

                @pl.when(ok & ends[1 - way])
                def _():
                    give(way, p, c).wait_recv()
                    for i in range(at, at + count):
                        part[p, i] = (part[p, i].astype(F32) + acc[p, i].astype(F32)).astype(BF)

                pl.when(ok & ends[way])(lambda: give(way, p, c).start())

        return 0

    def steps(at, to):
        lax.fori_loop(at, to, step_sum, 0)

    steps(0, 1)
    t_share = dot32(pr, dpre_ref[...], TN)
    for k in range(REP):
        tp[k // 4, k % 4] = t_share[k * TP : (k + 1) * TP]
    scatter_t = Scatter(pc, tp, t_got, t_tot, t_side, t_ss, t_rs)
    scatter_t.start()
    d_share = dot32(hg_ref[...], gm_all[...], TN)
    for k in range(REP):
        dp[k % 2, k // 2] = d_share[:, k * dsl : (k + 1) * dsl].astype(BF)
    scatter_d = Scatter(pc, dp, d_got, d_tot, d_side, d_ss, d_rs)
    scatter_d.start()
    steps(1, 2)
    scatter_t.add()
    scatter_d.add()
    steps(2, 3)
    scatter_t.pass_on()
    scatter_d.pass_on()
    steps(3, 4)
    tmine[...] = scatter_t.result()
    gather_t = Gather(pc, tmine, spot(tfull), tg_ss, tg_rs)
    own_t = pltpu.make_async_copy(tmine, spot(tfull)(pc.rep), loc.at[4])
    gather_t.start()
    own_t.start()
    gdown_ref[...] = scatter_d.result()
    steps(4, 5)
    gather_t.relay()
    steps(5, 6)
    gather_t.relay_far()
    steps(6, 7)

    def home(i):
        source = (5 * (pc.rep - i + 8)) % 8
        return source, rcopy(
            sums.at[i], slots.at[i, pc.e], ct_ss.at[i], ct_rs.at[pc.e], source * SH + m, pc.rep
        )

    keep_out = lambda i: pltpu.make_async_copy(sums.at[i], slots.at[i, pc.e], loc.at[5])
    for c, (at, count) in enumerate(CHUNKS):
        for way in range(2):
            pl.when(ends[1 - way])(lambda way=way, c=c: give(way, m, c).wait_recv())
        for i in range(at, at + count):
            sums[i] = part[m, i]
            for way in range(2):

                @pl.when(ends[1 - way])
                def _():
                    acc = (acc_l, acc_r)[way]
                    sums[i] = (sums[i].astype(F32) + acc[m, i].astype(F32)).astype(BF)

            source, copy = home(i)
            pl.when(source != pc.e)(lambda copy=copy: copy.start())
            pl.when(source == pc.e)(lambda i=i: keep_out(i).start())

    gather_t.finish()
    own_t.wait()
    t_hi, t_lo = split(tfull[...].reshape(TAPS, 2 * hid)[:taps])
    gw = dot32(sg_hi[...], t_hi, TN) + dot32(sg_hi[...], t_lo, TN) + dot32(sg_lo[...], t_hi, TN)
    ggate_ref[...] = gw[:, :hid]
    gup_ref[...] = gw[:, hid:]
    proj0 = dot32(s_ref[...], gm_ref[...], NT)
    proj1 = dot32(s_ref[...], stem_ref[...], NT)

    @pl.when(has_rows)
    def _():
        keep_out(pc.tile).wait()
        for k in range(1, EXP):
            e = (pc.e + k) % EXP
            rcopy(
                slots.at[pc.tile, e], slots.at[pc.tile, e], ct_ss.at[0], ct_rs.at[e], pc.exp, pc.partner
            ).wait_recv()

    gather_s = Gather(
        pc,
        slots.at[pc.tile % TILES],
        lambda rep: slots.at[pc.tile_of(rep) % TILES],
        sg_ss,
        sg_rs,
        lambda rep: pc.tile_of(rep) < TILES,
    )
    gather_s.start()
    gather_s.relay()
    gather_s.relay_far()
    scatter_t.finish()
    scatter_d.finish()
    gather_s.finish()

    def collect(k, _):
        for i in range(EXP):
            ret32[pl.ds(k * EXP * ROWS + i * ROWS, ROWS), :] = slots[k, i].astype(F32)
        return 0

    lax.fori_loop(0, TILES, collect, 0)
    count = TILES * EXP * ROWS
    hot_row = [(iota((count, tok), 0) == full_id(p, r)).astype(F32) for p, r in zip(pos_row, r_row)]
    hot_col = sum((iota((tok, count), 1) == full_id(p, r)).astype(F32) for p, r in zip(pos_col, r_col)).astype(BF)
    tail = ret32[:, pl.ds(dm, SIDE)]
    gg_slot = tail[:, TAPS : TAPS + 1] + tail[:, TAPS + 1 : TAPS + 2]
    gg_row = [jnp.sum(h * gg_slot, axis=0, keepdims=True) for h in hot_row]
    b = dot32(tail.astype(BF), (hot_row[0] + hot_row[1]).astype(BF), TN)[:taps]
    mean = gg_row[0] * gates[0] + gg_row[1] * gates[1]
    grad_picked = [(g - mean) / total * (c * (1.0 - c)) for g, c in zip(gg_row, chosen)]
    grad_logits = sel_row[0] * grad_picked[0] + sel_row[1] * grad_picked[1]
    b = b + rstd_row * jnp.dot(rproj, grad_logits, precision=lax.Precision.HIGHEST, preferred_element_type=F32)
    c_row = jnp.sum(pt * b, axis=0, keepdims=True) * (rstd_row * rstd_row * (1.0 / dm))
    proj = proj0 + b - c_row * proj1
    rows3 = []
    for i in range(3):
        rows3.append(
            sum(shifted(proj[(3 * i + j) * chan : (3 * i + j + 1) * chan], 1 - j) for j in range(3))
        )
    a_out[0] = rows3[0][:, :wide]
    a_out[1] = rows3[2][:, wide:]
    hb = (
        rcopy(a_out.at[0], a_next, hb_ss.at[0], hb_rs.at[0], pc.exp - 1, pc.rep),
        rcopy(a_out.at[1], a_prev, hb_ss.at[1], hb_rs.at[1], pc.exp + 1, pc.rep),
    )
    pl.when(jnp.logical_not(first_row))(lambda: hb[0].start())
    pl.when(jnp.logical_not(last_row))(lambda: hb[1].start())
    out = dot32(hot_col, ret32[:, pl.ds(0, dm)].astype(BF))
    mixed_ref[...] = (stem_ref[...].astype(F32) + out).astype(BF)
    glat_ref[0] = rows3[0][:, wide:] + rows3[1][:, :wide]
    glat_ref[1] = rows3[1][:, wide:] + rows3[2][:, :wide]

    @pl.when(jnp.logical_not(last_row))
    def _():
        rcopy(a_out.at[0], a_next, hb_ss.at[0], hb_rs.at[0], pc.exp, pc.partner).wait_recv()
        glat_ref[1] = glat_ref[1] + a_next[...]

    @pl.when(jnp.logical_not(first_row))
    def _():
        rcopy(a_out.at[1], a_prev, hb_ss.at[1], hb_rs.at[1], pc.exp, pc.partner).wait_recv()
        glat_ref[0] = glat_ref[0] + a_prev[...]

    for copy in (ha[1], hb[0]):
        pl.when(jnp.logical_not(first_row))(copy.wait_send)
    for copy in (ha[0], hb[1]):
        pl.when(jnp.logical_not(last_row))(copy.wait_send)

    @pl.when(has_rows)
    def _():
        for k in range(1, EXP):
            stage(k, False).wait_send()
            stage(k, True).wait_send()

    def drain(s, _):
        for way, p in ((0, m - s), (1, m + s)):

            @pl.when(((p >= 0) if way == 0 else (p < SH)) & ends[way])
            def _():
                hop_side(way, p, s).wait_send()
                for c in range(len(CHUNKS)):
                    hop(way, p, c, s).wait_send()

        for way, ok in ((0, s > m), (1, s < m)):

            @pl.when(ok & ends[way])
            def _():
                for c in range(len(CHUNKS)):
                    give(way, s, c).wait_send()

        return 0

    lax.fori_loop(0, SH, drain, 0)
    for i in range(TILES):
        source, copy = home(i)
        pl.when(source != pc.e)(lambda copy=copy: copy.wait_send())


def local(latent, stem_weight, norm_gain, router_weight, routes, gate_weight, up_weight, down_weight, grad_mixed):
    tok, dm = grad_mixed.shape
    dsl, hid = gate_weight.shape
    rows_here, chan, wide = latent.shape
    taps = stem_weight.shape[0]
    full = dm + SIDE
    dma = pltpu.SemaphoreType.DMA
    chunks = len(CHUNKS)
    v = pltpu.VMEM
    return pl.pallas_call(
        layer_kernel,
        out_shape=(
            jax.ShapeDtypeStruct((tok, dm), BF),
            jax.ShapeDtypeStruct((rows_here, chan, wide), F32),
            jax.ShapeDtypeStruct((dsl, hid), F32),
            jax.ShapeDtypeStruct((dsl, hid), F32),
            jax.ShapeDtypeStruct((hid, dsl), F32),
        ),
        in_specs=[VM] * 10,
        out_specs=(VM,) * 5,
        scratch_shapes=[
            v((EXP, ROWS, dm), BF),
            v((EXP, ROWS, SIDE), BF),
            v((SH, TILES, ROWS, dm), BF),
            v((SH, TILES, ROWS, SIDE), BF),
            v((dsl, hid), BF),
            v((REP, dsl, hid), BF),
            v((2, 4, TP, 2 * hid), F32),
            v((TP, 2 * hid), F32),
            v((REP, TP, 2 * hid), F32),
            v((chan, wide), BF),
            v((chan, wide), BF),
            v((4, chan, wide), F32),
            v((SIDE, tok), F32),
            v((tok, dm), BF),
            v((taps, dsl), BF),
            v((taps, dsl), BF),
            v((SH * PIECE, dm), F32),
            v((SH * PIECE, dm), BF),
            v((SH * PIECE, hid), BF),
            v((SH * PIECE, 2 * hid), BF),
            v((SH, TILES, ROWS, full), BF),
            v((SH, TILES, ROWS, full), BF),
            v((SH, TILES, ROWS, full), BF),
            v((TILES, ROWS, full), BF),
            v((SH * PIECE, full), F32),
            v((TILES, EXP, ROWS, full), BF),
            v((2, 4, hid, dsl), BF),
            v((2, 4, TP, 2 * hid), F32),
            v((TP, 2 * hid), F32),
            v((REP, TP, 2 * hid), F32),
            v((2, chan, wide), F32),
            v((chan, wide), F32),
            v((chan, wide), F32),
        ]
        + scatter_scratch((TP, 2 * hid), F32)
        + scatter_scratch((hid, dsl), BF)
        + scatter_scratch((TP, 2 * hid), F32)
        + gather_scratch() * 4
        + [
            dma((EXP,)),
            dma((TILES,)),
            dma((EXP,)),
            dma((TILES,)),
            dma((2, SH, chunks)),
            dma((SH, chunks)),
            dma((2, SH)),
            dma((SH,)),
            dma((SH, chunks)),
            dma((SH, chunks)),
            dma((SH, chunks)),
            dma((TILES,)),
            dma((EXP,)),
            dma((2,)),
            dma((2,)),
            dma((2,)),
            dma((2,)),
            dma((6,)),
        ],
        compiler_params=pltpu.CompilerParams(collective_id=0, has_side_effects=True),
        name="layer",
    )(
        latent, stem_weight, norm_gain.reshape(1, -1), router_weight.T, routes, routes.T,
        gate_weight, up_weight, down_weight, grad_mixed,
    )


def solution(mesh):
    return jax.shard_map(
        local,
        mesh=mesh,
        in_specs=(
            P("exp", None, None),
            P(),
            P(),
            P(),
            P("exp", None),
            P("rep", "exp"),
            P("rep", "exp"),
            P("exp", "rep"),
            P("exp", None),
        ),
        out_specs=(P("exp", None), P("exp", None, None), P("rep", "exp"), P("rep", "exp"), P("exp", "rep")),
        check_vma=False,
    )
```

time: 312 us -> 140 us (0.45)
  waiting for transfers between devices: 177 us -> 0 us
  Pallas kernels: 0 us -> 130 us
  blocking collectives: 58.8 us -> 0 us
  matrix products: 18.2 us -> 0 us
  between operations: 16 us -> 0.66 us
  local copies, waits for them, and re-layouts: 19.4 us -> 8.83 us
  starting transfers between devices: 10 us -> 0 us
  other arithmetic: 9.22 us -> 0 us
    pallas_call x0 -> x1, Pallas kernels: none -> 130 us  [local(): pl.pallas_call(layer_kernel, out_shape=(jax.ShapeDtypeStruct((tok, dm), B...]
    all_gather x3 -> x0, waiting for transfers between devices: 86.1 us -> none  [the longest x1 58.4 us: local(): lax.all_gather(stage, 'exp', axis=0, tiled=True, axis_index_groups=along)]
    reduce_scatter x2 -> x0, waiting for transfers between devices: 74 us -> none  [the longest x1 60.4 us: local(): lax.psum_scatter(ret, 'exp', scatter_dimension=0, axis_index_groups=along...]
    all_to_all x2 -> x0, blocking collectives: 58.8 us -> none  [the longest x1 33.3 us: local(): lax.all_to_all(send, 'exp', split_axis=0, concat_axis=0, tiled=True, axis...]
    dot_general x24 -> x0, matrix products: 18.2 us -> none  [the longest x12 9.71 us: dot32(): return lax.dot_general(a, b, (dims, ((), ())), preferred_element_type=F32)]
    psum x2 -> x0, waiting for transfers between devices: 13.2 us -> none  [the longest x1 13.2 us: local(): g_full = lax.psum(dot32(sg_hi, w2) + dot32(sg_lo, w2), 'rep')]
    ppermute x4 -> x0, starting transfers between devices: 9.75 us -> none  [the longest x2 7.16 us: halo(): lax.ppermute(tail, 'exp', [(i, i + 1) for i in range(count - 1)])]
    concatenate x7 -> x0, local copies, waits for them, and re-layouts: 5.12 us -> none  [the longest x3 4.75 us: local(): jnp.concatenate([out.astype(BF), back.astype(BF), gg_hi, gg_lo, jnp.zeros...]
  transfers between devices with their start and end apart: 11 -> 0, of which waited for: 8 -> 0; matrix products, arithmetic and copies ran while one was open for 7% -> 0% of each run, Pallas kernels for 0% -> 0%
where the time goes in v3:
time: 140 us
  Pallas kernels  130 us (93%)
  local copies, waits for them, and re-layouts  8.83 us (6%)
    pallas_call x1, Pallas kernels, local(): pl.pallas_call(layer_kernel, out_shape=(jax.ShapeDtypeStruct((tok, dm), B...  130 us
    unnamed x16, local copies, waits for them, and re-layouts  5.61 us

profile of v3, /device:TPU:1, one launch (start us, length us, event | category | flops | bytes accessed | tf_op | source)
XLA Modules:
  0.0 139.8 jit_solution(9229748968640976279)
XLA Ops:
  0.6 0.0 copy-start.4
  0.6 1.3 reshape.13.gain_ref
  1.9 0.0 copy-done.4
  1.9 0.7 copy.14.routes_ref
  2.7 1.7 %copy.15.wd_ref = bf16[384,192]{1,0:T(8,128)(2,1)} copy(bf16[384,192]{0,1:T(8,128)(2,1)} %param.16) | data formatting | bytes 294912 | tf_op args[7]
  4.4 130.3 %layer.1 = (bf16[128,1536]{1,0:T(8,128)(2,1)}, f32[2,16,64]{2,1,0:T(8,128)}, f32[192,384]{1,0:T(8,128)}, f32[192,384]{1,0:T(8,128)}, f32[384,192]{1,0:T(8,128)}) custom-call(bf16[2,16,64]{2,1,0:T(8,128)(2,1)} %latent.1, bf16[144,1536]{1,0:T(8,128)(2,1)} %s_ref.1, f32[1,1536]{1,0:T(1,128)} %reshape.13.gain_ref, bf16[8,1536]{1,0:T(8,128)(2,1)} %bitcast.2, ...), custom_call_target="tpu_custom_call" | custom-call | tf_op jit(solution)/shard_map/layer/pallas_call | solution.py:732
  134.7 0.0 copy-start
  134.7 1.9 %copy.16 = f32[384,192]{0,1:T(8,128)} copy(f32[384,192]{1,0:T(8,128)} %get-tuple-element.9) | data formatting | bytes 589824 | tf_op jit(solution)/shard_map/layer/pallas_call | solution.py:732
  136.6 0.0 copy-done
  136.6 0.0 copy-start.3
  136.6 0.0 copy-start.2
  136.6 0.7 copy.21
  137.4 0.0 copy-done.3
  137.4 0.6 copy.22
  138.0 0.0 copy-done.2
  138.0 0.0 copy-start.1
  138.0 0.7 copy.23
  138.7 0.4 copy-done.1
  139.1 0.7 copy.24
Async XLA Ops:
  0.6 1.3 copy-start.4
  134.7 1.9 %copy-start = (bf16[128,1536]{1,0:T(8,128)(2,1)S(1)}, bf16[128,1536]{1,0:T(8,128)(2,1)}, u32[]{:S(2)}) copy-start(bf16[128,1536]{1,0:T(8,128)(2,1)} %get-tuple-element.15) | copy-start | bytes 1179652
  136.6 0.8 copy-start.3
  136.6 1.4 copy-start.2
  138.0 1.1 copy-start.1

commit v4 on v3

--- a/solution.py
+++ b/solution.py
@@ -52,6 +52,8 @@
         self.exp = lax.axis_index("exp")
         self.rep = lax.axis_index("rep")
         self.e = self.exp // SH
+        self.half = self.e % 2
+        self.x = self.e // 2
         self.m = self.exp % SH
         self.y = self.rep // 2
         self.c = self.rep % 2
@@ -67,29 +69,23 @@
     def tile_of(self, rep):
         return (rep + 3 * self.e) % 8
 
-    def peers(self):
-        return [((self.e + k) % EXP) * SH + self.m for k in range(1, EXP)]
+    def greet(self):
+        bar = pltpu.get_barrier_semaphore()
+
+        def hello(exp, rep):
+            pl.semaphore_signal(bar, inc=1, device_id={"exp": exp, "rep": rep}, device_id_type=MESH)
+
+        for rep in (self.fwd, self.bwd, self.partner):
+            hello(self.exp, rep)
+
+        def body(n, _):
+            hello((self.exp + n) % (EXP * SH), self.rep)
+            return 0
+
+        lax.fori_loop(1, EXP * SH, body, 0)
 
     def enter(self):
-        bar = pltpu.get_barrier_semaphore()
-
-        def greet(exp, rep):
-            pl.semaphore_signal(bar, inc=1, device_id={"exp": exp, "rep": rep}, device_id_type=MESH)
-
-        for peer in self.peers():
-            greet(peer, self.rep)
-        for rep in (self.fwd, self.bwd, self.partner):
-            greet(self.exp, rep)
-
-        @pl.when(self.exp > 0)
-        def _():
-            greet(self.exp - 1, self.rep)
-
-        @pl.when(self.exp < EXP * SH - 1)
-        def _():
-            greet(self.exp + 1, self.rep)
-
-        pl.semaphore_wait(bar, 10 + (self.exp > 0).astype(jnp.int32) + (self.exp < EXP * SH - 1).astype(jnp.int32))
+        pl.semaphore_wait(pltpu.get_barrier_semaphore(), EXP * SH + 2)
 
 
 class Gather:
@@ -225,17 +221,17 @@
 
 
 def layer_kernel(
-    latent, s_ref, gain_ref, wr_ref, routes_ref, routes_t_ref, wg_ref, wu_ref, wd_ref, gm_ref,
+    latent, s_ref, gain_ref, wr_ref, routes_ref, wg_ref, wu_ref, wd_ref, gm_ref,
     mixed_ref, glat_ref, ggate_ref, gup_ref, gdown_ref,
-    send, send_side, recv, recv_side, w_own, wfull, gp, gmine, gfull,
+    send, send_side, recv, recv_side, wfull, gp, gmine, gfull,
     h_prev, h_next, lat4, ptx, stem_ref, sg_hi, sg_lo,
-    row32, gm_all, hg_ref, dpre_ref,
-    part, acc_l, acc_r, sums, ret32, slots, dp, tp, tmine, tfull, a_out, a_prev, a_next,
+    row32, side32, gm_all, hg_ref, dpre_ref,
+    part, acc_l, acc_r, sums, ret32, send_back, back_in, bsum, back_all, slots, dp, tp, tmine, tfull, a_out, a_prev, a_next,
     *sems
 ):
     (g_got, g_tot, g_side, g_ss, g_rs, d_got, d_tot, d_side, d_ss, d_rs, t_got, t_tot, t_side, t_ss, t_rs,
-     ag_ss, ag_rs, wg_ss, wg_rs, tg_ss, tg_rs, sg_ss, sg_rs,
-     st_ss, st_rs, sd_ss, sd_rs, ln_ss, ln_rs, sl_ss, sl_rs, ca_ss, cl_rs, cr_rs, ct_ss, ct_rs,
+     ag_ss, ag_rs, wg_ss, wg_rs, tg_ss, tg_rs, bg_ss, bg_rs, s0_ss, s0_rs, s1_ss, s1_rs,
+     st_ss, st_rs, sd_ss, sd_rs, ln_ss, ln_rs, ca_ss, cl_rs, cr_rs, ct_ss, ct_rs, bk_ss, bo_ss, bk_rs,
      ha_ss, ha_rs, hb_ss, hb_rs, loc) = sems
     pc = Place()
     m = pc.m
@@ -243,19 +239,16 @@
     hid = wg_ref.shape[1]
     taps = s_ref.shape[0]
     wide = tok // 2
-    top = routes_ref.shape[1]
+    top = routes_ref.shape[0]
     has_rows = pc.tile < TILES
 
+    pc.greet()
+
     upper = (iota((tok, tok), 0) < iota((tok, tok), 1)).astype(BF)
-    lower = (iota((tok, tok), 0) > iota((tok, tok), 1)).astype(BF)
-    r_row = [routes_t_ref[k : k + 1, :] for k in range(top)]
-    r_col = [routes_ref[:, k : k + 1] for k in range(top)]
+    r_row = [routes_ref[k : k + 1, :] for k in range(top)]
     sel_row = [(iota((EXP, tok), 0) == r).astype(F32) for r in r_row]
-    sel_col = [(iota((tok, EXP), 1) == r).astype(F32) for r in r_col]
     before_row = dot32((sel_row[0] + sel_row[1]).astype(BF), upper)
-    before_col = dot32(lower, (sel_col[0] + sel_col[1]).astype(BF))
     pos_row = [jnp.sum(s * before_row, axis=0, keepdims=True).astype(I32) for s in sel_row]
-    pos_col = [jnp.sum(s * before_col, axis=1, keepdims=True).astype(I32) for s in sel_col]
 
     def here_id(pos, r):
         q = pos - ROWS * pc.tile
@@ -263,15 +256,14 @@
 
     def full_id(pos, r):
         t = lax.shift_right_logical(pos, 3)
-        return t * (EXP * ROWS) + r * ROWS + (pos - t * ROWS)
+        place = (r & 1) * (EXP // 2) + lax.shift_right_logical(r, 1)
+        return t * (EXP * ROWS) + place * ROWS + (pos - t * ROWS)
 
     hot_here = [(iota((EXP * ROWS, tok), 0) == here_id(p, r)).astype(F32) for p, r in zip(pos_row, r_row)]
     hot_here_b = [h.astype(BF) for h in hot_here]
     picked_rows = dot32(hot_here_b[0] + hot_here_b[1], gm_ref[...])
     for e in range(EXP):
         send[e] = picked_rows[e * ROWS : (e + 1) * ROWS].astype(BF)
-    eye = (iota((hid, hid), 0) == iota((hid, hid), 1)).astype(BF)
-    w_own[...] = dot32(wd_ref[...], eye, TN).astype(BF)
 
     pc.enter()
 
@@ -283,27 +275,26 @@
     pl.when(jnp.logical_not(last_row))(lambda: ha[0].start())
     pl.when(jnp.logical_not(first_row))(lambda: ha[1].start())
 
-    def stage(k, side):
+    def stage(k):
         peer = (pc.e + k) % EXP
-        src, dst, ss, rs = (send_side, recv_side, sd_ss, sd_rs) if side else (send, recv, st_ss, st_rs)
-        return rcopy(src.at[peer], dst.at[m, pc.tile], ss.at[k], rs.at[pc.tile], peer * SH + m, pc.rep)
+        return rcopy(send.at[peer], recv.at[m, pc.tile], st_ss.at[k], st_rs.at[pc.tile], peer * SH + m, pc.rep)
 
     keep_gm = pltpu.make_async_copy(send.at[pc.e], recv.at[m, pc.tile], loc.at[0])
-    keep_side = pltpu.make_async_copy(send_side.at[pc.e], recv_side.at[m, pc.tile], loc.at[1])
 
     @pl.when(has_rows)
     def _():
         for k in (1, 7, 2, 6, 3, 5, 4):
-            stage(k, False).start()
+            stage(k).start()
         keep_gm.start()
 
-    gather_w = Gather(pc, w_own, lambda rep: wfull.at[rep], wg_ss, wg_rs)
-    own_w = pltpu.make_async_copy(w_own, wfull.at[pc.rep], loc.at[2])
+    gather_w = Gather(pc, wd_ref, lambda rep: wfull.at[rep], wg_ss, wg_rs)
+    own_w = pltpu.make_async_copy(wd_ref, wfull.at[pc.rep], loc.at[2])
     gather_w.start()
     own_w.start()
 
+    gain = gain_ref[...].reshape(1, dm)
     dsl = wg_ref.shape[0]
-    sg = s_ref[...].astype(F32) * gain_ref[...]
+    sg = s_ref[...].astype(F32) * gain
     hi, lo = split(sg)
     pick = (iota((dm, dsl), 0) == iota((dm, dsl), 1) + pc.rep * dsl).astype(BF)
     s_hi = dot32(hi, pick).astype(BF)
@@ -362,7 +353,7 @@
     sv = stem.astype(F32)
     rstd = lax.rsqrt(jnp.mean(sv * sv, axis=-1, keepdims=True) + 1e-06)
     rstd_row = jnp.transpose(jnp.broadcast_to(rstd, (tok, tok)))[0:1, :]
-    normed = (sv * rstd * gain_ref[...]).astype(BF)
+    normed = (sv * rstd * gain).astype(BF)
     logits = dot32(wr_ref[...], normed, NT)
     picked = [jnp.sum(s * logits, axis=0, keepdims=True) for s in sel_row]
     chosen = [jax.nn.sigmoid(p) for p in picked]
@@ -380,30 +371,37 @@
     for e in range(EXP):
         send_side[e] = side[e * ROWS : (e + 1) * ROWS].astype(BF)
 
+    def to_all(n):
+        dest = (pc.exp + n) % (EXP * SH)
+        e = dest // SH
+        return rcopy(send_side.at[e], recv_side.at[m, pc.tile], sd_ss.at[e], sd_rs.at[m], dest, pc.rep)
+
     @pl.when(has_rows)
     def _():
-        for k in (1, 7, 2, 6, 3, 5, 4):
-            stage(k, True).start()
-        keep_side.start()
+        def body(n, _):
+            to_all(n).start()
+            return 0
+
+        lax.fori_loop(1, EXP * SH, body, 0)
+        pltpu.make_async_copy(send_side.at[pc.e], recv_side.at[m, pc.tile], sd_rs.at[m]).start()
 
     ends = (m < SH - 1, m > 0)
 
     def hop(way, p, c, s):
         at = pl.ds(CHUNKS[c][0], CHUNKS[c][1])
         ref = recv.at[p, at]
-        return rcopy(ref, ref, ln_ss.at[way, s, c], ln_rs.at[p, c], pc.exp + 1 - 2 * way, pc.rep)
-
-    def hop_side(way, p, s):
-        ref = recv_side.at[p]
-        return rcopy(ref, ref, sl_ss.at[way, s], sl_rs.at[p], pc.exp + 1 - 2 * way, pc.rep)
-
-    def arrived(i, side):
+        return rcopy(ref, ref, ln_ss.at[way, s], ln_rs.at[p, c], pc.exp + 1 - 2 * way, pc.rep)
+
+    def arrived(i):
         source = (5 * (pc.rep - i + 8)) % 8
-        ref, ss, rs = (recv_side, sd_ss, sd_rs) if side else (recv, st_ss, st_rs)
 
         @pl.when(source != pc.e)
         def _():
-            rcopy(ref.at[m, i], ref.at[m, i], ss.at[0], rs.at[i], pc.exp, pc.partner).wait_recv()
+            rcopy(recv.at[m, i], recv.at[m, i], st_ss.at[0], st_rs.at[i], pc.exp, pc.partner).wait_recv()
+
+    def widen(p):
+        for i in range(TILES):
+            row32[pl.ds(pl.multiple_of(p * PIECE + i * ROWS, ROWS), ROWS), :] = recv[p, i].astype(F32)
 
     def step(s, _):
         for c in range(len(CHUNKS)):
@@ -418,20 +416,8 @@
                     def _():
                         hop(way, p, c, s).start()
 
-        return 0
-
-    def step_side(s, _):
         for way, p in ((0, m - s), (1, m + s)):
-            ok = (p >= 0) if way == 0 else (p < SH)
-
-            @pl.when(ok)
-            def _():
-                hop_side(way, p, s).wait_recv()
-
-                @pl.when(ends[way])
-                def _():
-                    hop_side(way, p, s).start()
-
+            pl.when((p >= 0) if way == 0 else (p < SH))(lambda p=p: widen(p))
         return 0
 
     scatter_g.add()
@@ -442,9 +428,10 @@
 
     for c, (at, count) in enumerate(CHUNKS):
         for i in range(at, at + count):
-            arrived(i, False)
+            arrived(i)
         for way in range(2):
             pl.when(ends[way])(lambda way=way, c=c: hop(way, m, c, 0).start())
+    widen(m)
     scatter_g.pass_on()
     gather_w.relay()
     lax.fori_loop(1, 2, step, 0)
@@ -454,43 +441,26 @@
     own_g = pltpu.make_async_copy(gmine, spot(gfull)(pc.rep), loc.at[3])
     gather_g.start()
     own_g.start()
-
-    @pl.when(has_rows)
-    def _():
-        keep_side.wait()
-
-    for i in range(TILES):
-        arrived(i, True)
-    for way in range(2):
-        pl.when(ends[way])(lambda way=way: hop_side(way, m, 0).start())
     gather_w.relay_far()
     lax.fori_loop(2, 3, step, 0)
     gather_g.relay()
-    lax.fori_loop(1, 3, step_side, 0)
     lax.fori_loop(3, 4, step, 0)
     gather_g.relay_far()
-    lax.fori_loop(3, 5, step_side, 0)
-    lax.fori_loop(4, 5, step, 0)
-    lax.fori_loop(5, 7, step_side, 0)
-    lax.fori_loop(5, 6, step, 0)
-    lax.fori_loop(7, 8, step_side, 0)
-    lax.fori_loop(6, 7, step, 0)
+    lax.fori_loop(4, 7, step, 0)
     gather_g.finish()
     gather_w.finish()
     scatter_g.finish()
     own_w.wait()
     own_g.wait()
 
-    def widen(ref, n):
-        def body(k, _):
-            for i in range(TILES):
-                row32[pl.ds(k * PIECE + i * ROWS, ROWS), pl.ds(0, n)] = ref[k, i].astype(F32)
-            return 0
-
-        lax.fori_loop(0, SH, body, 0)
-
-    widen(recv_side, SIDE)
-    more = row32[:, pl.ds(0, SIDE)]
+    def widen_side(p, _):
+        pltpu.make_async_copy(recv_side.at[p], recv_side.at[p], sd_rs.at[p]).wait()
+        for i in range(TILES):
+            side32[pl.ds(pl.multiple_of(p * PIECE + i * ROWS, ROWS), ROWS), :] = recv_side[p, i].astype(F32)
+        return 0
+
+    lax.fori_loop(0, SH, widen_side, 0)
+    more = side32[...]
     pr = more[:, :TAPS].astype(BF)
     rs = more[:, TAPS : TAPS + 1] + more[:, TAPS + 1 : TAPS + 2]
     gt = more[:, TAPS + 2 : TAPS + 3] + more[:, TAPS + 3 : TAPS + 4]
@@ -503,151 +473,183 @@
     slope = pu * sigma * (1.0 + pg * (1.0 - sigma))
     hg = (gt * hidden).astype(BF)
     down_t = wfull[...].reshape(dm, hid)
-    ret32[:, pl.ds(0, dm)] = dot32(hg, down_t, NT)
+    ret32[...] = dot32(hg, down_t, NT)
+    hg_ref[...] = hg
+
+    def give(way, p, c):
+        at = pl.ds(CHUNKS[c][0], CHUNKS[c][1])
+        dst, rsem = ((acc_l, cl_rs), (acc_r, cr_rs))[way]
+        return rcopy(
+            part.at[p, at], dst.at[p, at], ca_ss.at[p], rsem.at[p, c], pc.exp + 1 - 2 * way, pc.rep
+        )
+
+    def mine(p, i):
+        return ret32[pl.ds(pl.multiple_of(p * PIECE + i * ROWS, ROWS), ROWS), :]
+
+    def step_sum(tau, _):
+        for c, (at, count) in enumerate(CHUNKS):
+            for way, p in ((0, 7 - tau + m), (1, tau - 7 + m)):
+                ok = (tau >= m) if way == 0 else (p >= 0)
+                acc = (acc_l, acc_r)[way]
+
+                @pl.when(ok & ends[1 - way])
+                def _():
+                    give(way, p, c).wait_recv()
+                    for i in range(at, at + count):
+                        part[p, i] = (mine(p, i) + acc[p, i].astype(F32)).astype(BF)
+
+                @pl.when(ok & jnp.logical_not(ends[1 - way]))
+                def _():
+                    for i in range(at, at + count):
+                        part[p, i] = mine(p, i).astype(BF)
+
+                pl.when(ok & ends[way])(lambda: give(way, p, c).start())
+
+        return 0
+
+    def steps(at, to):
+        lax.fori_loop(at, to, step_sum, 0)
+
+    steps(0, 1)
     lax.fori_loop(7, 8, step, 0)
-    widen(recv, dm)
+
     gm_all[...] = row32[...].astype(BF)
     u = dot32(gm_all[...], down_t)
     gg = jnp.sum(hidden * u, axis=-1, keepdims=True)
     gu = (rs * gt) * u
     dpre = jnp.concatenate([gu * slope, gu * silu], axis=1).astype(BF)
     dpre_ref[...] = dpre
-    hg_ref[...] = hg
     back = dot32(dpre, g_hi, NT) + dot32(dpre, g_lo, NT)
     gg_hi = gg.astype(BF).astype(F32)
     lane = iota((SH * PIECE, SIDE - TAPS), 1)
     tail = jnp.where(lane == 0, gg_hi, jnp.where(lane == 1, gg - gg_hi, 0.0))
-    ret32[:, pl.ds(dm, SIDE)] = jnp.concatenate([back, tail], axis=1)
-
-    def narrow(k, _):
+    side32[...] = jnp.concatenate([back, tail], axis=1)
+    place = pc.half * (EXP // 2) + pc.x
+
+    def source_of(i):
+        return (5 * (pc.rep - i + 8)) % 8
+
+    def reply(p, i, sem):
+        return rcopy(send_back.at[p, i], back_in.at[m, place], sem, bk_rs.at[0], source_of(i) * SH + p, pc.rep)
+
+    def narrow(n, _):
+        p = (m + n) % SH
         for i in range(TILES):
-            part[k, i] = ret32[pl.ds(k * PIECE + i * ROWS, ROWS), :].astype(BF)
+            send_back[p, i] = side32[pl.ds(pl.multiple_of(p * PIECE + i * ROWS, ROWS), ROWS), :].astype(BF)
+        for i in range(TILES):
+            pl.when(p != m)(lambda i=i: reply(p, i, bk_ss.at[p]).start())
+
+            @pl.when((p == m) & (source_of(i) != pc.e))
+            def _():
+                reply(p, i, bo_ss.at[i]).start()
+
+            @pl.when((p == m) & (source_of(i) == pc.e))
+            def _():
+                pltpu.make_async_copy(send_back.at[p, i], back_in.at[m, place], bk_rs.at[0]).start()
+
         return 0
 
     lax.fori_loop(0, SH, narrow, 0)
-
-    def give(way, p, c):
-        at = pl.ds(CHUNKS[c][0], CHUNKS[c][1])
-        dst, rsem = ((acc_l, cl_rs), (acc_r, cr_rs))[way]
-        return rcopy(
-            part.at[p, at], dst.at[p, at], ca_ss.at[p, c], rsem.at[p, c], pc.exp + 1 - 2 * way, pc.rep
-        )
-
-    def step_sum(tau, _):
-        for c, (at, count) in enumerate(CHUNKS):
-            for way, p in ((0, 7 - tau + m), (1, tau - 7 + m)):
-                ok = (tau >= m) if way == 0 else (p >= 0)
-                acc = (acc_l, acc_r)[way]
-
-                @pl.when(ok & ends[1 - way])
-                def _():
-                    give(way, p, c).wait_recv()
-                    for i in range(at, at + count):
-                        part[p, i] = (part[p, i].astype(F32) + acc[p, i].astype(F32)).astype(BF)
-
-                pl.when(ok & ends[way])(lambda: give(way, p, c).start())
-
-        return 0
-
-    def steps(at, to):
-        lax.fori_loop(at, to, step_sum, 0)
-
-    steps(0, 1)
+    steps(1, 2)
     t_share = dot32(pr, dpre_ref[...], TN)
     for k in range(REP):
         tp[k // 4, k % 4] = t_share[k * TP : (k + 1) * TP]
     scatter_t = Scatter(pc, tp, t_got, t_tot, t_side, t_ss, t_rs)
     scatter_t.start()
-    d_share = dot32(hg_ref[...], gm_all[...], TN)
+    d_share = dot32(gm_all[...], hg_ref[...], TN)
     for k in range(REP):
-        dp[k % 2, k // 2] = d_share[:, k * dsl : (k + 1) * dsl].astype(BF)
+        dp[k % 2, k // 2] = d_share[k * dsl : (k + 1) * dsl].astype(BF)
     scatter_d = Scatter(pc, dp, d_got, d_tot, d_side, d_ss, d_rs)
     scatter_d.start()
-    steps(1, 2)
+    steps(2, 3)
     scatter_t.add()
     scatter_d.add()
-    steps(2, 3)
+    steps(3, 4)
     scatter_t.pass_on()
     scatter_d.pass_on()
-    steps(3, 4)
+    steps(4, 5)
     tmine[...] = scatter_t.result()
     gather_t = Gather(pc, tmine, spot(tfull), tg_ss, tg_rs)
     own_t = pltpu.make_async_copy(tmine, spot(tfull)(pc.rep), loc.at[4])
     gather_t.start()
     own_t.start()
+    with_rows = lambda rep: pc.tile_of(rep) < TILES
+    tile_at = lambda rep: pc.tile_of(rep) % TILES
+    gather_b = Gather(pc, bsum, lambda rep: back_all.at[tile_at(rep)], bg_ss, bg_rs, with_rows)
+    own_b = pltpu.make_async_copy(bsum, back_all.at[pc.tile % TILES], loc.at[1])
+
+    @pl.when(has_rows)
+    def _():
+        pltpu.make_async_copy(back_in, back_in, bk_rs.at[0]).wait()
+        for k in range(EXP):
+            bsum[k] = sum(back_in[j, k].astype(F32) for j in range(SH)).astype(BF)
+        own_b.start()
+
+    gather_b.start()
     gdown_ref[...] = scatter_d.result()
-    steps(4, 5)
+    steps(5, 6)
     gather_t.relay()
-    steps(5, 6)
-    gather_t.relay_far()
+    gather_b.relay()
     steps(6, 7)
 
     def home(i):
-        source = (5 * (pc.rep - i + 8)) % 8
+        source = source_of(i)
         return source, rcopy(
-            sums.at[i], slots.at[i, pc.e], ct_ss.at[i], ct_rs.at[pc.e], source * SH + m, pc.rep
+            sums.at[i], slots.at[i, pc.half, pc.x], ct_ss.at[i], ct_rs.at[pc.half], source * SH + m, pc.rep
         )
 
-    keep_out = lambda i: pltpu.make_async_copy(sums.at[i], slots.at[i, pc.e], loc.at[5])
+    keep_out = lambda i: pltpu.make_async_copy(sums.at[i], slots.at[i, pc.half, pc.x], ct_rs.at[pc.half])
     for c, (at, count) in enumerate(CHUNKS):
         for way in range(2):
             pl.when(ends[1 - way])(lambda way=way, c=c: give(way, m, c).wait_recv())
         for i in range(at, at + count):
-            sums[i] = part[m, i]
-            for way in range(2):
-
-                @pl.when(ends[1 - way])
-                def _():
-                    acc = (acc_l, acc_r)[way]
-                    sums[i] = (sums[i].astype(F32) + acc[m, i].astype(F32)).astype(BF)
+            @pl.when(m == 0)
+            def _():
+                sums[i] = (mine(m, i) + acc_r[m, i].astype(F32)).astype(BF)
+
+            @pl.when(m == SH - 1)
+            def _():
+                sums[i] = (mine(m, i) + acc_l[m, i].astype(F32)).astype(BF)
+
+            @pl.when(ends[0] & ends[1])
+            def _():
+                sums[i] = (mine(m, i) + acc_l[m, i].astype(F32) + acc_r[m, i].astype(F32)).astype(BF)
 
             source, copy = home(i)
             pl.when(source != pc.e)(lambda copy=copy: copy.start())
             pl.when(source == pc.e)(lambda i=i: keep_out(i).start())
 
+    def out_gather(h, ss, rs):
+        half = (pc.half + h) % 2
+        ready = slots.at[pc.tile % TILES, half]
+        gather = Gather(pc, ready, lambda rep: slots.at[tile_at(rep), half], ss, rs, with_rows)
+        wait = pltpu.make_async_copy(ready, ready, ct_rs.at[half])
+        return gather, wait
+
+    (near, near_wait), (away, away_wait) = out_gather(0, s0_ss, s0_rs), out_gather(1, s1_ss, s1_rs)
+    gather_t.relay_far()
+    gather_b.relay_far()
+    pl.when(has_rows)(near_wait.wait)
+    near.start()
     gather_t.finish()
     own_t.wait()
     t_hi, t_lo = split(tfull[...].reshape(TAPS, 2 * hid)[:taps])
     gw = dot32(sg_hi[...], t_hi, TN) + dot32(sg_hi[...], t_lo, TN) + dot32(sg_lo[...], t_hi, TN)
     ggate_ref[...] = gw[:, :hid]
     gup_ref[...] = gw[:, hid:]
-    proj0 = dot32(s_ref[...], gm_ref[...], NT)
-    proj1 = dot32(s_ref[...], stem_ref[...], NT)
-
-    @pl.when(has_rows)
-    def _():
-        keep_out(pc.tile).wait()
-        for k in range(1, EXP):
-            e = (pc.e + k) % EXP
-            rcopy(
-                slots.at[pc.tile, e], slots.at[pc.tile, e], ct_ss.at[0], ct_rs.at[e], pc.exp, pc.partner
-            ).wait_recv()
-
-    gather_s = Gather(
-        pc,
-        slots.at[pc.tile % TILES],
-        lambda rep: slots.at[pc.tile_of(rep) % TILES],
-        sg_ss,
-        sg_rs,
-        lambda rep: pc.tile_of(rep) < TILES,
-    )
-    gather_s.start()
-    gather_s.relay()
-    gather_s.relay_far()
-    scatter_t.finish()
-    scatter_d.finish()
-    gather_s.finish()
-
-    def collect(k, _):
-        for i in range(EXP):
-            ret32[pl.ds(k * EXP * ROWS + i * ROWS, ROWS), :] = slots[k, i].astype(F32)
-        return 0
-
-    lax.fori_loop(0, TILES, collect, 0)
+    pl.when(has_rows)(away_wait.wait)
+    away.start()
+    near.relay()
+    pl.when(has_rows)(own_b.wait)
+    gather_b.finish()
+
+    for t in range(TILES):
+        for k in range(EXP):
+            side32[pl.ds((t * EXP + k) * ROWS, ROWS), :] = back_all[t, k].astype(F32)
     count = TILES * EXP * ROWS
-    hot_row = [(iota((count, tok), 0) == full_id(p, r)).astype(F32) for p, r in zip(pos_row, r_row)]
-    hot_col = sum((iota((tok, count), 1) == full_id(p, r)).astype(F32) for p, r in zip(pos_col, r_col)).astype(BF)
-    tail = ret32[:, pl.ds(dm, SIDE)]
+    full_row = [full_id(p, r) for p, r in zip(pos_row, r_row)]
+    hot_row = [(iota((count, tok), 0) == f).astype(F32) for f in full_row]
+    tail = side32[...]
     gg_slot = tail[:, TAPS : TAPS + 1] + tail[:, TAPS + 1 : TAPS + 2]
     gg_row = [jnp.sum(h * gg_slot, axis=0, keepdims=True) for h in hot_row]
     b = dot32(tail.astype(BF), (hot_row[0] + hot_row[1]).astype(BF), TN)[:taps]
@@ -656,7 +658,11 @@
     grad_logits = sel_row[0] * grad_picked[0] + sel_row[1] * grad_picked[1]
     b = b + rstd_row * jnp.dot(rproj, grad_logits, precision=lax.Precision.HIGHEST, preferred_element_type=F32)
     c_row = jnp.sum(pt * b, axis=0, keepdims=True) * (rstd_row * rstd_row * (1.0 / dm))
+    proj0 = dot32(s_ref[...], gm_ref[...], NT)
+    proj1 = dot32(s_ref[...], stem_ref[...], NT)
     proj = proj0 + b - c_row * proj1
+    away.relay()
+    near.relay_far()
     rows3 = []
     for i in range(3):
         rows3.append(
@@ -670,8 +676,6 @@
     )
     pl.when(jnp.logical_not(first_row))(lambda: hb[0].start())
     pl.when(jnp.logical_not(last_row))(lambda: hb[1].start())
-    out = dot32(hot_col, ret32[:, pl.ds(0, dm)].astype(BF))
-    mixed_ref[...] = (stem_ref[...].astype(F32) + out).astype(BF)
     glat_ref[0] = rows3[0][:, wide:] + rows3[1][:, :wide]
     glat_ref[1] = rows3[1][:, wide:] + rows3[2][:, :wide]
 
@@ -684,40 +688,70 @@
     def _():
         rcopy(a_out.at[1], a_prev, hb_ss.at[1], hb_rs.at[1], pc.exp, pc.partner).wait_recv()
         glat_ref[0] = glat_ref[0] + a_prev[...]
+
+    away.relay_far()
+    square = [jnp.transpose(jnp.broadcast_to(f.astype(F32), (tok, tok)))[:, :1].astype(I32) for f in full_row]
+    hot_col = sum((iota((tok, count), 1) == f).astype(F32) for f in square).astype(BF)
 
     for copy in (ha[1], hb[0]):
         pl.when(jnp.logical_not(first_row))(copy.wait_send)
     for copy in (ha[0], hb[1]):
         pl.when(jnp.logical_not(last_row))(copy.wait_send)
+    scatter_t.finish()
+    scatter_d.finish()
 
     @pl.when(has_rows)
     def _():
         for k in range(1, EXP):
-            stage(k, False).wait_send()
-            stage(k, True).wait_send()
+            stage(k).wait_send()
+
+        def body(k, _):
+            rcopy(send_side, send_side, sd_ss.at[(pc.e + k) % EXP], sd_rs.at[0], pc.exp, pc.partner).wait_send()
+            return 0
+
+        lax.fori_loop(1, EXP, body, 0)
+        seven = send_side.at[pl.ds(0, EXP - 1)]
+        rcopy(seven, seven, sd_ss.at[pc.e], sd_rs.at[0], pc.exp, pc.partner).wait_send()
 
     def drain(s, _):
         for way, p in ((0, m - s), (1, m + s)):
 
             @pl.when(((p >= 0) if way == 0 else (p < SH)) & ends[way])
             def _():
-                hop_side(way, p, s).wait_send()
-                for c in range(len(CHUNKS)):
-                    hop(way, p, c, s).wait_send()
+                rcopy(recv.at[p], recv.at[p], ln_ss.at[way, s], ln_rs.at[p, 0], pc.exp, pc.partner).wait_send()
 
         for way, ok in ((0, s > m), (1, s < m)):
 
             @pl.when(ok & ends[way])
             def _():
-                for c in range(len(CHUNKS)):
-                    give(way, s, c).wait_send()
+                rcopy(part.at[s], acc_l.at[s], ca_ss.at[s], cl_rs.at[s, 0], pc.exp, pc.partner).wait_send()
+
+        @pl.when(s != m)
+        def _():
+            rcopy(send_back.at[s], send_back.at[s], bk_ss.at[s], bk_rs.at[0], pc.exp, pc.partner).wait_send()
 
         return 0
 
     lax.fori_loop(0, SH, drain, 0)
     for i in range(TILES):
-        source, copy = home(i)
-        pl.when(source != pc.e)(lambda copy=copy: copy.wait_send())
+
+        @pl.when(source_of(i) != pc.e)
+        def _():
+            home(i)[1].wait_send()
+            reply(m, i, bo_ss.at[i]).wait_send()
+
+    near.finish()
+    away.finish()
+
+    def collect(k, _):
+        for i in range(EXP):
+            at = pl.multiple_of(k * EXP * ROWS + i * ROWS, ROWS)
+            ret32[pl.ds(at, ROWS), :] = slots[k, i // 4, i % 4].astype(F32)
+        return 0
+
+    lax.fori_loop(0, TILES, collect, 0)
+    out = dot32(hot_col, ret32[...].astype(BF))
+    mixed_ref[...] = (stem_ref[...].astype(F32) + out).astype(BF)
 
 
 def local(latent, stem_weight, norm_gain, router_weight, routes, gate_weight, up_weight, down_weight, grad_mixed):
@@ -725,27 +759,25 @@
     dsl, hid = gate_weight.shape
     rows_here, chan, wide = latent.shape
     taps = stem_weight.shape[0]
-    full = dm + SIDE
     dma = pltpu.SemaphoreType.DMA
     chunks = len(CHUNKS)
     v = pltpu.VMEM
-    return pl.pallas_call(
+    outs = pl.pallas_call(
         layer_kernel,
         out_shape=(
             jax.ShapeDtypeStruct((tok, dm), BF),
             jax.ShapeDtypeStruct((rows_here, chan, wide), F32),
             jax.ShapeDtypeStruct((dsl, hid), F32),
             jax.ShapeDtypeStruct((dsl, hid), F32),
-            jax.ShapeDtypeStruct((hid, dsl), F32),
+            jax.ShapeDtypeStruct((dsl, hid), F32),
         ),
-        in_specs=[VM] * 10,
+        in_specs=[VM] * 9,
         out_specs=(VM,) * 5,
         scratch_shapes=[
             v((EXP, ROWS, dm), BF),
             v((EXP, ROWS, SIDE), BF),
             v((SH, TILES, ROWS, dm), BF),
             v((SH, TILES, ROWS, SIDE), BF),
-            v((dsl, hid), BF),
             v((REP, dsl, hid), BF),
             v((2, 4, TP, 2 * hid), F32),
             v((TP, 2 * hid), F32),
@@ -758,16 +790,21 @@
             v((taps, dsl), BF),
             v((taps, dsl), BF),
             v((SH * PIECE, dm), F32),
+            v((SH * PIECE, SIDE), F32),
             v((SH * PIECE, dm), BF),
             v((SH * PIECE, hid), BF),
             v((SH * PIECE, 2 * hid), BF),
-            v((SH, TILES, ROWS, full), BF),
-            v((SH, TILES, ROWS, full), BF),
-            v((SH, TILES, ROWS, full), BF),
-            v((TILES, ROWS, full), BF),
-            v((SH * PIECE, full), F32),
-            v((TILES, EXP, ROWS, full), BF),
-            v((2, 4, hid, dsl), BF),
+            v((SH, TILES, ROWS, dm), BF),
+            v((SH, TILES, ROWS, dm), BF),
+            v((SH, TILES, ROWS, dm), BF),
+            v((TILES, ROWS, dm), BF),
+            v((SH * PIECE, dm), F32),
+            v((SH, TILES, ROWS, SIDE), BF),
+            v((SH, EXP, ROWS, SIDE), BF),
+            v((EXP, ROWS, SIDE), BF),
+            v((TILES, EXP, ROWS, SIDE), BF),
+            v((TILES, 2, EXP // 2, ROWS, dm), BF),
+            v((2, 4, dsl, hid), BF),
             v((2, 4, TP, 2 * hid), F32),
             v((TP, 2 * hid), F32),
             v((REP, TP, 2 * hid), F32),
@@ -776,23 +813,24 @@
             v((chan, wide), F32),
         ]
         + scatter_scratch((TP, 2 * hid), F32)
-        + scatter_scratch((hid, dsl), BF)
+        + scatter_scratch((dsl, hid), BF)
         + scatter_scratch((TP, 2 * hid), F32)
-        + gather_scratch() * 4
+        + gather_scratch() * 6
         + [
             dma((EXP,)),
             dma((TILES,)),
             dma((EXP,)),
-            dma((TILES,)),
-            dma((2, SH, chunks)),
+            dma((SH,)),
+            dma((2, SH)),
             dma((SH, chunks)),
-            dma((2, SH)),
             dma((SH,)),
             dma((SH, chunks)),
             dma((SH, chunks)),
-            dma((SH, chunks)),
             dma((TILES,)),
-            dma((EXP,)),
+            dma((2,)),
+            dma((SH,)),
+            dma((TILES,)),
+            dma((1,)),
             dma((2,)),
             dma((2,)),
             dma((2,)),
@@ -802,9 +840,10 @@
         compiler_params=pltpu.CompilerParams(collective_id=0, has_side_effects=True),
         name="layer",
     )(
-        latent, stem_weight, norm_gain.reshape(1, -1), router_weight.T, routes, routes.T,
-        gate_weight, up_weight, down_weight, grad_mixed,
+        latent, stem_weight, norm_gain, router_weight.T, routes.T,
+        gate_weight, up_weight, down_weight.T, grad_mixed,
     )
+    return outs[:4] + (outs[4].T,)
 
 
 def solution(mesh):

time: 140 us -> 124 us (0.89)
  Pallas kernels: 130 us -> 117 us
  local copies, waits for them, and re-layouts: 8.83 us -> 5.28 us
    pallas_call x1, Pallas kernels: 130 us -> 117 us  [local(): pl.pallas_call(layer_kernel, out_shape=(jax.ShapeDtypeStruct((tok, dm), B...]
    pallas_call x1 -> x0, local copies, waits for them, and re-layouts: 1.91 us -> none  [local(): pl.pallas_call(layer_kernel, out_shape=(jax.ShapeDtypeStruct((tok, dm), B...]
    unnamed x16 -> x13, local copies, waits for them, and re-layouts: 5.61 us -> 5.28 us
where the time goes in v4:
time: 124 us; the launch traced here: 123 us
  Pallas kernels  117 us (94%)
  local copies, waits for them, and re-layouts  5.28 us (4%)
    pallas_call x1, Pallas kernels, local(): pl.pallas_call(layer_kernel, out_shape=(jax.ShapeDtypeStruct((tok, dm), B...  117 us
    unnamed x13, local copies, waits for them, and re-layouts  5.28 us

profile of v4, /device:TPU:1, one launch (start us, length us, event | category | flops | bytes accessed | tf_op | source)
XLA Modules:
  0.0 122.6 jit_solution(16754998924086424)
XLA Ops:
  0.6 116.7 %layer.1 = (bf16[128,1536]{1,0:T(8,128)(2,1)}, f32[2,16,64]{2,1,0:T(8,128)}, f32[192,384]{1,0:T(8,128)}, f32[192,384]{1,0:T(8,128)}, f32[192,384]{1,0:T(8,128)}) custom-call(bf16[2,16,64]{2,1,0:T(8,128)(2,1)} %latent.1, bf16[144,1536]{1,0:T(8,128)(2,1)} %s_ref.1, f32[1536]{0:T(1024)} %gain_ref.1, bf16[8,1536]{1,0:T(8,128)(2,1)} %bitcast.6, ...), custom_call_target="tpu_custom_call" | custom-call | tf_op jit(solution)/shard_map/layer/pallas_call | solution.py:765
  117.3 0.0 copy-start.3
  117.3 0.0 copy-start.2
  117.3 1.8 %copy.19 = bf16[128,1536]{1,0:T(8,128)(2,1)} copy(bf16[128,1536]{1,0:T(8,128)(2,1)} %get-tuple-element.20) | data formatting | bytes 786432
  119.2 0.0 copy-done.3
  119.2 0.6 copy.20
  119.8 0.0 copy-done.2
  119.8 0.0 copy-start.1
  119.8 0.7 copy.21
  120.5 0.4 copy-done.1
  120.8 0.0 copy-start
  120.8 0.7 copy.22
  121.6 0.4 copy-done
  121.9 0.7 copy.23
Async XLA Ops:
  117.3 1.8 %copy-start.3 = (f32[2,16,64]{2,1,0:T(8,128)S(1)}, f32[2,16,64]{2,1,0:T(8,128)}, u32[]{:S(2)}) copy-start(f32[2,16,64]{2,1,0:T(8,128)} %get-tuple-element.21) | copy-start | bytes 24580
  117.3 2.4 %copy-start.2 = (f32[192,384]{1,0:T(8,128)S(1)}, f32[192,384]{1,0:T(8,128)}, u32[]{:S(2)}) copy-start(f32[192,384]{1,0:T(8,128)} %get-tuple-element.22) | copy-start | bytes 884740
  119.8 1.1 copy-start.1
  120.8 1.1 copy-start

commit v5 on v4

--- a/solution.py
+++ b/solution.py
@@ -75,7 +75,7 @@
         def hello(exp, rep):
             pl.semaphore_signal(bar, inc=1, device_id={"exp": exp, "rep": rep}, device_id_type=MESH)
 
-        for rep in (self.fwd, self.bwd, self.partner):
+        for rep in (self.fwd, self.bwd, self.rep_at(2), self.partner):
             hello(self.exp, rep)
 
         def body(n, _):
@@ -85,7 +85,7 @@
         lax.fori_loop(1, EXP * SH, body, 0)
 
     def enter(self):
-        pl.semaphore_wait(pltpu.get_barrier_semaphore(), EXP * SH + 2)
+        pl.semaphore_wait(pltpu.get_barrier_semaphore(), EXP * SH + 3)
 
 
 class Gather:
@@ -110,7 +110,7 @@
             (self.src, own, 0, pc.fwd),
             (self.src, own, 1, pc.bwd),
             (self.src, own, 2, part),
-            (self.piece(pc.bwd), pc.bwd, 3, pc.fwd),
+            (self.src, own, 3, far),
             (self.piece(pc.bwd), pc.bwd, 4, part),
             (self.piece(pc.fwd), pc.fwd, 5, part),
             (self.piece(far), far, 6, part),
@@ -118,8 +118,9 @@
 
     def start(self):
         def go():
-            for mv in self.moves()[:3]:
-                self.copy(*mv).start()
+            mv = self.moves()
+            for k in (3, 0, 1, 2):
+                self.copy(*mv[k]).start()
 
         self.guard(self.pc.rep, go)
 
@@ -131,7 +132,6 @@
 
         def near():
             self.arrive(self.pc.bwd)
-            self.copy(*mv[3]).start()
             self.copy(*mv[4]).start()
 
         self.guard(self.pc.bwd, near)
@@ -169,7 +169,7 @@
         at = lambda dy: self.total.at[(y + dy + 4) % 4]
         src, dst, rep = (
             (self.src.at[1 - pc.c], self.got, pc.partner),
-            (at(2), self.side.at[0], pc.fwd),
+            (at(2), self.side.at[0], pc.rep_at(2)),
             (at(-d), self.side.at[1], pc.bwd),
             (at(d), self.side.at[2], pc.fwd),
         )[k]
@@ -186,20 +186,13 @@
             return 0
 
         lax.fori_loop(0, 4, body, 0)
-        self.copy(1).start()
-        self.copy(2).start()
-
-    def pass_on(self):
-        pc = self.pc
-        self.copy(1).wait_recv()
-        at = (pc.y + pc.d + 4) % 4
-        self.total[at] = (self.total[at].astype(F32) + self.side[0].astype(F32)).astype(self.total.dtype)
-        self.copy(3).start()
+        for k in (1, 2, 3):
+            self.copy(k).start()
 
     def result(self):
-        self.copy(2).wait_recv()
-        self.copy(3).wait_recv()
-        return self.total[self.pc.y].astype(F32) + self.side[1].astype(F32) + self.side[2].astype(F32)
+        for k in (1, 2, 3):
+            self.copy(k).wait_recv()
+        return self.total[self.pc.y].astype(F32) + sum(self.side[k].astype(F32) for k in range(3))
 
     def finish(self):
         for k in range(4):
@@ -265,33 +258,6 @@
     for e in range(EXP):
         send[e] = picked_rows[e * ROWS : (e + 1) * ROWS].astype(BF)
 
-    pc.enter()
-
-    ha = (
-        rcopy(latent.at[1], h_prev, ha_ss.at[0], ha_rs.at[0], pc.exp + 1, pc.rep),
-        rcopy(latent.at[0], h_next, ha_ss.at[1], ha_rs.at[1], pc.exp - 1, pc.rep),
-    )
-    first_row, last_row = pc.exp == 0, pc.exp == EXP * SH - 1
-    pl.when(jnp.logical_not(last_row))(lambda: ha[0].start())
-    pl.when(jnp.logical_not(first_row))(lambda: ha[1].start())
-
-    def stage(k):
-        peer = (pc.e + k) % EXP
-        return rcopy(send.at[peer], recv.at[m, pc.tile], st_ss.at[k], st_rs.at[pc.tile], peer * SH + m, pc.rep)
-
-    keep_gm = pltpu.make_async_copy(send.at[pc.e], recv.at[m, pc.tile], loc.at[0])
-
-    @pl.when(has_rows)
-    def _():
-        for k in (1, 7, 2, 6, 3, 5, 4):
-            stage(k).start()
-        keep_gm.start()
-
-    gather_w = Gather(pc, wd_ref, lambda rep: wfull.at[rep], wg_ss, wg_rs)
-    own_w = pltpu.make_async_copy(wd_ref, wfull.at[pc.rep], loc.at[2])
-    gather_w.start()
-    own_w.start()
-
     gain = gain_ref[...].reshape(1, dm)
     dsl = wg_ref.shape[0]
     sg = s_ref[...].astype(F32) * gain
@@ -309,6 +275,34 @@
     for k in range(REP):
         gp[k // 4, k % 4] = share[k * TP : (k + 1) * TP]
     rproj = dot32(hi, wr_ref[...], NT) + dot32(lo, wr_ref[...], NT)
+
+    pc.enter()
+
+    ha = (
+        rcopy(latent.at[1], h_prev, ha_ss.at[0], ha_rs.at[0], pc.exp + 1, pc.rep),
+        rcopy(latent.at[0], h_next, ha_ss.at[1], ha_rs.at[1], pc.exp - 1, pc.rep),
+    )
+    first_row, last_row = pc.exp == 0, pc.exp == EXP * SH - 1
+    pl.when(jnp.logical_not(last_row))(lambda: ha[0].start())
+    pl.when(jnp.logical_not(first_row))(lambda: ha[1].start())
+
+    def stage(k):
+        peer = (pc.e + k) % EXP
+        return rcopy(send.at[peer], recv.at[m, pc.tile], st_ss.at[k], st_rs.at[pc.tile], peer * SH + m, pc.rep)
+
+    keep_gm = pltpu.make_async_copy(send.at[pc.e], recv.at[m, pc.tile], loc.at[0])
+
+    @pl.when(has_rows)
+    def _():
+        for k in (1, 7, 2, 6, 3, 5, 4):
+            stage(k).start()
+        keep_gm.start()
+
+    gather_w = Gather(pc, wd_ref, lambda rep: wfull.at[rep], wg_ss, wg_rs)
+    own_w = pltpu.make_async_copy(wd_ref, wfull.at[pc.rep], loc.at[2])
+    gather_w.start()
+    own_w.start()
+
     scatter_g = Scatter(pc, gp, g_got, g_tot, g_side, g_ss, g_rs)
     scatter_g.start()
 
@@ -371,6 +365,8 @@
     for e in range(EXP):
         send_side[e] = side[e * ROWS : (e + 1) * ROWS].astype(BF)
 
+    scatter_g.add()
+
     def to_all(n):
         dest = (pc.exp + n) % (EXP * SH)
         e = dest // SH
@@ -419,8 +415,6 @@
         for way, p in ((0, m - s), (1, m + s)):
             pl.when((p >= 0) if way == 0 else (p < SH))(lambda p=p: widen(p))
         return 0
-
-    scatter_g.add()
 
     @pl.when(has_rows)
     def _():
@@ -431,22 +425,20 @@
             arrived(i)
         for way in range(2):
             pl.when(ends[way])(lambda way=way, c=c: hop(way, m, c, 0).start())
-    widen(m)
-    scatter_g.pass_on()
-    gather_w.relay()
-    lax.fori_loop(1, 2, step, 0)
     gmine[...] = scatter_g.result()
     spot = lambda ref: lambda rep: ref.at[(rep % 2) * 4 + rep // 2]
     gather_g = Gather(pc, gmine, spot(gfull), ag_ss, ag_rs)
     own_g = pltpu.make_async_copy(gmine, spot(gfull)(pc.rep), loc.at[3])
     gather_g.start()
     own_g.start()
+    widen(m)
+    gather_w.relay()
+    lax.fori_loop(1, 2, step, 0)
     gather_w.relay_far()
+    gather_g.relay()
     lax.fori_loop(2, 3, step, 0)
-    gather_g.relay()
+    gather_g.relay_far()
     lax.fori_loop(3, 4, step, 0)
-    gather_g.relay_far()
-    lax.fori_loop(4, 7, step, 0)
     gather_g.finish()
     gather_w.finish()
     scatter_g.finish()
@@ -510,8 +502,9 @@
     def steps(at, to):
         lax.fori_loop(at, to, step_sum, 0)
 
-    steps(0, 1)
-    lax.fori_loop(7, 8, step, 0)
+    for n in range(4):
+        steps(n, n + 1)
+        lax.fori_loop(4 + n, 5 + n, step, 0)
 
     gm_all[...] = row32[...].astype(BF)
     u = dot32(gm_all[...], down_t)
@@ -550,7 +543,7 @@
         return 0
 
     lax.fori_loop(0, SH, narrow, 0)
-    steps(1, 2)
+    steps(4, 5)
     t_share = dot32(pr, dpre_ref[...], TN)
     for k in range(REP):
         tp[k // 4, k % 4] = t_share[k * TP : (k + 1) * TP]
@@ -561,44 +554,24 @@
         dp[k % 2, k // 2] = d_share[k * dsl : (k + 1) * dsl].astype(BF)
     scatter_d = Scatter(pc, dp, d_got, d_tot, d_side, d_ss, d_rs)
     scatter_d.start()
-    steps(2, 3)
+    steps(5, 6)
     scatter_t.add()
     scatter_d.add()
-    steps(3, 4)
-    scatter_t.pass_on()
-    scatter_d.pass_on()
-    steps(4, 5)
-    tmine[...] = scatter_t.result()
+    steps(6, 7)
     gather_t = Gather(pc, tmine, spot(tfull), tg_ss, tg_rs)
     own_t = pltpu.make_async_copy(tmine, spot(tfull)(pc.rep), loc.at[4])
-    gather_t.start()
-    own_t.start()
     with_rows = lambda rep: pc.tile_of(rep) < TILES
     tile_at = lambda rep: pc.tile_of(rep) % TILES
     gather_b = Gather(pc, bsum, lambda rep: back_all.at[tile_at(rep)], bg_ss, bg_rs, with_rows)
     own_b = pltpu.make_async_copy(bsum, back_all.at[pc.tile % TILES], loc.at[1])
 
-    @pl.when(has_rows)
-    def _():
-        pltpu.make_async_copy(back_in, back_in, bk_rs.at[0]).wait()
-        for k in range(EXP):
-            bsum[k] = sum(back_in[j, k].astype(F32) for j in range(SH)).astype(BF)
-        own_b.start()
-
-    gather_b.start()
-    gdown_ref[...] = scatter_d.result()
-    steps(5, 6)
-    gather_t.relay()
-    gather_b.relay()
-    steps(6, 7)
-
     def home(i):
         source = source_of(i)
         return source, rcopy(
-            sums.at[i], slots.at[i, pc.half, pc.x], ct_ss.at[i], ct_rs.at[pc.half], source * SH + m, pc.rep
+            sums.at[i], slots.at[pc.half, i, pc.x], ct_ss.at[i], ct_rs.at[pc.half], source * SH + m, pc.rep
         )
 
-    keep_out = lambda i: pltpu.make_async_copy(sums.at[i], slots.at[i, pc.half, pc.x], ct_rs.at[pc.half])
+    keep_out = lambda i: pltpu.make_async_copy(sums.at[i], slots.at[pc.half, i, pc.x], ct_rs.at[pc.half])
     for c, (at, count) in enumerate(CHUNKS):
         for way in range(2):
             pl.when(ends[1 - way])(lambda way=way, c=c: give(way, m, c).wait_recv())
@@ -621,25 +594,36 @@
 
     def out_gather(h, ss, rs):
         half = (pc.half + h) % 2
-        ready = slots.at[pc.tile % TILES, half]
-        gather = Gather(pc, ready, lambda rep: slots.at[tile_at(rep), half], ss, rs, with_rows)
+        ready = slots.at[half, pc.tile % TILES]
+        gather = Gather(pc, ready, lambda rep: slots.at[half, tile_at(rep)], ss, rs, with_rows)
         wait = pltpu.make_async_copy(ready, ready, ct_rs.at[half])
-        return gather, wait
-
-    (near, near_wait), (away, away_wait) = out_gather(0, s0_ss, s0_rs), out_gather(1, s1_ss, s1_rs)
-    gather_t.relay_far()
-    gather_b.relay_far()
+        return half, gather, wait
+
+    near_half, near, near_wait = out_gather(0, s0_ss, s0_rs)
+    away_half, away, away_wait = out_gather(1, s1_ss, s1_rs)
+
+    @pl.when(has_rows)
+    def _():
+        pltpu.make_async_copy(back_in, back_in, bk_rs.at[0]).wait()
+        for k in range(EXP):
+            bsum[k] = sum(back_in[j, k].astype(F32) for j in range(SH)).astype(BF)
+        own_b.start()
+
+    gather_b.start()
+    tmine[...] = scatter_t.result()
+    gather_t.start()
+    own_t.start()
     pl.when(has_rows)(near_wait.wait)
     near.start()
-    gather_t.finish()
-    own_t.wait()
-    t_hi, t_lo = split(tfull[...].reshape(TAPS, 2 * hid)[:taps])
-    gw = dot32(sg_hi[...], t_hi, TN) + dot32(sg_hi[...], t_lo, TN) + dot32(sg_lo[...], t_hi, TN)
-    ggate_ref[...] = gw[:, :hid]
-    gup_ref[...] = gw[:, hid:]
+    gather_b.relay()
+    gather_t.relay()
+    gather_b.relay_far()
+    near.relay()
+    gather_t.relay_far()
+    near.relay_far()
     pl.when(has_rows)(away_wait.wait)
     away.start()
-    near.relay()
+    gdown_ref[...] = scatter_d.result()
     pl.when(has_rows)(own_b.wait)
     gather_b.finish()
 
@@ -661,8 +645,6 @@
     proj0 = dot32(s_ref[...], gm_ref[...], NT)
     proj1 = dot32(s_ref[...], stem_ref[...], NT)
     proj = proj0 + b - c_row * proj1
-    away.relay()
-    near.relay_far()
     rows3 = []
     for i in range(3):
         rows3.append(
@@ -689,9 +671,31 @@
         rcopy(a_out.at[1], a_prev, hb_ss.at[1], hb_rs.at[1], pc.exp, pc.partner).wait_recv()
         glat_ref[0] = glat_ref[0] + a_prev[...]
 
+    away.relay()
     away.relay_far()
+    gather_t.finish()
+    own_t.wait()
+    t_hi, t_lo = split(tfull[...].reshape(TAPS, 2 * hid)[:taps])
+    gw = dot32(sg_hi[...], t_hi, TN) + dot32(sg_hi[...], t_lo, TN) + dot32(sg_lo[...], t_hi, TN)
+    ggate_ref[...] = gw[:, :hid]
+    gup_ref[...] = gw[:, hid:]
     square = [jnp.transpose(jnp.broadcast_to(f.astype(F32), (tok, tok)))[:, :1].astype(I32) for f in full_row]
-    hot_col = sum((iota((tok, count), 1) == f).astype(F32) for f in square).astype(BF)
+    span = count // 2
+
+    def out_of(half, gather):
+        hot = jnp.zeros((tok, span), F32)
+        for f in square:
+            t = lax.shift_right_logical(f, 6)
+            own = (lax.shift_right_logical(f, 5) & 1) == half
+            at = jnp.where(own, t * (EXP // 2 * ROWS) + (f & 31), -1)
+            hot = hot + (iota((tok, span), 1) == at).astype(F32)
+        gather.finish()
+        for t in range(TILES):
+            for x in range(EXP // 2):
+                ret32[pl.ds((t * (EXP // 2) + x) * ROWS, ROWS), :] = slots[half, t, x].astype(F32)
+        return dot32(hot.astype(BF), ret32[pl.ds(0, span), :].astype(BF))
+
+    sv_out = stem_ref[...].astype(F32) + out_of(near_half, near)
 
     for copy in (ha[1], hb[0]):
         pl.when(jnp.logical_not(first_row))(copy.wait_send)
@@ -740,18 +744,7 @@
             home(i)[1].wait_send()
             reply(m, i, bo_ss.at[i]).wait_send()
 
-    near.finish()
-    away.finish()
-
-    def collect(k, _):
-        for i in range(EXP):
-            at = pl.multiple_of(k * EXP * ROWS + i * ROWS, ROWS)
-            ret32[pl.ds(at, ROWS), :] = slots[k, i // 4, i % 4].astype(F32)
-        return 0
-
-    lax.fori_loop(0, TILES, collect, 0)
-    out = dot32(hot_col, ret32[...].astype(BF))
-    mixed_ref[...] = (stem_ref[...].astype(F32) + out).astype(BF)
+    mixed_ref[...] = (sv_out + out_of(away_half, away)).astype(BF)
 
 
 def local(latent, stem_weight, norm_gain, router_weight, routes, gate_weight, up_weight, down_weight, grad_mixed):
@@ -803,7 +796,7 @@
             v((SH, EXP, ROWS, SIDE), BF),
             v((EXP, ROWS, SIDE), BF),
             v((TILES, EXP, ROWS, SIDE), BF),
-            v((TILES, 2, EXP // 2, ROWS, dm), BF),
+            v((2, TILES, EXP // 2, ROWS, dm), BF),
             v((2, 4, dsl, hid), BF),
             v((2, 4, TP, 2 * hid), F32),
             v((TP, 2 * hid), F32),

time: 124 us -> 110 us (0.89)
  Pallas kernels: 117 us -> 104 us
    pallas_call x1, Pallas kernels: 117 us -> 104 us  [local(): pl.pallas_call(layer_kernel, out_shape=(jax.ShapeDtypeStruct((tok, dm), B...]
where the time goes in v5:
time: 110 us
  Pallas kernels  104 us (95%)
  local copies, waits for them, and re-layouts  5.28 us (5%)
    pallas_call x1, Pallas kernels, local(): pl.pallas_call(layer_kernel, out_shape=(jax.ShapeDtypeStruct((tok, dm), B...  104 us
    unnamed x13, local copies, waits for them, and re-layouts  5.28 us

profile of v5, /device:TPU:1, one launch (start us, length us, event | category | flops | bytes accessed | tf_op | source)
XLA Modules:
  0.0 109.8 jit_solution(2645102544167750236)
XLA Ops:
  0.6 103.9 %layer.1 = (bf16[128,1536]{1,0:T(8,128)(2,1)}, f32[2,16,64]{2,1,0:T(8,128)}, f32[192,384]{1,0:T(8,128)}, f32[192,384]{1,0:T(8,128)}, f32[192,384]{1,0:T(8,128)}) custom-call(bf16[2,16,64]{2,1,0:T(8,128)(2,1)} %latent.1, bf16[144,1536]{1,0:T(8,128)(2,1)} %s_ref.1, f32[1536]{0:T(1024)} %gain_ref.1, bf16[8,1536]{1,0:T(8,128)(2,1)} %bitcast.6, ...), custom_call_target="tpu_custom_call" | custom-call | tf_op jit(solution)/shard_map/layer/pallas_call | solution.py:758
  104.5 0.0 copy-start.3
  104.5 0.0 copy-start.2
  104.6 1.8 %copy.19 = bf16[128,1536]{1,0:T(8,128)(2,1)} copy(bf16[128,1536]{1,0:T(8,128)(2,1)} %get-tuple-element.20) | data formatting | bytes 786432
  106.4 0.0 copy-done.3
  106.4 0.6 copy.20
  107.0 0.0 copy-done.2
  107.0 0.0 copy-start.1
  107.0 0.7 copy.21
  107.7 0.4 copy-done.1
  108.1 0.0 copy-start
  108.1 0.7 copy.22
  108.8 0.4 copy-done
  109.1 0.7 copy.23
Async XLA Ops:
  104.5 1.8 %copy-start.3 = (f32[2,16,64]{2,1,0:T(8,128)S(1)}, f32[2,16,64]{2,1,0:T(8,128)}, u32[]{:S(2)}) copy-start(f32[2,16,64]{2,1,0:T(8,128)} %get-tuple-element.21) | copy-start | bytes 24580
  104.5 2.4 %copy-start.2 = (f32[192,384]{1,0:T(8,128)S(1)}, f32[192,384]{1,0:T(8,128)}, u32[]{:S(2)}) copy-start(f32[192,384]{1,0:T(8,128)} %get-tuple-element.22) | copy-start | bytes 884740
  107.0 1.1 copy-start.1
  108.1 1.1 copy-start

commit v6 on v5

--- a/solution.py
+++ b/solution.py
@@ -436,9 +436,8 @@
     lax.fori_loop(1, 2, step, 0)
     gather_w.relay_far()
     gather_g.relay()
+    gather_g.relay_far()
     lax.fori_loop(2, 3, step, 0)
-    gather_g.relay_far()
-    lax.fori_loop(3, 4, step, 0)
     gather_g.finish()
     gather_w.finish()
     scatter_g.finish()
@@ -502,9 +501,9 @@
     def steps(at, to):
         lax.fori_loop(at, to, step_sum, 0)
 
-    for n in range(4):
+    for n in range(5):
         steps(n, n + 1)
-        lax.fori_loop(4 + n, 5 + n, step, 0)
+        lax.fori_loop(3 + n, 4 + n, step, 0)
 
     gm_all[...] = row32[...].astype(BF)
     u = dot32(gm_all[...], down_t)
@@ -512,6 +511,7 @@
     gu = (rs * gt) * u
     dpre = jnp.concatenate([gu * slope, gu * silu], axis=1).astype(BF)
     dpre_ref[...] = dpre
+    steps(5, 6)
     back = dot32(dpre, g_hi, NT) + dot32(dpre, g_lo, NT)
     gg_hi = gg.astype(BF).astype(F32)
     lane = iota((SH * PIECE, SIDE - TAPS), 1)
@@ -543,7 +543,41 @@
         return 0
 
     lax.fori_loop(0, SH, narrow, 0)
-    steps(4, 5)
+    steps(6, 7)
+    gather_t = Gather(pc, tmine, spot(tfull), tg_ss, tg_rs)
+    own_t = pltpu.make_async_copy(tmine, spot(tfull)(pc.rep), loc.at[4])
+    with_rows = lambda rep: pc.tile_of(rep) < TILES
+    tile_at = lambda rep: pc.tile_of(rep) % TILES
+    gather_b = Gather(pc, bsum, lambda rep: back_all.at[tile_at(rep)], bg_ss, bg_rs, with_rows)
+    own_b = pltpu.make_async_copy(bsum, back_all.at[pc.tile % TILES], loc.at[1])
+
+    def home(i):
+        source = source_of(i)
+        return source, rcopy(
+            sums.at[i], slots.at[pc.half, i, pc.x], ct_ss.at[i], ct_rs.at[pc.half], source * SH + m, pc.rep
+        )
+
+    keep_out = lambda i: pltpu.make_async_copy(sums.at[i], slots.at[pc.half, i, pc.x], ct_rs.at[pc.half])
+    for c, (at, count) in enumerate(CHUNKS):
+        for way in range(2):
+            pl.when(ends[1 - way])(lambda way=way, c=c: give(way, m, c).wait_recv())
+        for i in range(at, at + count):
+            @pl.when(m == 0)
+            def _():
+                sums[i] = (mine(m, i) + acc_r[m, i].astype(F32)).astype(BF)
+
+            @pl.when(m == SH - 1)
+            def _():
+                sums[i] = (mine(m, i) + acc_l[m, i].astype(F32)).astype(BF)
+
+            @pl.when(ends[0] & ends[1])
+            def _():
+                sums[i] = (mine(m, i) + acc_l[m, i].astype(F32) + acc_r[m, i].astype(F32)).astype(BF)
+
+            source, copy = home(i)
+            pl.when(source != pc.e)(lambda copy=copy: copy.start())
+            pl.when(source == pc.e)(lambda i=i: keep_out(i).start())
+
     t_share = dot32(pr, dpre_ref[...], TN)
     for k in range(REP):
         tp[k // 4, k % 4] = t_share[k * TP : (k + 1) * TP]
@@ -554,43 +588,6 @@
         dp[k % 2, k // 2] = d_share[k * dsl : (k + 1) * dsl].astype(BF)
     scatter_d = Scatter(pc, dp, d_got, d_tot, d_side, d_ss, d_rs)
     scatter_d.start()
-    steps(5, 6)
-    scatter_t.add()
-    scatter_d.add()
-    steps(6, 7)
-    gather_t = Gather(pc, tmine, spot(tfull), tg_ss, tg_rs)
-    own_t = pltpu.make_async_copy(tmine, spot(tfull)(pc.rep), loc.at[4])
-    with_rows = lambda rep: pc.tile_of(rep) < TILES
-    tile_at = lambda rep: pc.tile_of(rep) % TILES
-    gather_b = Gather(pc, bsum, lambda rep: back_all.at[tile_at(rep)], bg_ss, bg_rs, with_rows)
-    own_b = pltpu.make_async_copy(bsum, back_all.at[pc.tile % TILES], loc.at[1])
-
-    def home(i):
-        source = source_of(i)
-        return source, rcopy(
-            sums.at[i], slots.at[pc.half, i, pc.x], ct_ss.at[i], ct_rs.at[pc.half], source * SH + m, pc.rep
-        )
-
-    keep_out = lambda i: pltpu.make_async_copy(sums.at[i], slots.at[pc.half, i, pc.x], ct_rs.at[pc.half])
-    for c, (at, count) in enumerate(CHUNKS):
-        for way in range(2):
-            pl.when(ends[1 - way])(lambda way=way, c=c: give(way, m, c).wait_recv())
-        for i in range(at, at + count):
-            @pl.when(m == 0)
-            def _():
-                sums[i] = (mine(m, i) + acc_r[m, i].astype(F32)).astype(BF)
-
-            @pl.when(m == SH - 1)
-            def _():
-                sums[i] = (mine(m, i) + acc_l[m, i].astype(F32)).astype(BF)
-
-            @pl.when(ends[0] & ends[1])
-            def _():
-                sums[i] = (mine(m, i) + acc_l[m, i].astype(F32) + acc_r[m, i].astype(F32)).astype(BF)
-
-            source, copy = home(i)
-            pl.when(source != pc.e)(lambda copy=copy: copy.start())
-            pl.when(source == pc.e)(lambda i=i: keep_out(i).start())
 
     def out_gather(h, ss, rs):
         half = (pc.half + h) % 2
@@ -610,20 +607,21 @@
         own_b.start()
 
     gather_b.start()
+    scatter_t.add()
+    pl.when(has_rows)(near_wait.wait)
+    near.start()
+    scatter_d.add()
+    gather_b.relay()
+    gather_b.relay_far()
     tmine[...] = scatter_t.result()
     gather_t.start()
     own_t.start()
-    pl.when(has_rows)(near_wait.wait)
-    near.start()
-    gather_b.relay()
-    gather_t.relay()
-    gather_b.relay_far()
     near.relay()
-    gather_t.relay_far()
     near.relay_far()
     pl.when(has_rows)(away_wait.wait)
     away.start()
-    gdown_ref[...] = scatter_d.result()
+    gather_t.relay()
+    gather_t.relay_far()
     pl.when(has_rows)(own_b.wait)
     gather_b.finish()
 
@@ -673,6 +671,7 @@
 
     away.relay()
     away.relay_far()
+    gdown_ref[...] = scatter_d.result()
     gather_t.finish()
     own_t.wait()
     t_hi, t_lo = split(tfull[...].reshape(TAPS, 2 * hid)[:taps])
@@ -745,6 +744,12 @@
             reply(m, i, bo_ss.at[i]).wait_send()
 
     mixed_ref[...] = (sv_out + out_of(away_half, away)).astype(BF)
+
+
+def hand_over_kernel(*refs):
+    half = len(refs) // 2
+    for src, dst in zip(refs[:half], refs[half:]):
+        dst[...] = src[...]
 
 
 def local(latent, stem_weight, norm_gain, router_weight, routes, gate_weight, up_weight, down_weight, grad_mixed):
@@ -836,7 +841,14 @@
         latent, stem_weight, norm_gain, router_weight.T, routes.T,
         gate_weight, up_weight, down_weight.T, grad_mixed,
     )
-    return outs[:4] + (outs[4].T,)
+    outs = pl.pallas_call(
+        hand_over_kernel,
+        out_shape=tuple(jax.ShapeDtypeStruct(o.shape, o.dtype) for o in outs),
+        in_specs=[VM] * len(outs),
+        out_specs=(VM,) * len(outs),
+        name="hand_over",
+    )(*outs)
+    return tuple(outs[:4]) + (outs[4].T,)
 
 
 def solution(mesh):

time: 110 us -> 116 us (1.055)
  Pallas kernels: 104 us -> 114 us
  local copies, waits for them, and re-layouts: 5.28 us -> 0 us
    pallas_call x1, Pallas kernels: 104 us -> 112 us  [local(): pl.pallas_call(layer_kernel, out_shape=(jax.ShapeDtypeStruct((tok, dm), B...]
    unnamed x13 -> x0, local copies, waits for them, and re-layouts: 5.28 us -> none
    pallas_call x0 -> x1, Pallas kernels: none -> 2.34 us  [local(): pl.pallas_call(hand_over_kernel, out_shape=tuple((jax.ShapeDtypeStruct(o....]
where the time goes in v6:
time: 116 us; the launch traced here: 115 us
  Pallas kernels  114 us (98%)
    pallas_call x1, Pallas kernels, local(): pl.pallas_call(layer_kernel, out_shape=(jax.ShapeDtypeStruct((tok, dm), B...  112 us
    pallas_call x1, Pallas kernels, local(): pl.pallas_call(hand_over_kernel, out_shape=tuple((jax.ShapeDtypeStruct(o....  2.34 us

profile of v6, /device:TPU:1, one launch (start us, length us, event | category | flops | bytes accessed | tf_op | source)
XLA Modules:
  0.0 115.1 jit_solution(14813006060300513763)
XLA Ops:
  0.6 112.1 %layer.1 = (bf16[128,1536]{1,0:T(8,128)(2,1)}, f32[2,16,64]{2,1,0:T(8,128)}, f32[192,384]{1,0:T(8,128)}, f32[192,384]{1,0:T(8,128)}, f32[192,384]{1,0:T(8,128)}) custom-call(bf16[2,16,64]{2,1,0:T(8,128)(2,1)} %latent.1, bf16[144,1536]{1,0:T(8,128)(2,1)} %s_ref.1, f32[1536]{0:T(1024)} %gain_ref.1, bf16[8,1536]{1,0:T(8,128)(2,1)} %bitcast.5, ...), custom_call_target="tpu_custom_call" | custom-call | tf_op jit(solution)/shard_map/layer/pallas_call | solution.py:763
  112.7 2.3 %hand_over.1 = (bf16[128,1536]{1,0:T(8,128)(2,1)}, f32[2,16,64]{2,1,0:T(8,128)}, f32[192,384]{1,0:T(8,128)}, f32[192,384]{1,0:T(8,128)}, f32[192,384]{1,0:T(8,128)}) custom-call(bf16[128,1536]{1,0:T(8,128)(2,1)} %get-tuple-element.15.refs_0_, f32[2,16,64]{2,1,0:T(8,128)} %get-tuple-element.16.refs_1_, f32[192,384]{1,0:T(8,128)} %get-tuple-element.17.refs_2_, ...), custom_call_target="tpu_custom_call" | custom-call | tf_op jit(solution)/shard_map/hand_over/pallas_call | solution.py:844

commit v7 on v5

--- a/solution.py
+++ b/solution.py
@@ -745,6 +745,12 @@
             reply(m, i, bo_ss.at[i]).wait_send()
 
     mixed_ref[...] = (sv_out + out_of(away_half, away)).astype(BF)
+
+
+def hand_over_kernel(*refs):
+    half = len(refs) // 2
+    for src, dst in zip(refs[:half], refs[half:]):
+        dst[...] = src[...]
 
 
 def local(latent, stem_weight, norm_gain, router_weight, routes, gate_weight, up_weight, down_weight, grad_mixed):
@@ -836,7 +842,14 @@
         latent, stem_weight, norm_gain, router_weight.T, routes.T,
         gate_weight, up_weight, down_weight.T, grad_mixed,
     )
-    return outs[:4] + (outs[4].T,)
+    outs = pl.pallas_call(
+        hand_over_kernel,
+        out_shape=tuple(jax.ShapeDtypeStruct(o.shape, o.dtype) for o in outs),
+        in_specs=[VM] * len(outs),
+        out_specs=(VM,) * len(outs),
+        name="hand_over",
+    )(*outs)
+    return tuple(outs[:4]) + (outs[4].T,)
 
 
 def solution(mesh):

time: 110 us -> 107 us (0.973)
  local copies, waits for them, and re-layouts: 5.28 us -> 0 us
  Pallas kernels: 104 us -> 106 us
    unnamed x13 -> x0, local copies, waits for them, and re-layouts: 5.28 us -> none
    pallas_call x0 -> x1, Pallas kernels: none -> 2.34 us  [local(): pl.pallas_call(hand_over_kernel, out_shape=tuple((jax.ShapeDtypeStruct(o....]
where the time goes in v7:
time: 107 us
  Pallas kernels  106 us (99%)
    pallas_call x1, Pallas kernels, local(): pl.pallas_call(layer_kernel, out_shape=(jax.ShapeDtypeStruct((tok, dm), B...  104 us
    pallas_call x1, Pallas kernels, local(): pl.pallas_call(hand_over_kernel, out_shape=tuple((jax.ShapeDtypeStruct(o....  2.34 us

profile of v7, /device:TPU:1, one launch (start us, length us, event | category | flops | bytes accessed | tf_op | source)
XLA Modules:
  0.0 106.9 jit_solution(1048004945526472182)
XLA Ops:
  0.6 103.9 %layer.1 = (bf16[128,1536]{1,0:T(8,128)(2,1)}, f32[2,16,64]{2,1,0:T(8,128)}, f32[192,384]{1,0:T(8,128)}, f32[192,384]{1,0:T(8,128)}, f32[192,384]{1,0:T(8,128)}) custom-call(bf16[2,16,64]{2,1,0:T(8,128)(2,1)} %latent.1, bf16[144,1536]{1,0:T(8,128)(2,1)} %s_ref.1, f32[1536]{0:T(1024)} %gain_ref.1, bf16[8,1536]{1,0:T(8,128)(2,1)} %bitcast.5, ...), custom_call_target="tpu_custom_call" | custom-call | tf_op jit(solution)/shard_map/layer/pallas_call | solution.py:764
  104.5 2.3 %hand_over.1 = (bf16[128,1536]{1,0:T(8,128)(2,1)}, f32[2,16,64]{2,1,0:T(8,128)}, f32[192,384]{1,0:T(8,128)}, f32[192,384]{1,0:T(8,128)}, f32[192,384]{1,0:T(8,128)}) custom-call(bf16[128,1536]{1,0:T(8,128)(2,1)} %get-tuple-element.15.refs_0_, f32[2,16,64]{2,1,0:T(8,128)} %get-tuple-element.16.refs_1_, f32[192,384]{1,0:T(8,128)} %get-tuple-element.17.refs_2_, ...), custom_call_target="tpu_custom_call" | custom-call | tf_op jit(solution)/shard_map/hand_over/pallas_call | solution.py:845

commit v8 on v7

--- a/solution.py
+++ b/solution.py
@@ -436,9 +436,8 @@
     lax.fori_loop(1, 2, step, 0)
     gather_w.relay_far()
     gather_g.relay()
+    gather_g.relay_far()
     lax.fori_loop(2, 3, step, 0)
-    gather_g.relay_far()
-    lax.fori_loop(3, 4, step, 0)
     gather_g.finish()
     gather_w.finish()
     scatter_g.finish()
@@ -502,9 +501,9 @@
     def steps(at, to):
         lax.fori_loop(at, to, step_sum, 0)
 
-    for n in range(4):
+    for n in range(5):
         steps(n, n + 1)
-        lax.fori_loop(4 + n, 5 + n, step, 0)
+        lax.fori_loop(3 + n, 4 + n, step, 0)
 
     gm_all[...] = row32[...].astype(BF)
     u = dot32(gm_all[...], down_t)
@@ -512,38 +511,7 @@
     gu = (rs * gt) * u
     dpre = jnp.concatenate([gu * slope, gu * silu], axis=1).astype(BF)
     dpre_ref[...] = dpre
-    back = dot32(dpre, g_hi, NT) + dot32(dpre, g_lo, NT)
-    gg_hi = gg.astype(BF).astype(F32)
-    lane = iota((SH * PIECE, SIDE - TAPS), 1)
-    tail = jnp.where(lane == 0, gg_hi, jnp.where(lane == 1, gg - gg_hi, 0.0))
-    side32[...] = jnp.concatenate([back, tail], axis=1)
-    place = pc.half * (EXP // 2) + pc.x
-
-    def source_of(i):
-        return (5 * (pc.rep - i + 8)) % 8
-
-    def reply(p, i, sem):
-        return rcopy(send_back.at[p, i], back_in.at[m, place], sem, bk_rs.at[0], source_of(i) * SH + p, pc.rep)
-
-    def narrow(n, _):
-        p = (m + n) % SH
-        for i in range(TILES):
-            send_back[p, i] = side32[pl.ds(pl.multiple_of(p * PIECE + i * ROWS, ROWS), ROWS), :].astype(BF)
-        for i in range(TILES):
-            pl.when(p != m)(lambda i=i: reply(p, i, bk_ss.at[p]).start())
-
-            @pl.when((p == m) & (source_of(i) != pc.e))
-            def _():
-                reply(p, i, bo_ss.at[i]).start()
-
-            @pl.when((p == m) & (source_of(i) == pc.e))
-            def _():
-                pltpu.make_async_copy(send_back.at[p, i], back_in.at[m, place], bk_rs.at[0]).start()
-
-        return 0
-
-    lax.fori_loop(0, SH, narrow, 0)
-    steps(4, 5)
+    steps(5, 6)
     t_share = dot32(pr, dpre_ref[...], TN)
     for k in range(REP):
         tp[k // 4, k % 4] = t_share[k * TP : (k + 1) * TP]
@@ -554,7 +522,37 @@
         dp[k % 2, k // 2] = d_share[k * dsl : (k + 1) * dsl].astype(BF)
     scatter_d = Scatter(pc, dp, d_got, d_tot, d_side, d_ss, d_rs)
     scatter_d.start()
-    steps(5, 6)
+    back = dot32(dpre, g_hi, NT) + dot32(dpre, g_lo, NT)
+    gg_hi = gg.astype(BF).astype(F32)
+    lane = iota((SH * PIECE, SIDE - TAPS), 1)
+    tail = jnp.where(lane == 0, gg_hi, jnp.where(lane == 1, gg - gg_hi, 0.0))
+    side32[...] = jnp.concatenate([back, tail], axis=1)
+    place = pc.half * (EXP // 2) + pc.x
+
+    def source_of(i):
+        return (5 * (pc.rep - i + 8)) % 8
+
+    def reply(p, i, sem):
+        return rcopy(send_back.at[p, i], back_in.at[m, place], sem, bk_rs.at[0], source_of(i) * SH + p, pc.rep)
+
+    def narrow(n, _):
+        p = (m + n) % SH
+        for i in range(TILES):
+            send_back[p, i] = side32[pl.ds(pl.multiple_of(p * PIECE + i * ROWS, ROWS), ROWS), :].astype(BF)
+        for i in range(TILES):
+            pl.when(p != m)(lambda i=i: reply(p, i, bk_ss.at[p]).start())
+
+            @pl.when((p == m) & (source_of(i) != pc.e))
+            def _():
+                reply(p, i, bo_ss.at[i]).start()
+
+            @pl.when((p == m) & (source_of(i) == pc.e))
+            def _():
+                pltpu.make_async_copy(send_back.at[p, i], back_in.at[m, place], bk_rs.at[0]).start()
+
+        return 0
+
+    lax.fori_loop(0, SH, narrow, 0)
     scatter_t.add()
     scatter_d.add()
     steps(6, 7)

time: 107 us -> 108 us (level); the launches traced: 107 us -> 107 us
  no operation moved by 1% of the time
where the time goes in v8:
time: 108 us; the launch traced here: 107 us
  Pallas kernels  106 us (98%)
    pallas_call x1, Pallas kernels, local(): pl.pallas_call(layer_kernel, out_shape=(jax.ShapeDtypeStruct((tok, dm), B...  104 us
    pallas_call x1, Pallas kernels, local(): pl.pallas_call(hand_over_kernel, out_shape=tuple((jax.ShapeDtypeStruct(o....  2.34 us

profile of v8, /device:TPU:1, one launch (start us, length us, event | category | flops | bytes accessed | tf_op | source)
XLA Modules:
  0.0 106.5 jit_solution(12463975368770245966)
XLA Ops:
  0.6 103.5 %layer.1 = (bf16[128,1536]{1,0:T(8,128)(2,1)}, f32[2,16,64]{2,1,0:T(8,128)}, f32[192,384]{1,0:T(8,128)}, f32[192,384]{1,0:T(8,128)}, f32[192,384]{1,0:T(8,128)}) custom-call(bf16[2,16,64]{2,1,0:T(8,128)(2,1)} %latent.1, bf16[144,1536]{1,0:T(8,128)(2,1)} %s_ref.1, f32[1536]{0:T(1024)} %gain_ref.1, bf16[8,1536]{1,0:T(8,128)(2,1)} %bitcast.5, ...), custom_call_target="tpu_custom_call" | custom-call | tf_op jit(solution)/shard_map/layer/pallas_call | solution.py:762
  104.2 2.3 %hand_over.1 = (bf16[128,1536]{1,0:T(8,128)(2,1)}, f32[2,16,64]{2,1,0:T(8,128)}, f32[192,384]{1,0:T(8,128)}, f32[192,384]{1,0:T(8,128)}, f32[192,384]{1,0:T(8,128)}) custom-call(bf16[128,1536]{1,0:T(8,128)(2,1)} %get-tuple-element.15.refs_0_, f32[2,16,64]{2,1,0:T(8,128)} %get-tuple-element.16.refs_1_, f32[192,384]{1,0:T(8,128)} %get-tuple-element.17.refs_2_, ...), custom_call_target="tpu_custom_call" | custom-call | tf_op jit(solution)/shard_map/hand_over/pallas_call | solution.py:843
